TPU v7x, 32 devices: a whole 2x2x4 slice. The times are simulated.
32 devices in a mesh: expert: 4 (over y, x), shard: 8 (over z, core).
Axes of the slice: x: 2, y: 2, z: 4, core: 2. Of those that a mesh axis runs over, the one named last changes fastest.
Arguments:
- tokens: bfloat16 [32768, 768], P(('expert', 'shard')), may hold values from -6 to 6
- previous_logits: float32 [32768, 12], P(('expert', 'shard')), may hold values from -3 to 3
- routes: int32 [32768, 2], P(('expert', 'shard')), may hold values from 0 to 11, all different within a row
- prefix: int32 [32], P(('expert', 'shard')), may hold values from 1 to 1024
- slot_order: int32 [32, 1024], P(('expert', 'shard')), may hold values from 0 to 1023, each once within a row
- first_gain: bfloat16 [768], P('shard'), may hold values from 0.5 to 1.5
- query_weight: bfloat16 [768, 768], P('shard'), may hold values from -0.21875 to 0.21875
- key_weight: bfloat16 [768, 768], P('shard'), may hold values from -0.21875 to 0.21875
- value_weight: bfloat16 [768, 768], P('shard'), may hold values from -0.21875 to 0.21875
- output_weight: bfloat16 [768, 768], P('shard'), may hold values from -1.75 to 1.75
- second_gain: bfloat16 [768], P('shard'), may hold values from 0.5 to 1.5
- router_weight: bfloat16 [768, 12], P('shard'), may hold values from -0.109375 to 0.109375
- constant_mix: bfloat16 [768, 4], P('shard'), may hold values from -0.21875 to 0.21875
- constant_vectors: bfloat16 [2, 768], P(None, 'shard'), may hold values from -6 to 6
- gate_weight: bfloat16 [8, 768, 2048], P('expert', 'shard'), may hold values from -0.21875 to 0.21875
- up_weight: bfloat16 [8, 768, 2048], P('expert', 'shard'), may hold values from -0.21875 to 0.21875
- down_weight: bfloat16 [8, 2048, 768], P('expert', 'shard'), may hold values from -0.25 to 0.25
- cotangent: bfloat16 [32768, 768], P(('expert', 'shard')), may hold values from -6 to 6
Outputs:
- mixed: bfloat16 [32768, 768], P(('expert', 'shard'))
- tokens_grad: float32 [32768, 768], P(('expert', 'shard'))
- previous_grad: float32 [32768, 12], P(('expert', 'shard'))
- query_grad: float32 [768, 768], P('shard')
- key_grad: float32 [768, 768], P('shard')
- value_grad: float32 [768, 768], P('shard')
- output_grad: float32 [768, 768], P('shard')
- router_grad: float32 [768, 12], P('shard')
- mix_grad: float32 [768, 4], P('shard')
- vector_grad: float32 [2, 768], P(None, 'shard')
- first_grad: float32 [768], P('shard')
- second_grad: float32 [768], P('shard')
- gate_grad: float32 [8, 768, 2048], P('expert', 'shard')
- up_grad: float32 [8, 768, 2048], P('expert', 'shard')
- down_grad: float32 [8, 2048, 768], P('expert', 'shard')
Inputs may be any that keep to these rules, and one draw needn't show every extreme that they name: `routes`: each token names two different experts; number 8 is the zero expert, 9 the copy expert, 10 and 11 the two constant experts. `slot_order`: each row is a permutation of its device's 1024 token indices.
All inputs are finite; a program needn't handle non-finite values.
Results may differ from a plain program's by a relative error of at most 0.022.
Values may be sent and summed in bfloat16 or wider, within the bound.
No kernel may reach another device: no remote copies, remote signals or barrier semaphores. Data moves between devices by JAX's collectives and lax.ppermute only.
A program may use at most 256 MiB of HBM per device.

v0:
```python
import jax
import jax.numpy as jnp
from jax import lax
from jax.sharding import PartitionSpec as P

HEADS = 12
HEAD_DIM = 64
ZC = 4
TOP = 2
LEN = 1024


EPS = 1e-05
NEG = -1e30
highest = lax.Precision.HIGHEST


def rms_scale(values):
    return lax.rsqrt(jnp.mean(values * values, axis=-1, keepdims=True) + EPS)


def rotary_tables(length, head_dim):
    half_dim = head_dim // 2
    frequency = 10000.0 ** (-jnp.arange(half_dim, dtype=jnp.float32) * 2.0 / head_dim)
    angles = jnp.arange(length, dtype=jnp.float32)[:, None] * frequency[None, :]
    return (jnp.cos(angles), jnp.sin(angles))


def rotate(values, cosine_table, sine_table):
    half_dim = values.shape[-1] // 2
    first_half = values[..., :half_dim]
    second_half = values[..., half_dim:]
    cosine = cosine_table[:, None, :]
    sine_wave = sine_table[:, None, :]
    return jnp.concatenate(
        [
            first_half * cosine - second_half * sine_wave,
            second_half * cosine + first_half * sine_wave,
        ],
        axis=-1,
    )


def assign_slots(route_rows, turn_order, experts, capacity):
    tok_count = route_rows.shape[0]
    choices_count = route_rows.shape[1]
    ordered = route_rows[turn_order].reshape(-1)
    pair_ids = (
        turn_order[:, None] * choices_count + jnp.arange(choices_count, dtype=jnp.int32)[None, :]
    ).reshape(-1)
    onehot = (ordered[:, None] == jnp.arange(experts, dtype=jnp.int32)[None, :]).astype(jnp.int32)
    earlier = jnp.cumsum(onehot, axis=0, dtype=jnp.int32) - onehot
    position = jnp.sum(earlier * onehot, axis=1, dtype=jnp.int32)
    kept_pair = (ordered < experts) & (position < capacity)
    target = jnp.where(kept_pair, ordered * capacity + position, experts * capacity)
    slot_pair = (
        jnp.full((experts * capacity,), choices_count * tok_count, jnp.int32)
        .at[target]
        .set(pair_ids, mode="drop")
    )
    pair_dest = jnp.zeros((choices_count * tok_count,), jnp.int32).at[pair_ids].set(target)
    return (slot_pair, pair_dest.reshape(tok_count, choices_count))


def block_scores(query_block, keys_seq, row_start, prefix_len, score_scale):
    block_rows = query_block.shape[0]
    raw_scores = (
        jnp.einsum("qhd,khd->hqk", query_block, keys_seq, preferred_element_type=jnp.float32)
        * score_scale
    )
    query_pos = row_start + jnp.arange(block_rows, dtype=jnp.int32)
    key_pos = jnp.arange(keys_seq.shape[0], dtype=jnp.int32)
    visible = (key_pos[None, :] <= query_pos[:, None]) | (key_pos[None, :] < prefix_len)
    return jnp.where(visible[None], raw_scores, NEG)


def attend_forward(query_all, keys_all, values_all, prefix, score_scale):
    length = query_all.shape[1]
    block_rows = min(512, length)
    block_count = length // block_rows

    def one_sequence(operands):
        query_seq, keys_seq, values_seq, prefix_len = operands
        query_blocks = query_seq.reshape((block_count, block_rows) + query_seq.shape[1:])

        def one_block(pieces):
            query_block, row_start = pieces
            scores = block_scores(query_block, keys_seq, row_start, prefix_len, score_scale)
            row_max = jnp.max(scores, axis=-1, keepdims=True)
            exponent = jnp.exp(scores - row_max)
            row_total = jnp.sum(exponent, axis=-1, keepdims=True)
            weights = (exponent / row_total).astype(jnp.bfloat16)
            output = jnp.einsum(
                "hqk,khd->qhd", weights, values_seq, preferred_element_type=jnp.float32
            )
            return (output, (row_max + jnp.log(row_total))[..., 0])

        starts = jnp.arange(block_count, dtype=jnp.int32) * block_rows
        outputs, log_sums = lax.map(one_block, (query_blocks, starts))
        return (outputs.reshape(length, -1), log_sums)

    return lax.map(one_sequence, (query_all, keys_all, values_all, prefix))


def attend_backward(query_all, keys_all, values_all, prefix, log_sums, grad_all, score_scale):
    length = query_all.shape[1]
    block_rows = min(512, length)
    block_count = length // block_rows

    def one_sequence(operands):
        query_seq, keys_seq, values_seq, prefix_len, lse_seq, grad_seq = operands
        query_blocks = query_seq.reshape((block_count, block_rows) + query_seq.shape[1:])
        grad_blocks = grad_seq.reshape((block_count, block_rows) + grad_seq.shape[1:])

        def one_block(running, pieces):
            key_acc, value_acc = running
            query_block, grad_blk, lse_blk, row_start = pieces
            scores = block_scores(query_block, keys_seq, row_start, prefix_len, score_scale)
            weights = jnp.exp(scores - lse_blk[..., None])
            grad_probs = jnp.einsum(
                "qhd,khd->hqk", grad_blk, values_seq, preferred_element_type=jnp.float32
            )
            value_acc = value_acc + jnp.einsum(
                "hqk,qhd->khd",
                weights.astype(jnp.bfloat16),
                grad_blk,
                preferred_element_type=jnp.float32,
            )
            row_dot = jnp.sum(weights * grad_probs, axis=-1, keepdims=True)
            grad_scores = (weights * (grad_probs - row_dot)).astype(jnp.bfloat16)
            query_grad = (
                jnp.einsum(
                    "hqk,khd->qhd", grad_scores, keys_seq, preferred_element_type=jnp.float32
                )
                * score_scale
            )
            key_acc = (
                key_acc
                + jnp.einsum(
                    "hqk,qhd->khd", grad_scores, query_block, preferred_element_type=jnp.float32
                )
                * score_scale
            )
            return ((key_acc, value_acc), query_grad)

        empty_grads = jnp.zeros(keys_seq.shape, jnp.float32)
        starts = jnp.arange(block_count, dtype=jnp.int32) * block_rows
        (key_grad, value_grad), query_grads = lax.scan(
            one_block, (empty_grads, empty_grads), (query_blocks, grad_blocks, lse_seq, starts)
        )
        return (query_grads.reshape(keys_seq.shape), key_grad, value_grad)

    return lax.map(one_sequence, (query_all, keys_all, values_all, prefix, log_sums, grad_all))


def body(
    tokens,
    previous_logits,
    routes,
    prefix,
    slot_order,
    first_gain,
    query_weight,
    key_weight,
    value_weight,
    output_weight,
    second_gain,
    router_weight,
    constant_mix,
    constant_vectors,
    gate_weight,
    up_weight,
    down_weight,
    cotangent,
):
    owners = lax.axis_size("expert")
    local_experts = gate_weight.shape[0]
    experts = local_experts * owners
    tok_count, model_width = tokens.shape
    capacity = tok_count * TOP // (experts + ZC) // 8 * 8
    seq_count = tok_count // LEN
    score_scale = HEAD_DIM ** (-0.5)
    cosine_table, sine_table = rotary_tables(LEN, HEAD_DIM)
    head_shape = (seq_count, LEN, HEADS, HEAD_DIM)
    dense_full = (
        lax.all_gather(first_gain, "shard", axis=0, tiled=True),
        lax.all_gather(query_weight, "shard", axis=0, tiled=True),
        lax.all_gather(key_weight, "shard", axis=0, tiled=True),
        lax.all_gather(value_weight, "shard", axis=0, tiled=True),
        lax.all_gather(output_weight, "shard", axis=0, tiled=True),
        lax.all_gather(second_gain, "shard", axis=0, tiled=True),
        lax.all_gather(router_weight, "shard", axis=0, tiled=True),
        lax.all_gather(constant_mix, "shard", axis=0, tiled=True),
        lax.all_gather(constant_vectors, "shard", axis=1, tiled=True),
    )
    (
        gain_one,
        query_full,
        key_full,
        value_full,
        output_full,
        gain_two,
        router_full,
        mix_full,
        vectors_full,
    ) = dense_full
    inputs = tokens.astype(jnp.float32)
    scale_one = rms_scale(inputs)
    normed_one = (inputs * scale_one * gain_one.astype(jnp.float32)).astype(jnp.bfloat16)
    query_lin = jnp.dot(normed_one, query_full, preferred_element_type=jnp.float32)
    key_lin = jnp.dot(normed_one, key_full, preferred_element_type=jnp.float32)
    values = jnp.dot(normed_one, value_full, preferred_element_type=jnp.float32).astype(
        jnp.bfloat16
    )
    queries = rotate(query_lin.reshape(head_shape), cosine_table, sine_table).astype(jnp.bfloat16)
    keys_rot = rotate(key_lin.reshape(head_shape), cosine_table, sine_table).astype(jnp.bfloat16)
    values_heads = values.reshape(head_shape)
    expert_full = (
        lax.all_gather(gate_weight, "shard", axis=1, tiled=True),
        lax.all_gather(up_weight, "shard", axis=1, tiled=True),
        lax.all_gather(down_weight, "shard", axis=1, tiled=True),
    )
    gate_full, up_full, down_full = expert_full
    mixed_heads, log_sums = attend_forward(queries, keys_rot, values_heads, prefix, score_scale)
    attn_mix = mixed_heads.reshape(tok_count, model_width).astype(jnp.bfloat16)
    residual = inputs + jnp.dot(attn_mix, output_full, preferred_element_type=jnp.float32)
    scale_two = rms_scale(residual)
    normed_two = (residual * scale_two * gain_two.astype(jnp.float32)).astype(jnp.bfloat16)
    normed_float = normed_two.astype(jnp.float32)
    all_experts = experts + ZC
    route_hot = (
        routes[:, :, None] == jnp.arange(all_experts, dtype=jnp.int32)[None, None, :]
    ).astype(jnp.float32)
    logits = jnp.dot(normed_two, router_full, preferred_element_type=jnp.float32) + previous_logits
    chosen = jnp.sum(route_hot * logits[:, None, :], axis=-1)
    gate_values = jax.nn.softmax(chosen, axis=-1)
    mix_logits = jnp.dot(normed_two, mix_full, preferred_element_type=jnp.float32).reshape(
        tok_count, 2, 2
    )
    mix_weights = jax.nn.softmax(mix_logits, axis=-1)
    vectors_float = vectors_full.astype(jnp.float32)
    constant_out = (
        mix_weights[..., 0:1] * normed_float[:, None, :]
        + mix_weights[..., 1:2] * vectors_float[None]
    )
    slot_pair, pair_dest = assign_slots(routes, slot_order[0], experts, capacity)
    slot_token = slot_pair // 2
    padded_rows = jnp.concatenate([normed_two, jnp.zeros((1, model_width), jnp.bfloat16)], axis=0)
    send_rows = padded_rows[slot_token].reshape(experts, capacity, model_width)
    expert_rows = lax.all_to_all(send_rows, "expert", split_axis=0, concat_axis=1, tiled=True)
    gate_pre = jnp.einsum(
        "erd,edf->erf", expert_rows, gate_full, preferred_element_type=jnp.float32
    )
    up_pre = jnp.einsum("erd,edf->erf", expert_rows, up_full, preferred_element_type=jnp.float32)
    sigmoid_gate = jax.nn.sigmoid(gate_pre)
    silu_gate = gate_pre * sigmoid_gate
    hidden = (silu_gate * up_pre).astype(jnp.bfloat16)
    expert_out = jnp.einsum(
        "erf,efd->erd", hidden, down_full, preferred_element_type=jnp.float32
    ).astype(jnp.bfloat16)
    returned = lax.all_to_all(expert_out, "expert", split_axis=1, concat_axis=0, tiled=True)
    returned_pad = jnp.concatenate(
        [
            returned.reshape(experts * capacity, model_width),
            jnp.zeros((1, model_width), jnp.bfloat16),
        ],
        axis=0,
    )
    expert_pair = returned_pad[pair_dest].astype(jnp.float32)
    route_col = routes[:, :, None]
    branch = jnp.where(
        route_col < experts,
        expert_pair,
        jnp.where(
            route_col == experts + 1,
            normed_float[:, None, :],
            jnp.where(
                route_col == experts + 2,
                constant_out[:, 0:1, :],
                jnp.where(route_col == experts + 3, constant_out[:, 1:2, :], 0.0),
            ),
        ),
    )
    mixed_out = (residual + jnp.sum(gate_values[..., None] * branch, axis=1)).astype(jnp.bfloat16)
    out_grad = cotangent.astype(jnp.float32)
    gate_grads = jnp.sum(out_grad[:, None, :] * branch, axis=-1)
    logit_pair = gate_values * (
        gate_grads - jnp.sum(gate_values * gate_grads, axis=-1, keepdims=True)
    )
    logit_grad = jnp.sum(logit_pair[:, :, None] * route_hot, axis=1)
    pair_grads = (
        (gate_values[..., None] * out_grad[:, None, :])
        .astype(jnp.bfloat16)
        .reshape(2 * tok_count, model_width)
    )
    pair_pad = jnp.concatenate([pair_grads, jnp.zeros((1, model_width), jnp.bfloat16)], axis=0)
    slot_grads = pair_pad[slot_pair].reshape(experts, capacity, model_width)
    rows_out_grad = lax.all_to_all(slot_grads, "expert", split_axis=0, concat_axis=1, tiled=True)
    regathered = (
        lax.all_gather(first_gain, "shard", axis=0, tiled=True),
        lax.all_gather(query_weight, "shard", axis=0, tiled=True),
        lax.all_gather(key_weight, "shard", axis=0, tiled=True),
        lax.all_gather(value_weight, "shard", axis=0, tiled=True),
        lax.all_gather(output_weight, "shard", axis=0, tiled=True),
        lax.all_gather(second_gain, "shard", axis=0, tiled=True),
        lax.all_gather(router_weight, "shard", axis=0, tiled=True),
        lax.all_gather(constant_mix, "shard", axis=0, tiled=True),
        lax.all_gather(constant_vectors, "shard", axis=1, tiled=True),
        lax.all_gather(gate_weight, "shard", axis=1, tiled=True),
        lax.all_gather(up_weight, "shard", axis=1, tiled=True),
        lax.all_gather(down_weight, "shard", axis=1, tiled=True),
    )
    (
        gain_one,
        query_full,
        key_full,
        value_full,
        output_full,
        gain_two,
        router_full,
        mix_full,
        vectors_full,
        gate_full,
        up_full,
        down_full,
    ) = regathered
    hidden_grad = jnp.einsum(
        "erd,efd->erf", rows_out_grad, down_full, preferred_element_type=jnp.float32
    )
    gate_pre_grad = (
        hidden_grad * up_pre * (sigmoid_gate + silu_gate * (1.0 - sigmoid_gate))
    ).astype(jnp.bfloat16)
    up_pre_grad = (hidden_grad * silu_gate).astype(jnp.bfloat16)
    rows_grad = (
        jnp.einsum("erf,edf->erd", gate_pre_grad, gate_full, preferred_element_type=jnp.float32)
        + jnp.einsum("erf,edf->erd", up_pre_grad, up_full, preferred_element_type=jnp.float32)
    ).astype(jnp.bfloat16)
    rows_back = lax.all_to_all(rows_grad, "expert", split_axis=1, concat_axis=0, tiled=True)
    down_term = jnp.einsum(
        "erf,erd->efd", hidden, rows_out_grad, preferred_element_type=jnp.float32
    )
    gate_term = jnp.einsum(
        "erd,erf->edf", expert_rows, gate_pre_grad, preferred_element_type=jnp.float32
    )
    up_term = jnp.einsum(
        "erd,erf->edf", expert_rows, up_pre_grad, preferred_element_type=jnp.float32
    )
    expert_sums = (
        lax.psum_scatter(
            gate_term.astype(jnp.bfloat16), "shard", scatter_dimension=1, tiled=True
        ).astype(jnp.float32),
        lax.psum_scatter(
            up_term.astype(jnp.bfloat16), "shard", scatter_dimension=1, tiled=True
        ).astype(jnp.float32),
        lax.psum_scatter(
            down_term.astype(jnp.bfloat16), "shard", scatter_dimension=1, tiled=True
        ).astype(jnp.float32),
    )
    gate_sum, up_sum, down_sum = expert_sums
    back_pad = jnp.concatenate(
        [
            rows_back.reshape(experts * capacity, model_width),
            jnp.zeros((1, model_width), jnp.bfloat16),
        ],
        axis=0,
    )
    normed_grad = jnp.sum(back_pad[pair_dest].astype(jnp.float32), axis=1)
    copy_weight = jnp.sum(gate_values * (routes == experts + 1), axis=1)
    const_sel = jnp.stack(
        [
            jnp.sum(gate_values * (routes == experts + 2), axis=1),
            jnp.sum(gate_values * (routes == experts + 3), axis=1),
        ],
        axis=1,
    )
    normed_grad = (
        normed_grad
        + (copy_weight + jnp.sum(const_sel * mix_weights[..., 0], axis=1))[:, None] * out_grad
    )
    vector_term = jnp.einsum(
        "tc,td->cd",
        const_sel * mix_weights[..., 1],
        out_grad,
        precision=highest,
        preferred_element_type=jnp.float32,
    )
    along_normed = jnp.sum(out_grad * normed_float, axis=-1)
    along_vectors = jnp.einsum(
        "td,cd->tc", out_grad, vectors_float, precision=highest, preferred_element_type=jnp.float32
    )
    weight_grad = const_sel[..., None] * jnp.stack(
        [jnp.broadcast_to(along_normed[:, None], (tok_count, 2)), along_vectors], axis=-1
    )
    mix_logit_grad = (
        mix_weights * (weight_grad - jnp.sum(mix_weights * weight_grad, axis=-1, keepdims=True))
    ).reshape(tok_count, 4)
    normed_grad = normed_grad + jnp.einsum(
        "tc,dc->td",
        mix_logit_grad,
        mix_full.astype(jnp.float32),
        precision=highest,
        preferred_element_type=jnp.float32,
    )
    normed_grad = normed_grad + jnp.einsum(
        "te,de->td",
        logit_grad,
        router_full.astype(jnp.float32),
        precision=highest,
        preferred_element_type=jnp.float32,
    )
    router_term = jnp.einsum(
        "td,te->de", normed_float, logit_grad, precision=highest, preferred_element_type=jnp.float32
    )
    mix_term = jnp.einsum(
        "td,tc->dc",
        normed_float,
        mix_logit_grad,
        precision=highest,
        preferred_element_type=jnp.float32,
    )
    scaled_two = normed_grad * gain_two.astype(jnp.float32)
    second_term = jnp.sum(normed_grad * residual * scale_two, axis=0)
    residual_grad = (
        out_grad
        + scale_two * scaled_two
        - residual * scale_two**3 * jnp.mean(scaled_two * residual, axis=-1, keepdims=True)
    )
    attn_grad = residual_grad.astype(jnp.bfloat16)
    output_term = jnp.einsum("td,te->de", attn_mix, attn_grad, preferred_element_type=jnp.float32)
    mix_heads_grad = (
        jnp.einsum("te,de->td", attn_grad, output_full, preferred_element_type=jnp.float32)
        .astype(jnp.bfloat16)
        .reshape(head_shape)
    )
    query_rot_grad, key_rot_grad, value_heads_grad = attend_backward(
        queries, keys_rot, values_heads, prefix, log_sums, mix_heads_grad, score_scale
    )
    query_lin_grad = (
        rotate(query_rot_grad, cosine_table, -sine_table)
        .reshape(tok_count, model_width)
        .astype(jnp.bfloat16)
    )
    key_lin_grad = (
        rotate(key_rot_grad, cosine_table, -sine_table)
        .reshape(tok_count, model_width)
        .astype(jnp.bfloat16)
    )
    value_lin_grad = value_heads_grad.reshape(tok_count, model_width).astype(jnp.bfloat16)
    query_term = jnp.einsum(
        "td,te->de", normed_one, query_lin_grad, preferred_element_type=jnp.float32
    )
    key_term = jnp.einsum("td,te->de", normed_one, key_lin_grad, preferred_element_type=jnp.float32)
    value_term = jnp.einsum(
        "td,te->de", normed_one, value_lin_grad, preferred_element_type=jnp.float32
    )
    normed_one_grad = (
        jnp.einsum("te,de->td", query_lin_grad, query_full, preferred_element_type=jnp.float32)
        + jnp.einsum("te,de->td", key_lin_grad, key_full, preferred_element_type=jnp.float32)
        + jnp.einsum("te,de->td", value_lin_grad, value_full, preferred_element_type=jnp.float32)
    )
    scaled_one = normed_one_grad * gain_one.astype(jnp.float32)
    first_term = jnp.sum(normed_one_grad * inputs * scale_one, axis=0)
    tokens_grad = (
        residual_grad
        + scale_one * scaled_one
        - inputs * scale_one**3 * jnp.mean(scaled_one * inputs, axis=-1, keepdims=True)
    )
    dense_sums = (
        lax.psum_scatter(
            first_term.astype(jnp.bfloat16), "shard", scatter_dimension=0, tiled=True
        ).astype(jnp.float32),
        lax.psum_scatter(
            query_term.astype(jnp.bfloat16), "shard", scatter_dimension=0, tiled=True
        ).astype(jnp.float32),
        lax.psum_scatter(
            key_term.astype(jnp.bfloat16), "shard", scatter_dimension=0, tiled=True
        ).astype(jnp.float32),
        lax.psum_scatter(
            value_term.astype(jnp.bfloat16), "shard", scatter_dimension=0, tiled=True
        ).astype(jnp.float32),
        lax.psum_scatter(
            output_term.astype(jnp.bfloat16), "shard", scatter_dimension=0, tiled=True
        ).astype(jnp.float32),
        lax.psum_scatter(
            second_term.astype(jnp.bfloat16), "shard", scatter_dimension=0, tiled=True
        ).astype(jnp.float32),
        lax.psum_scatter(
            router_term.astype(jnp.bfloat16), "shard", scatter_dimension=0, tiled=True
        ).astype(jnp.float32),
        lax.psum_scatter(
            mix_term.astype(jnp.bfloat16), "shard", scatter_dimension=0, tiled=True
        ).astype(jnp.float32),
        lax.psum_scatter(
            vector_term.astype(jnp.bfloat16), "shard", scatter_dimension=1, tiled=True
        ).astype(jnp.float32),
    )
    dense_total = (
        lax.psum(dense_sums[0].astype(jnp.bfloat16), "expert").astype(jnp.float32),
        lax.psum(dense_sums[1].astype(jnp.bfloat16), "expert").astype(jnp.float32),
        lax.psum(dense_sums[2].astype(jnp.bfloat16), "expert").astype(jnp.float32),
        lax.psum(dense_sums[3].astype(jnp.bfloat16), "expert").astype(jnp.float32),
        lax.psum(dense_sums[4].astype(jnp.bfloat16), "expert").astype(jnp.float32),
        lax.psum(dense_sums[5].astype(jnp.bfloat16), "expert").astype(jnp.float32),
        lax.psum(dense_sums[6].astype(jnp.bfloat16), "expert").astype(jnp.float32),
        lax.psum(dense_sums[7].astype(jnp.bfloat16), "expert").astype(jnp.float32),
        lax.psum(dense_sums[8].astype(jnp.bfloat16), "expert").astype(jnp.float32),
    )
    return (
        mixed_out,
        tokens_grad,
        logit_grad,
        dense_total[1],
        dense_total[2],
        dense_total[3],
        dense_total[4],
        dense_total[6],
        dense_total[7],
        dense_total[8],
        dense_total[0],
        dense_total[5],
        gate_sum,
        up_sum,
        down_sum,
    )


def solution(mesh):
    return jax.shard_map(
        body,
        mesh=mesh,
        in_specs=(
            P(("expert", "shard"), None),
            P(("expert", "shard"), None),
            P(("expert", "shard"), None),
            P(("expert", "shard")),
            P(("expert", "shard"), None),
            P("shard"),
            P("shard", None),
            P("shard", None),
            P("shard", None),
            P("shard", None),
            P("shard"),
            P("shard", None),
            P("shard", None),
            P(None, "shard"),
            P("expert", "shard", None),
            P("expert", "shard", None),
            P("expert", "shard", None),
            P(("expert", "shard"), None),
        ),
        out_specs=(
            P(("expert", "shard"), None),
            P(("expert", "shard"), None),
            P(("expert", "shard"), None),
            P("shard", None),
            P("shard", None),
            P("shard", None),
            P("shard", None),
            P("shard", None),
            P("shard", None),
            P(None, "shard"),
            P("shard"),
            P("shard"),
            P("expert", "shard", None),
            P("expert", "shard", None),
            P("expert", "shard", None),
        ),
        check_vma=False,
    )
```

profile of v0, /device:TPU:0, one launch (start us, length us, event | category | flops | bytes accessed | tf_op | source)
XLA Modules:
  0.0 1235.6 jit_solution(13394069500922460471)
XLA Ops:
  26.2 18.1 %all-reduce.9 = (bf16[768]{0:T(1024)(128)(2,1)S(1)}, bf16[768]{0:T(1024)(128)(2,1)S(1)}) all-reduce(bf16[768]{0:T(1024)(128)(2,1)S(1)} %dynamic-update-slice, bf16[768]{0:T(1024)(128)(2,1)S(1)} %dynamic-update-slice.1), channel_id=1, replica_groups=mesh['expert'=4,'shard'=8] {'shard'}, use_global_device_ids=true, to_apply=%add.4 | all-reduce | flops 1536 | bytes 6144
  45.9 14.1 %all-gather = bf16[8,96,12]{1,2,0:T(8,128)(2,1)S(1)} all-gather(bf16[1,96,12]{1,2,0:T(8,128)(2,1)S(1)} %bitcast.288), channel_id=1, replica_groups=mesh['expert'=4,'shard'=8] {'shard'}, dimensions={0}, use_global_device_ids=true | all-gather | bytes 20736 | tf_op jit(solution)/shard_map/all_gather | solution.py:192
  125.3 75.9 %while.47 = (s32[]{:T(128)}, bf16[2,512,12,64]{1,3,2,0:T(8,128)(2,1)}, f32[2,12,512]{2,1,0:T(8,128)S(1)}, s32[2]{0:T(128)S(1)}, s32[]{:T(128)}, /*index=5*/bf16[...) while((s32[]{:T(128)}, ...), condition=%wide.region_4.5_spmd, body=%wide.region_1.4_spmd.sunk | while | flops 1687154176 | bytes 190281904 | solution.py:99
  138.6 12.6 %fusion.157 = f32[12,512]{1,0:T(8,128)S(1)} fusion(f32[12,512,1024]{2,1,0:T(8,128)} %get-tuple-element.475, f32[12,512]{1,0:T(8,128)S(1)} %get-tuple-element.476, pred[512,1024]{1,0:T(8,128)(4,1)S(1)} %fusion.155), kind=kLoop, calls=%fused_computation.11.clone.1 | loop fusion | flops 25159680 | bytes 25739264 | tf_op jit(solution)/shard_map/while/body/eval_jaxpr/while/body/eval_jaxpr/reduce_sum | solution.py:91
  176.0 13.2 %fusion.157 = f32[12,512]{1,0:T(8,128)S(1)} fusion(f32[12,512,1024]{2,1,0:T(8,128)} %get-tuple-element.475, f32[12,512]{1,0:T(8,128)S(1)} %get-tuple-element.476, pred[512,1024]{1,0:T(8,128)(4,1)S(1)} %fusion.155), kind=kLoop, calls=%fused_computation.11.clone.1 | loop fusion | flops 25159680 | bytes 25739264 | tf_op jit(solution)/shard_map/while/body/eval_jaxpr/while/body/eval_jaxpr/reduce_sum | solution.py:91
  237.3 12.2 all-to-all-done
  289.4 12.6 %fusion.75 = f32[2,672,2048]{2,1,0:T(8,128)} fusion(bf16[2,672,768]{2,1,0:T(8,128)(2,1)} %bitcast.266, bf16[2,768,2048]{2,1,0:T(8,128)(2,1)} %all-gather.21.cloned.1.call-done), kind=kOutput, calls=%fused_computation.205 | convolution fusion | flops 4227858432 | bytes 19365888 | tf_op jit(solution)/shard_map/erd,edf->erf/dot_general | solution.py:254
  302.1 12.1 fusion.74
  314.1 20.4 %multiply_convert_fusion.1 = (bf16[2,672,2048]{2,1,0:T(8,128)(2,1)}, bf16[2,672,2048]{2,1,0:T(8,128)(2,1)}, bf16[2,672,2048]{2,1,0:T(8,128)(2,1)}) fusion(f32[2,672,2048]{2,1,0:T(8,128)} %fusion.74, f32[2,672,2048]{2,1,0:T(8,128)} %fusion.75, bf16[2,672,768]{2,1,0:T(8,128)(2,1)S(1)} %bitcast.264, bf16[2,2048,768]{2,1,0:T(8,128)(2,1)} %all-gather.23.cloned.1.call-done), kind=kOutput, calls=%fused_computation.55 | convolution fusion | flops 4266393600 | bytes 46891008 | tf_op jit(solution)/shard_map/erd,efd->erf/dot_general | solution.py:327
  391.2 12.7 %fusion.72 = (f32[1024,1,768]{2,1,0:T(1,128)}, f32[1024,1,768]{2,1,0:T(1,128)}) fusion(f32[1024,2,768]{2,1,0:T(2,128)} %multiply_add_fusion), kind=kLoop, calls=%fused_computation.202 | loop fusion | bytes 12582912 | tf_op jit(solution)/shard_map/slice | solution.py:279
  415.1 11.9 gather_fusion.2
  452.3 25.7 %multiply_reduce_fusion.1 = (f32[1024,2]{1,0:T(8,128)}, f32[1024,768]{1,0:T(8,128)}) fusion(f32[1024,768]{1,0:T(8,128)} %convert_element_type.219, f32[1024,2]{1,0:T(8,128)} %copy-done.29, f32[1024,2,768]{2,1,0:T(2,128)} %reshape.689, f32[1024,768]{1,0:T(8,128)} %get-tuple-element.364, pred[1024,2]{1,0:T(8,128)(4,1)S(1)} %copy.137, ...), kind=kLoop, calls=%fused_computation.66 | loop fusion | flops 11794432 | bytes 22044672 | tf_op jit(solution)/shard_map/reduce_sum | solution.py:286
  489.8 12.1 reduce_sum.217
  523.7 233.2 %while.48 = (s32[]{:T(128)}, f32[1024,12,64]{0,2,1:T(8,128)}, f32[1024,12,64]{0,2,1:T(8,128)}, f32[2,512,12,64]{1,0,3,2:T(2,128)}, bf16[2,512,12,64]{1,3,2,0:T(8...) while((s32[]{:T(128)}, f32[1024,12,64]{0,2,1:T(8,128)}, ...), condition=%wide.region_30.31_spmd.clone, body=%wide.region_28.30_spmd.clone.sunk | while | flops 4126273024 | bytes 238213392 | solution.py:148
  537.6 13.5 %bitcast_add_fusion.5 = f32[1024,12,64]{0,2,1:T(8,128)} fusion(f32[1024,12,64]{0,2,1:T(8,128)} %get-tuple-element.532, f32[12,512,1024]{2,1,0:T(8,128)} %fusion.167, f32[12,512]{1,0:T(8,128)S(1)} %dynamic-slice_bitcast_fusion.2, pred[512,1024]{1,0:T(8,128)(4,1)S(1)} %fusion.168, pred[]{:T(512)S(6)} %compare.9, ...), kind=kOutput, calls=%fused_computation.31.clone.1 | convolution fusion | flops 832045056 | bytes 32800772 | tf_op jit(solution)/shard_map/while/body/eval_jaxpr/while/body/eval_jaxpr/hqk,qhd->khd/dot_general | solution.py:123
  551.2 18.1 %multiply_reduce_fusion.11 = (f32[12,512]{1,0:T(8,128)S(1)}, f32[12,512,1024]{2,1,0:T(8,128)}) fusion(f32[12,512,1024]{2,1,0:T(8,128)} %fusion.167, f32[12,512]{1,0:T(8,128)S(1)} %dynamic-slice_bitcast_fusion.2, pred[512,1024]{1,0:T(8,128)(4,1)S(1)} %fusion.168, bf16[1024,12,64]{0,2,1:T(8,128)(2,1)} %get-tuple-element.553, ...), kind=kOutput, calls=%fused_computation.26.clone.1 | convolution fusion | flops 836757504 | bytes 53264388 | tf_op jit(solution)/shard_map/while/body/eval_jaxpr/while/body/eval_jaxpr/qhd,khd->hqk/dot_general | solution.py:120
  569.3 21.2 %multiply_convert_fusion.8 = bf16[12,512,1024]{2,1,0:T(8,128)(2,1)} fusion(f32[12,512,1024]{2,1,0:T(8,128)} %get-tuple-element.488, f32[12,512,1024]{2,1,0:T(8,128)} %fusion.167, f32[12,512]{1,0:T(8,128)S(1)} %get-tuple-element.489, f32[12,512]{1,0:T(8,128)S(1)} %dynamic-slice_bitcast_fusion.2, pred[512,1024]{1,0:T(8,128)(4,1)S(1)} %fusion.168), kind=kLoop, calls=%fused_computation.25.clone.1 | loop fusion | flops 37748736 | bytes 63488000 | tf_op jit(solution)/shard_map/while/body/eval_jaxpr/while/body/eval_jaxpr/convert_element_type | solution.py:130
  610.6 28.8 %dynamic_update_slice.32 = f32[2,512,12,64]{1,0,3,2:T(2,128)} dynamic-update-slice(f32[2,512,12,64]{1,0,3,2:T(2,128)} %get-tuple-element.533, f32[1,512,12,64]{1,0,3,2:T(1,128)S(1)} %copy.199, s32[]{:T(128)S(6)} %copy.219, s32[]{:T(128)} %constant.84.clone.1..sunk, s32[]{:T(128)} %constant.84.clone.1..sunk, s32[]{:T(128)} %constant.84.clone.1..sunk) | dynamic-update-slice | bytes 3145732 | tf_op jit(solution)/shard_map/while/body/eval_jaxpr/while/body/jit(dynamic_update_index_in_dim)/dynamic_update_slice | solution.py:99
  653.1 14.3 %bitcast_add_fusion.5 = f32[1024,12,64]{0,2,1:T(8,128)} fusion(f32[1024,12,64]{0,2,1:T(8,128)} %get-tuple-element.532, f32[12,512,1024]{2,1,0:T(8,128)} %fusion.167, f32[12,512]{1,0:T(8,128)S(1)} %dynamic-slice_bitcast_fusion.2, pred[512,1024]{1,0:T(8,128)(4,1)S(1)} %fusion.168, pred[]{:T(512)S(6)} %compare.9, ...), kind=kOutput, calls=%fused_computation.31.clone.1 | convolution fusion | flops 832045056 | bytes 32800772 | tf_op jit(solution)/shard_map/while/body/eval_jaxpr/while/body/eval_jaxpr/hqk,qhd->khd/dot_general | solution.py:123
  667.5 18.1 %multiply_reduce_fusion.11 = (f32[12,512]{1,0:T(8,128)S(1)}, f32[12,512,1024]{2,1,0:T(8,128)}) fusion(f32[12,512,1024]{2,1,0:T(8,128)} %fusion.167, f32[12,512]{1,0:T(8,128)S(1)} %dynamic-slice_bitcast_fusion.2, pred[512,1024]{1,0:T(8,128)(4,1)S(1)} %fusion.168, bf16[1024,12,64]{0,2,1:T(8,128)(2,1)} %get-tuple-element.553, ...), kind=kOutput, calls=%fused_computation.26.clone.1 | convolution fusion | flops 836757504 | bytes 53264388 | tf_op jit(solution)/shard_map/while/body/eval_jaxpr/while/body/eval_jaxpr/qhd,khd->hqk/dot_general | solution.py:120
  685.6 21.2 %multiply_convert_fusion.8 = bf16[12,512,1024]{2,1,0:T(8,128)(2,1)} fusion(f32[12,512,1024]{2,1,0:T(8,128)} %get-tuple-element.488, f32[12,512,1024]{2,1,0:T(8,128)} %fusion.167, f32[12,512]{1,0:T(8,128)S(1)} %get-tuple-element.489, f32[12,512]{1,0:T(8,128)S(1)} %dynamic-slice_bitcast_fusion.2, pred[512,1024]{1,0:T(8,128)(4,1)S(1)} %fusion.168), kind=kLoop, calls=%fused_computation.25.clone.1 | loop fusion | flops 37748736 | bytes 63488000 | tf_op jit(solution)/shard_map/while/body/eval_jaxpr/while/body/eval_jaxpr/convert_element_type | solution.py:130
  727.8 28.8 %dynamic_update_slice.32 = f32[2,512,12,64]{1,0,3,2:T(2,128)} dynamic-update-slice(f32[2,512,12,64]{1,0,3,2:T(2,128)} %get-tuple-element.533, f32[1,512,12,64]{1,0,3,2:T(1,128)S(1)} %copy.199, s32[]{:T(128)S(6)} %copy.219, s32[]{:T(128)} %constant.84.clone.1..sunk, s32[]{:T(128)} %constant.84.clone.1..sunk, s32[]{:T(128)} %constant.84.clone.1..sunk) | dynamic-update-slice | bytes 3145732 | tf_op jit(solution)/shard_map/while/body/eval_jaxpr/while/body/jit(dynamic_update_index_in_dim)/dynamic_update_slice | solution.py:99
  786.8 17.5 %reduce-scatter.19.cloned.1.call-done = bf16[96,768]{1,0:T(8,128)(2,1)} async-done(((bf16[768,768]{1,0:T(8,128)(2,1)}), bf16[96,768]{1,0:T(8,128)(2,1)}) %reduce-scatter.19.cloned.1.call-update) | async-done | bytes 147472 | tf_op jit(solution)/shard_map/reduce_scatter | solution.py:475
  804.4 33.3 %reduce-scatter.17.cloned.1.call-done = bf16[96,768]{1,0:T(8,128)(2,1)} async-done(((bf16[768,768]{1,0:T(8,128)(2,1)}), bf16[96,768]{1,0:T(8,128)(2,1)}) %reduce-scatter.17.cloned.1.call-update) | async-done | bytes 147472 | tf_op jit(solution)/shard_map/reduce_scatter | solution.py:472
  837.7 33.5 %reduce-scatter.21.cloned.1.call-done = bf16[96,768]{1,0:T(8,128)(2,1)} async-done(((bf16[768,768]{1,0:T(8,128)(2,1)}), bf16[96,768]{1,0:T(8,128)(2,1)}) %reduce-scatter.21.cloned.1.call-update) | async-done | bytes 147472 | tf_op jit(solution)/shard_map/reduce_scatter | solution.py:478
  893.8 11.8 convolution_convert_fusion
  915.0 13.8 %all-reduce.8 = (bf16[768]{0:T(1024)(128)(2,1)S(1)}, bf16[768]{0:T(1024)(128)(2,1)S(1)}) all-reduce(bf16[768]{0:T(1024)(128)(2,1)S(1)} %get-tuple-element.257, bf16[768]{0:T(1024)(128)(2,1)S(1)} %copy-done.87), channel_id=9, replica_groups=mesh['expert'=4,'shard'=8] {'shard'}, use_global_device_ids=true, to_apply=%region_47.48.clone | all-reduce | flops 1536 | bytes 6144
  935.3 30.8 %reduce-scatter.31.cloned.1.call-done = bf16[96,12]{1,0:T(8,128)(2,1)} async-done(((bf16[768,12]{1,0:T(8,128)(2,1)}), bf16[96,12]{1,0:T(8,128)(2,1)}) %reduce-scatter.31.cloned.1.call-update) | async-done | bytes 2320
  979.8 33.8 %all-reduce.14.cloned.1.call-done = (bf16[96,768]{1,0:T(8,128)(2,1)}, bf16[96,768]{1,0:T(8,128)(2,1)}, bf16[96,768]{1,0:T(8,128)(2,1)}, bf16[96,768]{1,0:T(8,128)(2,1)}) async-done(((bf16[96,768]{1,0:T(8,128)(2,1)}, bf16[96,768]{1,0:T(8,128)(2,1)}, bf16[96,768]{1,0:T(8,128)(2,1)}, bf16[96,768]{1,0:T(8,128)(2,1)}), (bf16[96,768]{1,0:T(8,128)(2,1)}, bf16[96,768]{1,0:T(8,128)(2,1)}, bf16[96,768]{1,0:T(8,128)(2,1)}, ...) | async-done | bytes 589840 | tf_op jit(solution)/shard_map/psum | solution.py:499
  1020.1 65.3 %reduce-scatter.27.cloned.1.call-done = bf16[2,96,2048]{2,1,0:T(8,128)(2,1)} async-done(((bf16[2,768,2048]{2,1,0:T(8,128)(2,1)}), bf16[2,96,2048]{2,1,0:T(8,128)(2,1)}) %reduce-scatter.27.cloned.1.call-update) | async-done | bytes 786448 | tf_op jit(solution)/shard_map/reduce_scatter | solution.py:352
  1087.9 67.9 %reduce-scatter.25.cloned.1.call-done = bf16[2,96,2048]{2,1,0:T(8,128)(2,1)} async-done(((bf16[2,768,2048]{2,1,0:T(8,128)(2,1)}), bf16[2,96,2048]{2,1,0:T(8,128)(2,1)}) %reduce-scatter.25.cloned.1.call-update) | async-done | bytes 786448 | tf_op jit(solution)/shard_map/reduce_scatter | solution.py:349
  1158.3 67.9 %reduce-scatter.29.cloned.1.call-done = bf16[2,256,768]{2,1,0:T(8,128)(2,1)} async-done(((bf16[2,2048,768]{2,1,0:T(8,128)(2,1)}), bf16[2,256,768]{2,1,0:T(8,128)(2,1)}) %reduce-scatter.29.cloned.1.call-update) | async-done | bytes 786448 | tf_op jit(solution)/shard_map/reduce_scatter | solution.py:355
  (474 shorter events, 500.1 us)
Async XLA Ops:
  7.2 97.7 %all-gather.13.cloned.1.call-start = ((), (), s32[]{:S(2)}) async-start(), calls=%async_computation.15 | async-start | bytes 1327104 | tf_op jit(solution)/shard_map/all_gather | solution.py:188
  7.9 101.5 %all-gather.11.cloned.1.call-start = ((), (), s32[]{:S(2)}) async-start(), calls=%async_computation.14 | async-start | bytes 1327104 | tf_op jit(solution)/shard_map/all_gather | solution.py:187
  8.7 112.1 %all-gather.15.cloned.1.call-start = ((), (), s32[]{:S(2)}) async-start(), calls=%async_computation.16 | async-start | bytes 1327104 | tf_op jit(solution)/shard_map/all_gather | solution.py:189
  9.4 197.5 %all-gather.17.cloned.1.call-start = ((), (), s32[]{:S(2)}) async-start(), calls=%async_computation.17 | async-start | bytes 1327104 | tf_op jit(solution)/shard_map/all_gather | solution.py:190
  10.0 279.4 %all-gather.21.cloned.1.call-start = ((), (), s32[]{:S(2)}) async-start(), calls=%async_computation.19 | async-start | bytes 7077888 | tf_op jit(solution)/shard_map/all_gather | solution.py:220
  10.6 291.5 %all-gather.19.cloned.1.call-start = ((), (), s32[]{:S(2)}) async-start(), calls=%async_computation.18 | async-start | bytes 7077888 | tf_op jit(solution)/shard_map/all_gather | solution.py:219
  11.2 303.0 %all-gather.23.cloned.1.call-start = ((), (), s32[]{:S(2)}) async-start(), calls=%async_computation.20 | async-start | bytes 7077888 | tf_op jit(solution)/shard_map/all_gather | solution.py:221
  15.5 29.4 %copy-start.20 = (bf16[1024,768]{1,0:T(8,128)(2,1)S(1)}, bf16[1024,768]{1,0:T(8,128)(2,1)}, u32[]{:S(2)}) copy-start(bf16[1024,768]{1,0:T(8,128)(2,1)} %param.22) | copy-start | bytes 4718596
  19.1 26.8 %copy-start.88 = (bf16[96,12]{0,1:T(8,128)(2,1)S(1)}, bf16[96,12]{0,1:T(8,128)(2,1)}, u32[]{:S(2)}) copy-start(bf16[96,12]{0,1:T(8,128)(2,1)} %param.33) | copy-start | bytes 6916
  19.4 72.0 %copy-start.7 = (bf16[1024,768]{1,0:T(8,128)(2,1)S(1)}, bf16[1024,768]{1,0:T(8,128)(2,1)}, u32[]{:S(2)}) copy-start(bf16[1024,768]{1,0:T(8,128)(2,1)} %param.39) | copy-start | bytes 4718596
  44.3 76.5 %copy-start.74 = (f32[768]{0:T(1024)}, f32[768]{0:T(1024)S(1)}, u32[]{:S(2)}) copy-start(f32[768]{0:T(1024)S(1)} %convert_element_type.204) | copy-start | bytes 9220
  45.9 74.9 %copy-start.72 = (f32[1024]{0:T(1024)}, f32[1024]{0:T(1024)S(1)}, u32[]{:S(2)}) copy-start(f32[1024]{0:T(1024)S(1)} %get-tuple-element.350) | copy-start | bytes 12292
  61.9 50.5 %copy-start.44 = (f32[1024,32]{0,1:T(8,128)}, f32[1024,32]{0,1:T(8,128)S(1)}, u32[]{:S(2)}) copy-start(f32[1024,32]{0,1:T(8,128)S(1)} %get-tuple-element.357) | copy-start | bytes 393220
  219.3 30.2 %all-to-all-start = ((bf16[8,168,768]{2,1,0:T(8,128)(2,1)}), bf16[8,168,768]{2,1,0:T(8,128)(2,1)}, u32[]{:S(2)}, u32[]{:S(2)}) async-start(bf16[8,168,768]{2,1,0:T(8,128)(2,1)} %bitcast.258), calls=%async_computation | async-start | bytes 4128768 | tf_op jit(solution)/shard_map/all_to_all | solution.py:250
  249.5 38.2 %all-to-all-start.2 = ((bf16[8,168,768]{2,1,0:T(8,128)(2,1)}), bf16[8,168,768]{2,1,0:T(8,128)(2,1)}, u32[]{:S(2)}, u32[]{:S(2)}) async-start(bf16[8,168,768]{2,1,0:T(8,128)(2,1)} %bitcast.257), calls=%async_computation.2 | async-start | bytes 4128768 | tf_op jit(solution)/shard_map/all_to_all | solution.py:298
  254.0 24.9 %copy-start.80 = (pred[1024,2]{0,1:T(4,128)(4,1)}, pred[1024,2]{0,1:T(4,128)(4,1)S(1)}, u32[]{:S(2)}) copy-start(pred[1024,2]{0,1:T(4,128)(4,1)S(1)} %get-tuple-element.346) | copy-start | bytes 6148
  254.0 24.9 %copy-start.81 = (pred[1024,2]{0,1:T(4,128)(4,1)}, pred[1024,2]{0,1:T(4,128)(4,1)S(1)}, u32[]{:S(2)}) copy-start(pred[1024,2]{0,1:T(4,128)(4,1)S(1)} %get-tuple-element.347) | copy-start | bytes 6148
  283.5 107.1 %copy-start.55 = (f32[1024,2]{0,1:T(2,128)}, f32[1024,2]{0,1:T(2,128)S(1)}, u32[]{:S(2)}) copy-start(f32[1024,2]{0,1:T(2,128)S(1)} %reduce_max.28) | copy-start | bytes 24580
  283.5 106.4 %copy-start.63 = (f32[1024,2]{0,1:T(2,128)}, f32[1024,2]{0,1:T(2,128)S(1)}, u32[]{:S(2)}) copy-start(f32[1024,2]{0,1:T(2,128)S(1)} %fusion.63) | copy-start | bytes 24580
  346.8 29.5 %all-to-all-start.1 = ((bf16[2,672,768]{2,0,1:T(2,128)(2,1)}), bf16[2,672,768]{2,0,1:T(2,128)(2,1)S(1)}, u32[]{:S(2)}, u32[]{:S(2)}) async-start(bf16[2,672,768]{2,0,1:T(2,128)(2,1)} %copy.128), calls=%async_computation.1 | async-start | bytes 4128768 | tf_op jit(solution)/shard_map/all_to_all | solution.py:261
  376.3 35.1 %all-to-all-start.3 = ((bf16[2,672,768]{2,0,1:T(2,128)(2,1)}), bf16[2,672,768]{2,0,1:T(2,128)(2,1)}, u32[]{:S(2)}, u32[]{:S(2)}) async-start(bf16[2,672,768]{2,0,1:T(2,128)(2,1)} %copy.140), calls=%async_computation.3 | async-start | bytes 4128768 | tf_op jit(solution)/shard_map/all_to_all | solution.py:338
  380.8 406.0 %reduce-scatter.23.cloned.1.call-start = ((), (), s32[]{:S(2)}) async-start(), calls=%async_computation.24 | async-start | bytes 1327104 | tf_op jit(solution)/shard_map/reduce_scatter | solution.py:481
  514.2 290.2 %reduce-scatter.19.cloned.1.call-start = ((), (), s32[]{:S(2)}) async-start(), calls=%async_computation.22 | async-start | bytes 1327104 | tf_op jit(solution)/shard_map/reduce_scatter | solution.py:475
  771.5 66.2 %reduce-scatter.17.cloned.1.call-start = ((), (), s32[]{:S(2)}) async-start(), calls=%async_computation.21 | async-start | bytes 1327104 | tf_op jit(solution)/shard_map/reduce_scatter | solution.py:472
  775.6 95.6 %reduce-scatter.21.cloned.1.call-start = ((), (), s32[]{:S(2)}) async-start(), calls=%async_computation.23 | async-start | bytes 1327104 | tf_op jit(solution)/shard_map/reduce_scatter | solution.py:478
  781.7 151.7 %reduce-scatter.35.cloned.1.call-start = ((), (), s32[]{:S(2)}) async-start(), calls=%async_computation.30 | async-start | bytes 221184
  783.4 151.0 %reduce-scatter.33.cloned.1.call-start = ((), (), s32[]{:S(2)}) async-start(), calls=%async_computation.29 | async-start | bytes 221184
  785.1 181.0 %reduce-scatter.31.cloned.1.call-start = ((), (), s32[]{:S(2)}) async-start(), calls=%async_computation.28 | async-start | bytes 221184
  786.7 226.8 %all-reduce.14.cloned.1.call-start = ((), (), s32[]{:S(2)}) async-start(), calls=%async_computation.31 | async-start | bytes 1179648 | tf_op jit(solution)/shard_map/psum | solution.py:499
  871.2 214.2 %reduce-scatter.27.cloned.1.call-start = ((), (), s32[]{:S(2)}) async-start(), calls=%async_computation.26 | async-start | bytes 7077888 | tf_op jit(solution)/shard_map/reduce_scatter | solution.py:352
  880.9 274.9 %reduce-scatter.25.cloned.1.call-start = ((), (), s32[]{:S(2)}) async-start(), calls=%async_computation.25 | async-start | bytes 7077888 | tf_op jit(solution)/shard_map/reduce_scatter | solution.py:349
  892.2 334.0 %reduce-scatter.29.cloned.1.call-start = ((), (), s32[]{:S(2)}) async-start(), calls=%async_computation.27 | async-start | bytes 7077888 | tf_op jit(solution)/shard_map/reduce_scatter | solution.py:355
  (94 other events, 586.6 us)
Sparse Core Ops, SparseCore 0:
  9.6 25.4 all-gather.12
  36.8 22.6 all-gather.10
  61.2 22.2 all-gather.14
  84.9 22.4 all-gather.16
  108.8 64.3 all-gather.20
  174.7 63.3 all-gather.18
  239.6 63.4 all-gather.22
  514.3 32.6 reduce-scatter.22
  771.6 32.6 reduce-scatter.18
  806.5 31.1 reduce-scatter.16
  840.0 31.1 reduce-scatter.20
  873.9 28.8 reduce-scatter.34
  905.6 28.7 reduce-scatter.32
  937.1 28.8 reduce-scatter.30
  969.1 44.4 all-reduce.13
  1015.7 69.7 reduce-scatter.26
  1087.6 68.1 reduce-scatter.24
  1158.0 68.1 reduce-scatter.28
where the time goes:
time: 1250 us; the launch traced here: 1240 us
  waiting for transfers between devices  372 us (30%)
  matrix products  316 us (25%)
  local copies, waits for them, and re-layouts  245 us (20%)
  other arithmetic  190 us (15%)
  blocking collectives  75.8 us (6%)
  starting transfers between devices  18.8 us (2%)
  between operations  17.2 us (1%)
    reduce_scatter x1, waiting for transfers between devices, body(): lax.psum_scatter(gate_term.astype(jnp.bfloat16), 'shard', scatter_dimensi...  67.9 us
    reduce_scatter x1, waiting for transfers between devices, body(): lax.psum_scatter(down_term.astype(jnp.bfloat16), 'shard', scatter_dimensi...  67.9 us
    reduce_scatter x1, waiting for transfers between devices, body(): lax.psum_scatter(up_term.astype(jnp.bfloat16), 'shard', scatter_dimension...  65.3 us
    dynamic_update_slice x4, local copies, waits for them, and re-layouts, one_sequence(): outputs, log_sums = lax.map(one_block, (query_blocks, starts))  60.9 us
    dot_general x4, matrix products, block_scores(): jnp.einsum('qhd,khd->hqk', query_block, keys_seq, preferred_element_type=...  44.5 us
    convert_element_type x2, other arithmetic, one_block(): grad_scores = (weights * (grad_probs - row_dot)).astype(jnp.bfloat16)  42.5 us
    dot_general x2, matrix products, one_block(): jnp.einsum('qhd,khd->hqk', grad_blk, values_seq, preferred_element_type=j...  36.3 us
    unnamed x21, waiting for transfers between devices  35.5 us
  transfers between devices with their start and end apart: 22, of which 11 were waited for; matrix products, arithmetic and copies ran while one was open for 48% of the time, Pallas kernels for 0%

commit v1 on v0

v1 whole, which is shorter than its diff:
```python
import functools
import numpy as np
import jax
import jax.numpy as jnp
from jax import lax
from jax.experimental import pallas as pl
from jax.experimental.pallas import tpu as pltpu
from jax.sharding import PartitionSpec as P

HEADS = 12
HEAD_DIM = 64
ZC = 4
TOP = 2
LEN = 1024
EPS = 1e-05
NEG = -1e30
LANES = 128
BLOCK = 256
FTILE = 512
F32 = jnp.float32
BF16 = jnp.bfloat16
VMEM_LIMIT = 56 << 20


def call(body, name, grid, in_specs, out_specs, out_shape, scratch=(), flops=0, traffic=0, trans=0, prefetch=0):
    return pl.pallas_call(
        body,
        name=name,
        grid_spec=pltpu.PrefetchScalarGridSpec(
            num_scalar_prefetch=prefetch,
            grid=grid,
            in_specs=in_specs,
            out_specs=out_specs,
            scratch_shapes=scratch,
        ),
        out_shape=out_shape,
        compiler_params=pltpu.CompilerParams(
            dimension_semantics=("arbitrary",) * len(grid), vmem_limit_bytes=VMEM_LIMIT
        ),
        cost_estimate=pl.CostEstimate(flops=flops, transcendentals=trans, bytes_accessed=traffic),
    )


def mm(a, b):
    return lax.dot_general(a, b, (((1,), (0,)), ((), ())), preferred_element_type=F32)


def mm_nt(a, b):
    return lax.dot_general(a, b, (((1,), (1,)), ((), ())), preferred_element_type=F32)


def mm_tn(a, b):
    return lax.dot_general(a, b, (((0,), (0,)), ((), ())), preferred_element_type=F32)


def iota(shape, axis):
    return lax.broadcasted_iota(jnp.int32, shape, axis)


def whole(shape):
    return pl.BlockSpec(shape, lambda *idx: (0,) * len(shape))


def rows_of(block, width):
    return pl.BlockSpec((block, width), lambda i, *rest: (i, 0))


def split_high_low(values):
    high = values.astype(BF16)
    low = (values - high.astype(F32)).astype(BF16)
    return high, low


def pack_kernel(q, k, v, gain1, gain2, router, mix, vectors, out, scratch):
    rows, width = q.shape
    out[:, 0:width] = q[...]
    out[:, width : 2 * width] = k[...]
    out[:, 2 * width : 3 * width] = v[...]
    base = 3 * width
    out[:, base : base + LANES] = jnp.zeros((rows, LANES), BF16)
    scratch[...] = jnp.zeros_like(scratch)
    scratch[0:1, 0:rows] = gain1[...].astype(F32)
    scratch[1:2, 0:rows] = gain2[...].astype(F32)
    scratch[2:4, 0:rows] = vectors[...].astype(F32)
    columns = scratch[...].T
    n_router = router.shape[1]
    n_mix = mix.shape[1]
    out[:, base : base + n_router] = router[...]
    out[:, base + n_router : base + n_router + n_mix] = mix[...]
    out[:, base + 16 : base + 24] = columns[0:rows, 0:8].astype(BF16)


def slots_kernel(experts, capacity, stride, routes, order_row, order_col, dest_col, dest_row):
    tokens = routes.shape[0]
    r0 = routes[:, 0:1]
    r1 = routes[:, 1:2]
    lane = iota((tokens, LANES), 1)
    hot = jnp.where((lane == r0) | (lane == r1), 1.0, 0.0)
    hot = jnp.where(lane < experts, hot, 0.0).astype(BF16)
    row = iota((tokens, tokens), 0)
    col = iota((tokens, tokens), 1)
    to_turn = jnp.where(order_col[...] == col, 1.0, 0.0).astype(BF16)
    hot_turn = mm(to_turn, hot).astype(BF16)
    earlier = mm(jnp.where(col < row, 1.0, 0.0).astype(BF16), hot_turn)
    earlier = jnp.minimum(earlier, 255.0).astype(BF16)
    to_token = jnp.where(order_row[...] == row, 1.0, 0.0).astype(BF16)
    position = mm(to_token, earlier)
    p0 = jnp.sum(jnp.where(lane == r0, position, 0.0), axis=1, keepdims=True)
    p1 = jnp.sum(jnp.where(lane == r1, position, 0.0), axis=1, keepdims=True)
    d0 = jnp.where((r0 < experts) & (p0 < capacity), r0.astype(F32) * stride + p0, -1.0)
    d1 = jnp.where((r1 < experts) & (p1 < capacity), r1.astype(F32) * stride + p1, -1.0)
    both = jnp.where(lane == 0, d0, jnp.where(lane == 1, d1, 0.0))
    dest_col[...] = both.astype(jnp.int32)
    dest_row[...] = both.T[0:8, :].astype(jnp.int32)


def half_swap(values):
    lane = iota(values.shape, 1) % HEAD_DIM
    half = HEAD_DIM // 2
    return jnp.where(
        lane < half, pltpu.roll(values, LANES - half, 1), pltpu.roll(values, half, 1)
    )


def project_kernel(x, wq, wk, wv, small, cosine, sine, q_out, k_out, v_out, n_out, small_t):
    @pl.when(pl.program_id(0) == 0)
    def _():
        small_t[...] = small[...].astype(F32).T

    width = x.shape[1]
    rows = x[...].astype(F32)
    scale = lax.rsqrt(jnp.mean(rows * rows, axis=1, keepdims=True) + EPS)
    normed = (rows * scale * small_t[16:17, :]).astype(BF16)
    n_out[...] = normed
    cos = cosine[...]
    sin = sine[...]
    for weight, out, factor in ((wq, q_out, HEAD_DIM**-0.5), (wk, k_out, None)):
        lin = mm(normed, weight[...])
        for c in range(width // LANES):
            part = lin[:, c * LANES : (c + 1) * LANES]
            turned = part * cos + half_swap(part) * sin
            if factor is not None:
                turned = turned * factor
            out[:, c * LANES : (c + 1) * LANES] = turned.astype(BF16)
    v_out[...] = mm(normed, wv[...]).astype(BF16)


def attend_kernel(
    prefix, q, k, v, x, wo, small, small_t, prev, routes,
    mix_out, lse_out, res_out, n_out, tok_out, bias, mixed, lse,
):
    block, width = q.shape
    length = k.shape[0]
    start = pl.program_id(0) * block
    limit = jnp.maximum(start + iota((block, 1), 0) + 1, prefix[0])
    bias[...] = jnp.where(iota((block, length), 1) < limit, 0.0, NEG)
    lane = iota((block, LANES), 1)
    first = lane < HEAD_DIM
    lse[...] = jnp.zeros_like(lse)

    def one_pair(pair, carry):
        columns = pl.ds(pl.multiple_of(pair * LANES, LANES), LANES)
        q_pair = q[:, columns]
        k_pair = k[:, columns]
        v_pair = v[:, columns]
        outs = []
        for head in range(2):
            mine = first if head == 0 else jnp.logical_not(first)
            q_head = jnp.where(mine, q_pair, jnp.zeros_like(q_pair))
            scores = mm_nt(q_head, k_pair) + bias[...]
            top = jnp.max(scores, axis=1, keepdims=True)
            weights = jnp.exp(scores - top)
            total = jnp.sum(weights, axis=1, keepdims=True)
            outs.append(mm(weights.astype(BF16), v_pair) / total)
            lse[...] = jnp.where(lane == 2 * pair + head, top + jnp.log(total), lse[...])
        mixed[:, columns] = jnp.where(first, outs[0], outs[1]).astype(BF16)
        return carry

    lax.fori_loop(0, width // LANES, one_pair, 0)
    mix_out[...] = mixed[...]
    lse_out[...] = lse[...].T[0:16, :]
    residual = x[...].astype(F32) + mm(mixed[...], wo[...])
    res_out[...] = residual
    scale = lax.rsqrt(jnp.mean(residual * residual, axis=1, keepdims=True) + EPS)
    normed = (residual * scale * small_t[17:18, :]).astype(BF16)
    n_out[...] = normed
    lin = mm(normed, small[...])
    kinds = prev.shape[1]
    logits = lin[:, 0:kinds] + prev[...]
    kind = iota((block, kinds), 1)
    c0 = jnp.sum(jnp.where(kind == routes[:, 0:1], logits, 0.0), axis=1, keepdims=True)
    c1 = jnp.sum(jnp.where(kind == routes[:, 1:2], logits, 0.0), axis=1, keepdims=True)

    def pair_softmax(a, b):
        top = jnp.maximum(a, b)
        ea = jnp.exp(a - top)
        eb = jnp.exp(b - top)
        total = ea + eb
        return ea / total, eb / total

    g0, g1 = pair_softmax(c0, c1)
    m00, m01 = pair_softmax(lin[:, kinds : kinds + 1], lin[:, kinds + 1 : kinds + 2])
    m10, m11 = pair_softmax(lin[:, kinds + 2 : kinds + 3], lin[:, kinds + 3 : kinds + 4])
    packed = jnp.zeros((block, LANES), F32)
    for index, column in enumerate((g0, g1, m00, m01, m10, m11, scale)):
        packed = jnp.where(lane == index, column, packed)
    tok_out[...] = packed


def dispatch_kernel(normed, grad, tok, routes, dest_row, out, gates):
    expert = pl.program_id(0)
    tokens = normed.shape[0]
    stride = out.shape[3]

    @pl.when(expert == 0)
    def _():
        lane = iota((tokens, LANES), 1)
        kind = lane % HEAD_DIM
        value = jnp.where(kind == routes[:, 0:1], tok[:, 0:1], 0.0)
        value = value + jnp.where(kind == routes[:, 1:2], tok[:, 1:2], 0.0)
        high = value.astype(BF16).astype(F32)
        gates[...] = jnp.where(lane < HEAD_DIM, high, value - high).astype(BF16)

    slot = expert * stride + iota((stride, tokens), 0)
    hit = (dest_row[0:1, :] == slot) | (dest_row[1:2, :] == slot)
    take = jnp.where(hit, 1.0, 0.0).astype(BF16)
    out[0, 0, 0] = mm(take, normed[...]).astype(BF16)
    slot_gates = mm(take, gates[...])
    mine = iota((stride, LANES), 1) % HEAD_DIM == expert
    slot_gate = jnp.sum(jnp.where(mine, slot_gates, 0.0), axis=1, keepdims=True)
    out[0, 1, 0] = (mm(take, grad[...]) * slot_gate).astype(BF16)


def expert_up_kernel(rows, grads, gate, up, hidden, slope, silu_out, down_grad):
    n_src, stride, width = rows.shape[0], rows.shape[3], rows.shape[4]
    r = rows[...].reshape(n_src * stride, width)
    s = grads[...].reshape(n_src * stride, width)
    ftile = gate.shape[-1]
    gate_pre = mm(r, gate[...].reshape(width, ftile))
    up_pre = mm(r, up[...].reshape(width, ftile))
    sig = jax.nn.sigmoid(gate_pre)
    silu = gate_pre * sig
    hid = (silu * up_pre).astype(BF16)
    hidden[0] = hid
    silu_out[0] = silu.astype(BF16)
    slope[0] = (up_pre * (sig + silu * (1.0 - sig))).astype(BF16)
    down_grad[...] = mm_tn(hid, s).astype(BF16).reshape(down_grad.shape)


def expert_down_kernel(
    rows, grads, gate, up, down, hidden, slope, silu, back, grad_out, out_acc, row_acc
):
    step = pl.program_id(0)
    n_src, stride, width = rows.shape[0], rows.shape[3], rows.shape[4]
    count = n_src * stride
    ftile = gate.shape[-1]

    @pl.when(step == 0)
    def _():
        out_acc[...] = jnp.zeros_like(out_acc)
        row_acc[...] = jnp.zeros_like(row_acc)

    r = rows[...].reshape(count, width)
    s = grads[...].reshape(count, width)
    d = down[...].reshape(ftile, width)
    hidden_g = mm_nt(s, d)
    out_acc[...] += mm(hidden[0], d)
    gate_g = (hidden_g * slope[0].astype(F32)).astype(BF16)
    up_g = (hidden_g * silu[0].astype(F32)).astype(BF16)
    row_acc[...] += mm_nt(gate_g, gate[...].reshape(width, ftile)) + mm_nt(
        up_g, up[...].reshape(width, ftile)
    )
    shape = (grad_out.shape[0], grad_out.shape[2], ftile)
    grad_out[:, 0] = mm_tn(r, gate_g).astype(BF16).reshape(shape)
    grad_out[:, 1] = mm_tn(r, up_g).astype(BF16).reshape(shape)

    @pl.when(step == pl.num_programs(0) - 1)
    def _():
        back[:, 0] = out_acc[...].astype(BF16).reshape(n_src, stride, width)
        back[:, 1] = row_acc[...].astype(BF16).reshape(n_src, stride, width)


def combine_kernel(
    experts, eo0, rg0, eo1, rg1, residual, normed, grad, tok, routes, dest, mix, wo, small_t,
    mixed_out, prev_out, resg_out, headg_out, delta_out, wo_out, small_out, wo_acc, small_acc, second_acc,
):
    step = pl.program_id(0)
    block, width = residual.shape
    n_src, stride = eo0.shape[0], eo0.shape[2]
    local = n_src * stride

    @pl.when(step == 0)
    def _():
        wo_acc[...] = jnp.zeros_like(wo_acc)
        small_acc[...] = jnp.zeros_like(small_acc)
        second_acc[...] = jnp.zeros_like(second_acc)

    slot = iota((block, local), 1)
    owner_slot = slot // stride * (2 * stride) + slot % stride

    ep = [None, None]
    back = None
    for l, (eo_ref, rg_ref) in enumerate(((eo0, rg0), (eo1, rg1))):
        ident = owner_slot + l * stride
        t0 = jnp.where(dest[:, 0:1] == ident, 1.0, 0.0)
        t1 = jnp.where(dest[:, 1:2] == ident, 1.0, 0.0)
        eo = eo_ref[...].reshape(local, width)
        rg = rg_ref[...].reshape(local, width)
        e0 = mm(t0.astype(BF16), eo)
        e1 = mm(t1.astype(BF16), eo)
        b = mm((t0 + t1).astype(BF16), rg)
        ep[0] = e0 if ep[0] is None else ep[0] + e0
        ep[1] = e1 if ep[1] is None else ep[1] + e1
        back = b if back is None else back + b

    res = residual[...]
    n_low = normed[...]
    nf = n_low.astype(F32)
    g_low = grad[...]
    g = g_low.astype(F32)
    gate = [tok[:, 0:1], tok[:, 1:2]]
    mw = [[tok[:, 2:3], tok[:, 3:4]], [tok[:, 4:5], tok[:, 5:6]]]
    scale = tok[:, 6:7]
    vec = [small_t[18:19, :], small_t[19:20, :]]
    along_n = jnp.sum(g * nf, axis=1, keepdims=True)
    along_vec = [jnp.sum(g * vec[c], axis=1, keepdims=True) for c in range(2)]
    gate_g = []
    on_n = 0.0
    sel = [0.0, 0.0]
    copy_weight = 0.0
    for t in range(TOP):
        route = routes[:, t : t + 1]
        is_copy = jnp.where(route == experts + 1, 1.0, 0.0)
        is_const = [jnp.where(route == experts + 2 + c, 1.0, 0.0) for c in range(2)]
        a = is_copy + is_const[0] * mw[0][0] + is_const[1] * mw[1][0]
        b = [is_const[c] * mw[c][1] for c in range(2)]
        gate_g.append(
            jnp.sum(g * ep[t], axis=1, keepdims=True)
            + a * along_n
            + b[0] * along_vec[0]
            + b[1] * along_vec[1]
        )
        on_n = on_n + gate[t] * a
        copy_weight = copy_weight + gate[t] * is_copy
        sel = [sel[c] + gate[t] * is_const[c] for c in range(2)]
    vec_w = [sel[c] * mw[c][1] for c in range(2)]
    mixed_out[...] = (
        res + gate[0] * ep[0] + gate[1] * ep[1] + on_n * nf + vec_w[0] * vec[0] + vec_w[1] * vec[1]
    ).astype(BF16)

    centre = gate[0] * gate_g[0] + gate[1] * gate_g[1]
    pair_g = [gate[t] * (gate_g[t] - centre) for t in range(TOP)]
    lane = iota((block, LANES), 1)
    logit_g = jnp.where(lane == routes[:, 0:1], pair_g[0], 0.0)
    logit_g = logit_g + jnp.where(lane == routes[:, 1:2], pair_g[1], 0.0)
    kinds = prev_out.shape[1]
    prev_out[...] = logit_g[:, 0:kinds]
    for c in range(2):
        w0 = sel[c] * along_n
        w1 = sel[c] * along_vec[c]
        mid = mw[c][0] * w0 + mw[c][1] * w1
        logit_g = jnp.where(lane == kinds + 2 * c, mw[c][0] * (w0 - mid), logit_g)
        logit_g = jnp.where(lane == kinds + 2 * c + 1, mw[c][1] * (w1 - mid), logit_g)
    high, low = split_high_low(logit_g)
    table = small_t[...]
    table = jnp.where(iota(table.shape, 0) < 16, table, 0.0).astype(BF16)
    direct = copy_weight + sel[0] * mw[0][0] + sel[1] * mw[1][0]
    normed_g = back + direct * g + mm(high, table) + mm(low, table)
    gain = small_t[17:18, :]
    scaled = normed_g * gain
    second_acc[...] += jnp.sum(
        (normed_g * res * scale).reshape(block // 8, 8, width), axis=0
    )
    resg = g + scale * scaled - res * (scale * scale * scale) * jnp.mean(
        scaled * res, axis=1, keepdims=True
    )
    resg_out[...] = resg
    attn_g = resg.astype(BF16)
    am = mix[...]
    wo_acc[...] += mm_tn(am, attn_g)
    heads_g = mm_nt(attn_g, wo[...]).astype(BF16)
    headg_out[...] = heads_g
    product = heads_g.astype(F32) * am.astype(F32)
    p_high, p_low = split_high_low(product)
    head_of = jnp.where(
        iota((16, width), 1) // HEAD_DIM == iota((16, width), 0), 1.0, 0.0
    ).astype(BF16)
    delta_out[...] = mm_nt(head_of, p_high) + mm_nt(head_of, p_low)
    small_acc[...] += mm_tn(n_low, high) + mm_tn(n_low, low)
    coefficient = jnp.where(lane == 18, vec_w[0], jnp.where(lane == 19, vec_w[1], 0.0))
    c_high, c_low = split_high_low(coefficient)
    small_acc[...] += mm_tn(g_low, c_high) + mm_tn(g_low, c_low)

    @pl.when(step == pl.num_programs(0) - 1)
    def _():
        wo_out[...] = wo_acc[...].astype(BF16)
        second = jnp.sum(second_acc[...], axis=0, keepdims=True)
        row = iota((LANES, width), 0)
        small_out[...] = small_acc[...] + jnp.where(row == 17, second, 0.0).T


def attend_back_kernel(
    prefix, q, k, v, grad, lse, delta, cosine, sine, dq_out, dk_out, dv_out, bias, dq_acc
):
    length = q.shape[0]
    pair = pl.program_id(0)
    block = BLOCK
    lane_all = iota((length, LANES), 1)
    lane = iota((block, LANES), 1)

    @pl.when(pair == 0)
    def _():
        limit = jnp.maximum(iota((1, length), 1) + 1, prefix[0])
        bias[...] = jnp.where(iota((length, length), 0) < limit, 0.0, NEG).astype(BF16)

    q_pair = q[...]
    g_pair = grad[...]
    zero = jnp.zeros_like(q_pair)
    q_head = []
    g_head = []
    for head in range(2):
        mine = (lane_all // HEAD_DIM) == head
        q_head.append(jnp.where(mine, q_pair, zero))
        g_head.append(jnp.where(mine, g_pair, zero))
    dq_acc[...] = jnp.zeros_like(dq_acc)

    def one_block(index, carry):
        place = pl.ds(pl.multiple_of(index * block, block), block)
        k_pair = k[place, :]
        v_pair = v[place, :]
        dk = None
        dv = None
        for head in range(2):
            mine = (lane // HEAD_DIM) == head
            k_head = jnp.where(mine, k_pair, jnp.zeros_like(k_pair))
            lse_row = lse[pl.ds(2 * pair + head, 1), :]
            delta_row = delta[pl.ds(2 * pair + head, 1), :]
            scores = mm_nt(k_pair, q_head[head]) + bias[place, :].astype(F32)
            weights = jnp.exp(scores - lse_row)
            probs_g = mm_nt(v_pair, g_head[head])
            one_dv = mm(weights.astype(BF16), g_head[head])
            scores_g = (weights * (probs_g - delta_row)).astype(BF16)
            one_dk = mm(scores_g, q_head[head])
            dq_acc[...] += mm_tn(scores_g, k_head)
            dk = one_dk if dk is None else dk + one_dk
            dv = one_dv if dv is None else dv + one_dv
        cos = cosine[place, :]
        sin = sine[place, :]
        dk_out[place, :] = (dk * cos - half_swap(dk) * sin).astype(BF16)
        dv_out[place, :] = dv.astype(BF16)
        return carry

    lax.fori_loop(0, length // block, one_block, 0)
    dq = dq_acc[...] * (HEAD_DIM**-0.5)
    dq_out[...] = (dq * cosine[...] - half_swap(dq) * sine[...]).astype(BF16)


def project_back_kernel(
    x, normed, dq, dk, dv, resg, wq, wk, wv, small_t, small_g, tok_out, grad_out, acc, first_acc
):
    step = pl.program_id(0)
    block, width = x.shape

    @pl.when(step == 0)
    def _():
        acc[...] = jnp.zeros_like(acc)
        first_acc[...] = jnp.zeros_like(first_acc)

    rows = x[...].astype(F32)
    scale = lax.rsqrt(jnp.mean(rows * rows, axis=1, keepdims=True) + EPS)
    normed_g = mm_nt(dq[...], wq[...]) + mm_nt(dk[...], wk[...]) + mm_nt(dv[...], wv[...])
    n_low = normed[...]
    for index, part in enumerate((dq, dk, dv)):
        acc[:, index * width : (index + 1) * width] += mm_tn(n_low, part[...])
    first_acc[...] += jnp.sum(
        (normed_g * rows * scale).reshape(block // 8, 8, width), axis=0
    )
    scaled = normed_g * small_t[16:17, :]
    tok_out[...] = resg[...] + scale * scaled - rows * (scale * scale * scale) * jnp.mean(
        scaled * rows, axis=1, keepdims=True
    )

    @pl.when(step == pl.num_programs(0) - 1)
    def _():
        grad_out[:, 0 : 3 * width] = acc[...].astype(BF16)
        first = jnp.sum(first_acc[...], axis=0, keepdims=True)
        row = iota((LANES, width), 0)
        extra = small_g[...] + jnp.where(row == 16, first, 0.0).T
        grad_out[:, 3 * width : 3 * width + LANES] = extra.astype(BF16)


def rotary_tables():
    half = HEAD_DIM // 2
    frequency = np.float32(10000.0) ** (
        -np.arange(half, dtype=np.float32) * np.float32(2.0) / np.float32(HEAD_DIM)
    )
    angles = np.arange(LEN, dtype=np.float32)[:, None] * frequency[None, :].astype(np.float32)
    cos = np.cos(angles.astype(np.float64)).astype(np.float32)
    sin = np.sin(angles.astype(np.float64)).astype(np.float32)
    return np.tile(cos, (1, 4)), np.tile(np.concatenate([-sin, sin], axis=1), (1, 2))


def body(
    tokens, previous_logits, routes, prefix, slot_order, first_gain, query_weight, key_weight,
    value_weight, output_weight, second_gain, router_weight, constant_mix, constant_vectors,
    gate_weight, up_weight, down_weight, cotangent,
):
    owners = lax.axis_size("expert")
    shards = lax.axis_size("shard")
    local_experts, shard_rows, ff = gate_weight.shape
    experts = local_experts * owners
    count, width = tokens.shape
    kinds = experts + ZC
    capacity = count * TOP // kinds // 8 * 8
    stride = -(-capacity // 16) * 16
    ftile = FTILE
    fsteps = ff // ftile
    down_rows = down_weight.shape[1]
    per_tile = ftile // down_rows
    packed_width = 3 * width + LANES
    cosine, sine = (jnp.asarray(t) for t in rotary_tables())
    struct = jax.ShapeDtypeStruct

    packed = call(
        pack_kernel, "pack", (1,),
        [whole((shard_rows, width))] * 3
        + [whole((1, shard_rows))] * 2
        + [whole((shard_rows, kinds)), whole((shard_rows, 4)), whole((2, shard_rows))],
        whole((shard_rows, packed_width)),
        struct((shard_rows, packed_width), BF16),
        scratch=[pltpu.VMEM((8, LANES), F32)],
        traffic=1 << 20,
    )(
        query_weight, key_weight, value_weight, first_gain[None], second_gain[None],
        router_weight, constant_mix, constant_vectors,
    )
    qkv_full = lax.all_gather(packed, "shard", axis=0, tiled=True)
    output_full = lax.all_gather(output_weight, "shard", axis=0, tiled=True)
    gate_up = jnp.stack([gate_weight, up_weight], axis=1)
    gate_up_full = lax.all_gather(gate_up, "shard", axis=0, tiled=False)
    down_full = lax.all_gather(down_weight, "shard", axis=0, tiled=False)

    dest_col, dest_row = call(
        functools.partial(slots_kernel, experts, capacity, stride), "slots", (1,),
        [whole((count, TOP)), whole((1, count)), whole((count, 1))],
        [whole((count, LANES)), whole((8, count))],
        [struct((count, LANES), jnp.int32), struct((8, count), jnp.int32)],
        flops=2 * 3 * count * count * LANES, traffic=1 << 20,
    )(routes, slot_order, slot_order.reshape(count, 1))

    steps = count // BLOCK
    weight_block = [
        pl.BlockSpec((width, width), lambda i, *rest, j=j: (0, j)) for j in range(3)
    ]
    small_block = pl.BlockSpec((width, LANES), lambda i, *rest: (0, 3 * width // LANES))
    wide = rows_of(BLOCK, width)
    table = rows_of(BLOCK, LANES)
    act = struct((count, width), BF16)
    queries, keys, values, normed_one, small_t = call(
        project_kernel, "project", (steps,),
        [wide] + weight_block + [small_block, table, table],
        [wide] * 4 + [whole((LANES, width))],
        [act] * 4 + [struct((LANES, width), F32)],
        flops=6 * count * width * width, traffic=12 << 20,
    )(tokens, qkv_full, qkv_full, qkv_full, qkv_full, cosine, sine)

    attn_mix, lse, residual, normed_two, tok = call(
        attend_kernel, "attend", (steps,),
        [wide, whole((count, width)), whole((count, width)), wide, whole((width, width)),
         small_block, whole((LANES, width)), rows_of(BLOCK, kinds), rows_of(BLOCK, TOP)],
        [wide, pl.BlockSpec((16, BLOCK), lambda i, *rest: (0, i)), wide, wide, table],
        [act, struct((16, count), F32), struct((count, width), F32), act,
         struct((count, LANES), F32)],
        scratch=[pltpu.VMEM((BLOCK, count), F32), pltpu.VMEM((BLOCK, width), BF16),
                 pltpu.VMEM((BLOCK, LANES), F32)],
        flops=30 << 30, traffic=16 << 20, trans=HEADS * count * count, prefetch=1,
    )(prefix, queries, keys, values, tokens, output_full, qkv_full, small_t,
      previous_logits, routes)

    send = call(
        dispatch_kernel, "dispatch", (experts,),
        [whole((count, width)), whole((count, width)), whole((count, LANES)),
         whole((count, TOP)), whole((8, count))],
        pl.BlockSpec(
            (1, 2, 1, stride, width),
            lambda e: (e // local_experts, 0, e % local_experts, 0, 0),
        ),
        struct((owners, 2, local_experts, stride, width), BF16),
        scratch=[pltpu.VMEM((count, LANES), BF16)],
        flops=4 * experts * stride * count * width, traffic=8 << 20,
    )(normed_two, cotangent, tok, routes, dest_row)
    received = lax.all_to_all(send, "expert", split_axis=0, concat_axis=0, tiled=True)

    aligned = shard_rows % 16 == 0
    if aligned:
        chunks, chunk_rows = shards, shard_rows
        gate_up_kernel = gate_up_full
    else:
        chunks, chunk_rows = 1, width
        gate_up_kernel = gate_up_full.transpose(1, 2, 0, 3, 4).reshape(
            1, local_experts, 2, width, ff
        )
    local = owners * stride

    def part(kind, pick):
        return pl.BlockSpec(
            (owners, 1, 1, stride, width), lambda *idx: (0, kind, pick(*idx), 0, 0)
        )

    expert_flops = 2 * local * width * ff
    hidden_block = pl.BlockSpec((1, local, ftile), lambda l, f: (l, 0, f))
    hidden_shape = struct((local_experts, local, ff), BF16)
    hidden, slope, silu, down_grad = call(
        expert_up_kernel, "expert_up", (local_experts, fsteps),
        [part(0, lambda l, f: l), part(1, lambda l, f: l)]
        + [
            pl.BlockSpec((chunks, 1, 1, chunk_rows, ftile), lambda l, f, j=j: (0, l, j, 0, f))
            for j in range(2)
        ],
        [hidden_block] * 3
        + [pl.BlockSpec((per_tile, 1, down_rows, width), lambda l, f: (f, l, 0, 0))],
        [hidden_shape] * 3 + [struct((shards, local_experts, down_rows, width), BF16)],
        flops=3 * local_experts * expert_flops, traffic=35 << 20,
        trans=local_experts * local * ff,
    )(received, received, gate_up_kernel, gate_up_kernel)
    down_sum = lax.psum_scatter(down_grad, "shard", scatter_dimension=0, tiled=False)

    returned = []
    gate_up_sums = []
    for l in range(local_experts):
        pick = lambda f, l=l: l
        hid = pl.BlockSpec((1, local, ftile), lambda f, l=l: (l, 0, f))
        back, gu_grad = call(
            expert_down_kernel, "expert_down", (fsteps,),
            [part(0, pick), part(1, pick)]
            + [
                pl.BlockSpec(
                    (chunks, 1, 1, chunk_rows, ftile), lambda f, j=j, l=l: (0, l, j, 0, f)
                )
                for j in range(2)
            ]
            + [pl.BlockSpec((per_tile, 1, down_rows, width), lambda f, l=l: (f, l, 0, 0))]
            + [hid] * 3,
            [whole((owners, 2, stride, width)),
             pl.BlockSpec((chunks, 2, chunk_rows, ftile), lambda f: (0, 0, 0, f))],
            [struct((owners, 2, stride, width), BF16),
             struct((chunks, 2, chunk_rows, ff), BF16)],
            scratch=[pltpu.VMEM((local, width), F32)] * 2,
            flops=6 * expert_flops, traffic=30 << 20,
        )(received, received, gate_up_kernel, gate_up_kernel, down_full, hidden, slope, silu)
        if not aligned:
            gu_grad = gu_grad.reshape(2, shards, shard_rows, ff).transpose(1, 0, 2, 3)
        gate_up_sums.append(
            lax.psum_scatter(gu_grad, "shard", scatter_dimension=0, tiled=False)
        )
        returned.append(
            lax.all_to_all(back, "expert", split_axis=0, concat_axis=0, tiled=True)
        )

    def kind_block(kind):
        return pl.BlockSpec((owners, 1, stride, width), lambda i: (0, kind, 0, 0))

    mixed, previous_grad, residual_grad, heads_grad, delta, output_grad, small_grad = call(
        functools.partial(combine_kernel, experts), "combine", (steps,),
        [kind_block(0), kind_block(1)] * 2
        + [wide, wide, wide, table, rows_of(BLOCK, TOP), table, wide, whole((width, width)),
           whole((LANES, width))],
        [wide, rows_of(BLOCK, kinds), wide, wide, pl.BlockSpec((16, BLOCK), lambda i: (0, i)),
         whole((width, width)), whole((width, LANES))],
        [act, struct((count, kinds), F32), struct((count, width), F32), act,
         struct((16, count), F32), struct((width, width), BF16), struct((width, LANES), F32)],
        scratch=[pltpu.VMEM((width, width), F32), pltpu.VMEM((width, LANES), F32),
                 pltpu.VMEM((8, width), F32)],
        flops=6 * count * 2 * local * width + 4 * count * width * width, traffic=24 << 20,
    )(returned[0], returned[0], returned[1], returned[1], residual, normed_two, cotangent, tok,
      routes, dest_col, attn_mix, output_full, small_t)
    output_sum = lax.psum_scatter(output_grad, "shard", scatter_dimension=0, tiled=True)

    pair_block = pl.BlockSpec((count, LANES), lambda i, *rest: (0, i))
    dq, dk, dv = call(
        attend_back_kernel, "attend_back", (width // LANES,),
        [pair_block] * 4
        + [whole((16, count))] * 2
        + [whole((count, LANES))] * 2,
        [pair_block] * 3,
        [act] * 3,
        scratch=[pltpu.VMEM((count, count), BF16), pltpu.VMEM((count, LANES), F32)],
        flops=60 << 30, traffic=12 << 20, trans=HEADS * count * count, prefetch=1,
    )(prefix, queries, keys, values, heads_grad, lse, delta, cosine, sine)

    tokens_grad, dense_grad = call(
        project_back_kernel, "project_back", (steps,),
        [wide] * 6 + weight_block + [whole((LANES, width)), whole((width, LANES))],
        [wide, whole((width, packed_width))],
        [struct((count, width), F32), struct((width, packed_width), BF16)],
        scratch=[pltpu.VMEM((width, 3 * width), F32), pltpu.VMEM((8, width), F32)],
        flops=12 * count * width * width, traffic=24 << 20,
    )(tokens, normed_one, dq, dk, dv, residual_grad, qkv_full, qkv_full, qkv_full, small_t,
      small_grad)
    dense_sum = lax.psum_scatter(dense_grad, "shard", scatter_dimension=0, tiled=True)
    dense_all = lax.all_gather(
        jnp.concatenate([dense_sum, output_sum], axis=1), "expert", axis=0, tiled=False
    )
    dense = jnp.sum(dense_all.astype(F32), axis=0)
    small = dense[:, 3 * width : 3 * width + LANES]
    gate_sum = jnp.stack([s[0] for s in gate_up_sums]).astype(F32)
    up_sum = jnp.stack([s[1] for s in gate_up_sums]).astype(F32)
    return (
        mixed,
        tokens_grad,
        previous_grad,
        dense[:, 0:width],
        dense[:, width : 2 * width],
        dense[:, 2 * width : 3 * width],
        dense[:, packed_width:],
        small[:, 0:kinds],
        small[:, kinds : kinds + 4],
        small[:, 18:20].T,
        small[:, 16],
        small[:, 17],
        gate_sum,
        up_sum,
        down_sum.astype(F32),
    )


def solution(mesh):
    rows = P(("expert", "shard"), None)
    expert = P("expert", "shard", None)
    flat = P("shard", None)
    return jax.shard_map(
        body,
        mesh=mesh,
        in_specs=(
            rows, rows, rows, P(("expert", "shard")), rows, P("shard"), flat, flat, flat, flat,
            P("shard"), flat, flat, P(None, "shard"), expert, expert, expert, rows,
        ),
        out_specs=(
            rows, rows, rows, flat, flat, flat, flat, flat, flat, P(None, "shard"), P("shard"),
            P("shard"), expert, expert, expert,
        ),
        check_vma=False,
    )
```

time: 1250 us -> 740 us (0.59); the launches traced: 1240 us -> 739 us
  matrix products: 316 us -> 0 us
  local copies, waits for them, and re-layouts: 245 us -> 24.1 us
  Pallas kernels: 0 us -> 218 us
  other arithmetic: 190 us -> 9.73 us
  waiting for transfers between devices: 372 us -> 433 us
  blocking collectives: 75.8 us -> 30.5 us
    dot_general x43 -> x0, matrix products: 316 us -> none  [the longest x4 44.5 us: block_scores(): jnp.einsum('qhd,khd->hqk', query_block, keys_seq, preferred_element_type=...]
    pallas_call x0 -> x11, Pallas kernels: none -> 218 us  [the longest x1 46.4 us: body(): call(attend_back_kernel, 'attend_back', (width // LANES,), [pair_block] *...]
    all_gather x7 -> x5, waiting for transfers between devices: 0.06 us -> 178 us  [the longest x1 63.6 us: body(): gate_up_full = lax.all_gather(gate_up, 'shard', axis=0, tiled=False)]
    convert_element_type x22 -> x2, other arithmetic: 71.7 us -> 4.25 us  [the longest x1 2.38 us: body(): down_sum.astype(F32)]
    reduce_sum x14 -> x1, other arithmetic: 68.6 us -> 2.21 us  [body(): dense = jnp.sum(dense_all.astype(F32), axis=0)]
    dynamic_update_slice x4 -> x0, local copies, waits for them, and re-layouts: 60.9 us -> none  [one_sequence(): outputs, log_sums = lax.map(one_block, (query_blocks, starts))]
    reduce_scatter x7 -> x5, waiting for transfers between devices: 286 us -> 245 us  [the longest x2 137 us: body(): lax.psum_scatter(gu_grad, 'shard', scatter_dimension=0, tiled=False)]
    gather x5 -> x0, local copies, waits for them, and re-layouts: 35.3 us -> none  [the longest x1 11.9 us: body(): expert_pair = returned_pad[pair_dest].astype(jnp.float32)]
  transfers between devices with their start and end apart: 22 -> 12, of which waited for: 11 -> 10; matrix products, arithmetic and copies ran while one was open for 48% -> 3% of each run, Pallas kernels for 0% -> 23%
where the time goes in v1:
time: 740 us; the launch traced here: 739 us
  waiting for transfers between devices  433 us (59%)
  Pallas kernels  218 us (29%)
  blocking collectives  30.5 us (4%)
  local copies, waits for them, and re-layouts  24.1 us (3%)
  between operations  14.9 us (2%)
  other arithmetic  9.73 us (1%)
  starting transfers between devices  9.06 us (1%)
    reduce_scatter x2, waiting for transfers between devices, body(): lax.psum_scatter(gu_grad, 'shard', scatter_dimension=0, tiled=False)  137 us
    reduce_scatter x1, waiting for transfers between devices, body(): lax.psum_scatter(down_grad, 'shard', scatter_dimension=0, tiled=False)  67.5 us
    all_gather x1, waiting for transfers between devices, body(): gate_up_full = lax.all_gather(gate_up, 'shard', axis=0, tiled=False)  63.6 us
    pallas_call x1, Pallas kernels, body(): call(attend_back_kernel, 'attend_back', (width // LANES,), [pair_block] *...  46.4 us
    reduce_scatter x1, waiting for transfers between devices, body(): lax.psum_scatter(dense_grad, 'shard', scatter_dimension=0, tiled=True)  40.4 us
    pallas_call x2, Pallas kernels, body(): call(expert_down_kernel, 'expert_down', (fsteps,), [part(0, pick), part(1...  40.4 us
    pallas_call x1, Pallas kernels, body(): call(attend_kernel, 'attend', (steps,), [wide, whole((count, width)), who...  39 us
    all_gather x1, waiting for transfers between devices, body(): lax.all_gather(jnp.concatenate([dense_sum, output_sum], axis=1), 'expert'...  35.3 us
  transfers between devices with their start and end apart: 12, of which 10 were waited for; matrix products, arithmetic and copies ran while one was open for 3% of the time, Pallas kernels for 23%

profile of v1, /device:TPU:0, one launch (start us, length us, event | category | flops | bytes accessed | tf_op | source)
XLA Modules:
  0.0 738.9 jit_solution(5334657428957253180)
XLA Ops:
  7.2 1.5 copy.75.router
  8.8 1.4 copy.76.mix
  10.1 2.0 pack.1
  13.0 1.3 pad_maximum_fusion
  18.7 6.8 slots.1
  25.5 32.6 %all-gather.9.cloned.1.call-done.wq.wk.wv.small = bf16[768,2432]{1,0:T(8,128)(2,1)} async-done(((bf16[96,2432]{1,0:T(8,128)(2,1)}), bf16[768,2432]{1,0:T(8,128)(2,1)}) %all-gather.9.cloned.1.call-update) | async-done | bytes 3735568 | tf_op jit(solution)/shard_map/all_gather | solution.py:537
  58.2 8.7 %project.1 = (bf16[1024,768]{1,0:T(8,128)(2,1)}, bf16[1024,768]{1,0:T(8,128)(2,1)}, bf16[1024,768]{1,0:T(8,128)(2,1)}, bf16[1024,768]{1,0:T(8,128)(2,1)}, f32[128,768]{1,0:T(8,128)}) custom-call(bf16[1024,768]{1,0:T(8,128)(2,1)} %x.5, bf16[768,2432]{1,0:T(8,128)(2,1)} %all-gather.9.cloned.1.call-done.wq.wk.wv.small, ...), custom_call_target="tpu_custom_call" | custom-call | flops 3623878656 | bytes 12582912 | tf_op jit(solution)/shard_map/project/pallas_call | solution.py:559
  66.9 14.6 %all-gather.11.cloned.1.call-done.wo = bf16[768,768]{1,0:T(8,128)(2,1)} async-done(((bf16[96,768]{1,0:T(8,128)(2,1)}), bf16[768,768]{1,0:T(8,128)(2,1)}) %all-gather.11.cloned.1.call-update) | async-done | bytes 1179664 | tf_op jit(solution)/shard_map/all_gather | solution.py:538
  81.4 39.0 %attend.1 = (bf16[1024,768]{1,0:T(8,128)(2,1)}, f32[16,1024]{1,0:T(8,128)}, f32[1024,768]{1,0:T(8,128)}, bf16[1024,768]{1,0:T(8,128)(2,1)}, f32[1024,128]{1,0:T(8,128)}) custom-call(s32[1]{0:T(128)S(6)} %copy.88.prefix, bf16[1024,768]{1,0:T(8,128)(2,1)} %get-tuple-element.47.q, bf16[1024,768]{1,0:T(8,128)(2,1)} %get-tuple-element.48.k, ...), custom_call_target="tpu_custom_call" | custom-call | flops 32212254720 | bytes 16777216 | tf_op jit(solution)/shard_map/attend/pallas_call | solution.py:567
  120.4 10.9 %dispatch.1 = bf16[4,2,2,176,768]{4,3,2,1,0:T(8,128)(2,1)} custom-call(bf16[1024,768]{1,0:T(8,128)(2,1)} %get-tuple-element.51.normed, bf16[1024,768]{1,0:T(8,128)(2,1)} %grad.3, f32[1024,128]{1,0:T(8,128)} %get-tuple-element.52.tok, s32[1024,2]{1,0:T(8,128)} %copy.78.routes, s32[8,1024]{1,0:T(8,128)} %get-tuple-element.53.dest_row), custom_call_target="tpu_custom_call" | custom-call | flops 4429185024 | bytes 8388608 | tf_op jit(solution)/shard_map/dispatch/pallas_call | solution.py:580
  131.3 5.0 all-to-all-start
  136.4 63.6 %all-gather.13.cloned.1.call-done = bf16[16,2,96,2048]{3,2,0,1:T(8,128)(2,1)} async-done(((bf16[2,2,96,2048]{3,2,0,1:T(8,128)(2,1)}), bf16[16,2,96,2048]{3,2,0,1:T(8,128)(2,1)}) %all-gather.13.cloned.1.call-update) | async-done | bytes 12582928 | tf_op jit(solution)/shard_map/all_gather | solution.py:540
  200.0 11.0 %copy.82 = bf16[16,2,96,2048]{3,2,1,0:T(8,128)(2,1)} copy(bf16[16,2,96,2048]{3,2,0,1:T(8,128)(2,1)} %all-gather.13.cloned.1.call-done) | data formatting | bytes 25165824 | tf_op jit(solution)/shard_map/all_gather | solution.py:540
  211.0 21.7 %expert_up.1 = (bf16[2,704,2048]{2,1,0:T(8,128)(2,1)}, bf16[2,704,2048]{2,1,0:T(8,128)(2,1)}, bf16[2,704,2048]{2,1,0:T(8,128)(2,1)}, bf16[8,2,256,768]{3,2,1,0:T(8,128)(2,1)}) custom-call(bf16[4,2,2,176,768]{4,3,2,1,0:T(8,128)(2,1)} %all-to-all-done.rows.grads, bf16[4,2,2,176,768]{4,3,2,1,0:T(8,128)(2,1)} %all-to-all-done.rows.grads, ...), custom_call_target="tpu_custom_call" | custom-call | flops 13287555072 | bytes 36700160 | tf_op jit(solution)/shard_map/expert_up/pallas_call | solution.py:613
  232.7 31.7 %all-gather.15.cloned.1.call-done = bf16[16,256,768]{2,1,0:T(8,128)(2,1)} async-done(((bf16[2,256,768]{2,1,0:T(8,128)(2,1)}), bf16[16,256,768]{2,1,0:T(8,128)(2,1)}) %all-gather.15.cloned.1.call-update) | async-done | bytes 6291472 | tf_op jit(solution)/shard_map/all_gather | solution.py:541
  264.4 20.2 %expert_down.3 = (bf16[4,2,176,768]{3,2,1,0:T(8,128)(2,1)}, bf16[8,2,96,2048]{3,2,1,0:T(8,128)(2,1)}) custom-call(bf16[4,2,2,176,768]{4,3,2,1,0:T(8,128)(2,1)} %all-to-all-done.rows.grads, bf16[4,2,2,176,768]{4,3,2,1,0:T(8,128)(2,1)} %all-to-all-done.rows.grads, bf16[8,2,2,96,2048]{4,3,2,1,0:T(8,128)(2,1)} %bitcast.24, ...), custom_call_target="tpu_custom_call" | custom-call | flops 13287555072 | bytes 31457280 | tf_op jit(solution)/shard_map/expert_down/pallas_call | solution.py:633
  284.6 3.6 all-to-all-start.2
  288.3 20.2 %expert_down.2 = (bf16[4,2,176,768]{3,2,1,0:T(8,128)(2,1)}, bf16[8,2,96,2048]{3,2,1,0:T(8,128)(2,1)}) custom-call(bf16[4,2,2,176,768]{4,3,2,1,0:T(8,128)(2,1)} %all-to-all-done.rows.grads, bf16[4,2,2,176,768]{4,3,2,1,0:T(8,128)(2,1)} %all-to-all-done.rows.grads, bf16[8,2,2,96,2048]{4,3,2,1,0:T(8,128)(2,1)} %bitcast.26, ...), custom_call_target="tpu_custom_call" | custom-call | flops 13287555072 | bytes 31457280 | tf_op jit(solution)/shard_map/expert_down/pallas_call | solution.py:633
  308.5 6.0 all-to-all-done.2.eo1.rg1
  314.5 30.5 %all_to_all.15.eo0.rg0 = bf16[4,2,176,768]{3,2,1,0:T(8,128)(2,1)} all-to-all(bf16[4,2,176,768]{3,2,1,0:T(8,128)(2,1)} %get-tuple-element.57), channel_id=1, replica_groups=mesh['expert'=4,'shard'=8] {'expert'}, dimensions={0} | all-to-all | bytes 4325376 | tf_op jit(solution)/shard_map/all_to_all | solution.py:657
  345.0 26.8 %combine.1 = (bf16[1024,768]{1,0:T(8,128)(2,1)}, f32[1024,12]{1,0:T(8,128)}, f32[1024,768]{1,0:T(8,128)}, bf16[1024,768]{1,0:T(8,128)(2,1)}, f32[16,1024]{1,0:T(...) custom-call(bf16[4,2,176,768]{3,2,1,0:T(8,128)(2,1)} %all_to_all.15.eo0.rg0, ...), custom_call_target="tpu_custom_call" | custom-call | flops 9059696640 | bytes 25165824 | tf_op jit(solution)/shard_map/combine/pallas_call | solution.py:663
  371.9 46.4 %attend_back.1 = (bf16[1024,768]{1,0:T(8,128)(2,1)}, bf16[1024,768]{1,0:T(8,128)(2,1)}, bf16[1024,768]{1,0:T(8,128)(2,1)}) custom-call(s32[1]{0:T(128)S(6)} %copy.88.prefix, bf16[1024,768]{1,0:T(8,128)(2,1)} %get-tuple-element.47.q, bf16[1024,768]{1,0:T(8,128)(2,1)} %get-tuple-element.48.k, bf16[1024,768]{1,0:T(8,128)(2,1)} %get-tuple-element.49.v, ...), custom_call_target="tpu_custom_call" | custom-call | flops 64424509440 | bytes 12582912 | tf_op jit(solution)/shard_map/attend_back/pallas_call | solution.py:680
  418.3 15.2 %project_back.1 = (f32[1024,768]{1,0:T(8,128)}, bf16[768,2432]{1,0:T(8,128)(2,1)}) custom-call(bf16[1024,768]{1,0:T(8,128)(2,1)} %x.5, bf16[1024,768]{1,0:T(8,128)(2,1)} %get-tuple-element.63.normed, bf16[1024,768]{1,0:T(8,128)(2,1)} %get-tuple-element.67.dq, bf16[1024,768]{1,0:T(8,128)(2,1)} %get-tuple-element.68.dk, ...), custom_call_target="tpu_custom_call" | custom-call | flops 7247757312 | bytes 25165824 | tf_op jit(solution)/shard_map/project_back/pallas_call | solution.py:691
  435.8 40.4 %reduce-scatter.6.cloned.1.call-done = bf16[96,2432]{1,0:T(8,128)(2,1)} async-done(((bf16[768,2432]{1,0:T(8,128)(2,1)}), bf16[96,2432]{1,0:T(8,128)(2,1)}) %reduce-scatter.6.cloned.1.call-update) | async-done | bytes 466960 | tf_op jit(solution)/shard_map/reduce_scatter | solution.py:700
  476.2 2.0 pad_maximum_fusion.1
  479.1 67.5 %reduce-scatter.14.cloned.1.call-done = bf16[1,2,256,768]{3,2,1,0:T(8,128)(2,1)} async-done(((bf16[8,2,256,768]{3,2,1,0:T(8,128)(2,1)}), bf16[1,2,256,768]{3,2,1,0:T(8,128)(2,1)}) %reduce-scatter.14.cloned.1.call-update) | async-done | bytes 786448 | tf_op jit(solution)/shard_map/reduce_scatter | solution.py:626
  546.6 2.4 bitcast_convert_fusion
  549.0 68.1 %reduce-scatter.12.cloned.1.call-done = bf16[1,2,96,2048]{3,2,1,0:T(8,128)(2,1)} async-done(((bf16[8,2,96,2048]{3,2,1,0:T(8,128)(2,1)}), bf16[1,2,96,2048]{3,2,1,0:T(8,128)(2,1)}) %reduce-scatter.12.cloned.1.call-update) | async-done | bytes 786448 | tf_op jit(solution)/shard_map/reduce_scatter | solution.py:654
  618.3 69.4 %reduce-scatter.10.cloned.1.call-done = bf16[1,2,96,2048]{3,2,1,0:T(8,128)(2,1)} async-done(((bf16[8,2,96,2048]{3,2,1,0:T(8,128)(2,1)}), bf16[1,2,96,2048]{3,2,1,0:T(8,128)(2,1)}) %reduce-scatter.10.cloned.1.call-update) | async-done | bytes 786448 | tf_op jit(solution)/shard_map/reduce_scatter | solution.py:654
  688.8 1.9 maximum_convert_fusion
  690.7 35.3 %all-gather.17.cloned.1.call-done = bf16[384,3200]{1,0:T(8,128)(2,1)} async-done(((bf16[96,3200]{1,0:T(8,128)(2,1)}), bf16[384,3200]{1,0:T(8,128)(2,1)}) %all-gather.17.cloned.1.call-update) | async-done | bytes 2457616 | tf_op jit(solution)/shard_map/all_gather | solution.py:701
  726.0 2.2 convert_reduce_fusion
  (50 shorter events, 14.0 us)
Async XLA Ops:
  7.2 5.8 copy-start.2
  7.2 5.8 copy-start.1
  7.2 51.0 %all-gather.9.cloned.1.call-start = ((), (), s32[]{:S(2)}) async-start(), calls=%async_computation.8 | async-start | bytes 4202496 | tf_op jit(solution)/shard_map/all_gather | solution.py:537
  12.2 69.2 %all-gather.11.cloned.1.call-start = ((), (), s32[]{:S(2)}) async-start(), calls=%async_computation.9 | async-start | bytes 1327104 | tf_op jit(solution)/shard_map/all_gather | solution.py:538
  13.0 187.0 %all-gather.13.cloned.1.call-start = ((), (), s32[]{:S(2)}) async-start(), calls=%async_computation.15 | async-start | bytes 14155776 | tf_op jit(solution)/shard_map/all_gather | solution.py:540
  14.3 0.7 copy-start.5
  14.3 2.4 copy-start.4
  14.3 3.4 copy-start.6
  14.3 250.1 %all-gather.15.cloned.1.call-start = ((), (), s32[]{:S(2)}) async-start(), calls=%async_computation.16 | async-start | bytes 7077888 | tf_op jit(solution)/shard_map/all_gather | solution.py:541
  131.3 79.7 %all-to-all-start = ((bf16[4,2,2,176,768]{4,3,2,1,0:T(8,128)(2,1)}), bf16[4,2,2,176,768]{4,3,2,1,0:T(8,128)(2,1)}, u32[]{:S(2)}, u32[]{:S(2)}) async-start(bf16[4,2,2,176,768]{4,3,2,1,0:T(8,128)(2,1)} %dispatch.1), calls=%async_computation | async-start | bytes 8650752 | tf_op jit(solution)/shard_map/all_to_all | solution.py:592
  284.6 29.8 %all-to-all-start.2 = ((bf16[4,2,176,768]{3,2,1,0:T(8,128)(2,1)}), bf16[4,2,176,768]{3,2,1,0:T(8,128)(2,1)S(1)}, u32[]{:S(2)}, u32[]{:S(2)}) async-start(bf16[4,2,176,768]{3,2,1,0:T(8,128)(2,1)} %get-tuple-element.58), calls=%async_computation.2 | async-start | bytes 4325376 | tf_op jit(solution)/shard_map/all_to_all | solution.py:657
  288.3 147.5 %reduce-scatter.8.cloned.1.call-start = ((), (), s32[]{:S(2)}) async-start(), calls=%async_computation.11 | async-start | bytes 1327104 | tf_op jit(solution)/shard_map/reduce_scatter | solution.py:677
  314.5 30.5 %copy-start = (bf16[4,2,176,768]{3,2,1,0:T(8,128)(2,1)}, bf16[4,2,176,768]{3,2,1,0:T(8,128)(2,1)S(1)}, u32[]{:S(2)}) copy-start(bf16[4,2,176,768]{3,2,1,0:T(8,128)(2,1)S(1)} %all-to-all-done.2.eo1.rg1) | copy-start | bytes 6488068
  371.8 104.4 %reduce-scatter.6.cloned.1.call-start = ((), (), s32[]{:S(2)}) async-start(), calls=%async_computation.10 | async-start | bytes 4202496 | tf_op jit(solution)/shard_map/reduce_scatter | solution.py:700
  433.5 113.1 %reduce-scatter.14.cloned.1.call-start = ((), (), s32[]{:S(2)}) async-start(), calls=%async_computation.14 | async-start | bytes 7077888 | tf_op jit(solution)/shard_map/reduce_scatter | solution.py:626
  434.2 182.9 %reduce-scatter.12.cloned.1.call-start = ((), (), s32[]{:S(2)}) async-start(), calls=%async_computation.13 | async-start | bytes 7077888 | tf_op jit(solution)/shard_map/reduce_scatter | solution.py:654
  435.0 252.6 %reduce-scatter.10.cloned.1.call-start = ((), (), s32[]{:S(2)}) async-start(), calls=%async_computation.12 | async-start | bytes 7077888 | tf_op jit(solution)/shard_map/reduce_scatter | solution.py:654
  435.7 42.5 %copy-start.3 = (f32[1024,12]{1,0:T(8,128)S(1)}, f32[1024,12]{1,0:T(8,128)}, u32[]{:S(2)}) copy-start(f32[1024,12]{1,0:T(8,128)} %get-tuple-element.126) | copy-start | bytes 147460
  435.7 290.2 %all-gather.17.cloned.1.call-start = ((), (), s32[]{:S(2)}) async-start(), calls=%async_computation.17 | async-start | bytes 3072000 | tf_op jit(solution)/shard_map/all_gather | solution.py:701
Sparse Core Ops, SparseCore 0:
  12.3 45.7 all-gather.8
  59.8 21.5 all-gather.10
  83.6 116.3 all-gather.12
  201.5 62.8 all-gather.14
  371.9 29.8 reduce-scatter.7
  433.6 42.5 reduce-scatter.5
  478.5 68.0 reduce-scatter.13
  548.9 68.1 reduce-scatter.11
  619.4 68.1 reduce-scatter.9
  689.3 36.6 all-gather.16

commit v2 on v1

--- a/solution.py
+++ b/solution.py
@@ -16,7 +16,7 @@
 NEG = -1e30
 LANES = 128
 BLOCK = 256
-FTILE = 512
+TILE = 256
 F32 = jnp.float32
 BF16 = jnp.bfloat16
 VMEM_LIMIT = 56 << 20
@@ -207,12 +207,46 @@
     tok_out[...] = packed
 
 
-def dispatch_kernel(normed, grad, tok, routes, dest_row, out, gates):
-    expert = pl.program_id(0)
+def pack_expert_kernel(gate, up, down, out):
+    rows, ff = gate.shape[1:]
+    down_rows, width = down.shape[1:]
+    tiles = ff // TILE
+    for index, ref in enumerate((gate, up)):
+        for f in range(tiles):
+            start = (index * tiles + f) * rows
+            out[start : start + rows, :] = ref[0, :, f * TILE : (f + 1) * TILE]
+    base = 2 * tiles * rows
+    for c in range(width // TILE):
+        out[base + c * down_rows : base + (c + 1) * down_rows, :] = down[
+            0, :, c * TILE : (c + 1) * TILE
+        ]
+
+
+def unpack_expert_kernel(*refs):
+    gate, up, down = refs[-3:]
+    rows, ff = gate.shape[1:]
+    down_rows, width = down.shape[1:]
+    tiles = ff // TILE
+    base = 2 * tiles * rows
+    for l, ref in enumerate(refs[:-3]):
+        for index, out in enumerate((gate, up)):
+            for f in range(tiles):
+                start = (index * tiles + f) * rows
+                out[l, :, f * TILE : (f + 1) * TILE] = ref[start : start + rows, :].astype(F32)
+        for c in range(width // TILE):
+            down[l, :, c * TILE : (c + 1) * TILE] = ref[
+                base + c * down_rows : base + (c + 1) * down_rows, :
+            ].astype(F32)
+
+
+def dispatch_kernel(local_experts, l, me, normed, grad, tok, routes, dest_row, *rest):
+    outs, gates = rest[:-1], rest[-1]
+    step = pl.program_id(0)
     tokens = normed.shape[0]
-    stride = out.shape[3]
-
-    @pl.when(expert == 0)
+    stride = outs[0].shape[1]
+    expert = (me[0] ^ step) * local_experts + l
+
+    @pl.when(step == 0)
     def _():
         lane = iota((tokens, LANES), 1)
         kind = lane % HEAD_DIM
@@ -224,88 +258,117 @@
     slot = expert * stride + iota((stride, tokens), 0)
     hit = (dest_row[0:1, :] == slot) | (dest_row[1:2, :] == slot)
     take = jnp.where(hit, 1.0, 0.0).astype(BF16)
-    out[0, 0, 0] = mm(take, normed[...]).astype(BF16)
+    row = mm(take, normed[...]).astype(BF16)
     slot_gates = mm(take, gates[...])
     mine = iota((stride, LANES), 1) % HEAD_DIM == expert
     slot_gate = jnp.sum(jnp.where(mine, slot_gates, 0.0), axis=1, keepdims=True)
-    out[0, 1, 0] = (mm(take, grad[...]) * slot_gate).astype(BF16)
-
-
-def expert_up_kernel(rows, grads, gate, up, hidden, slope, silu_out, down_grad):
-    n_src, stride, width = rows.shape[0], rows.shape[3], rows.shape[4]
-    r = rows[...].reshape(n_src * stride, width)
-    s = grads[...].reshape(n_src * stride, width)
-    ftile = gate.shape[-1]
-    gate_pre = mm(r, gate[...].reshape(width, ftile))
-    up_pre = mm(r, up[...].reshape(width, ftile))
+    slot_g = (mm(take, grad[...]) * slot_gate).astype(BF16)
+    for k, out in enumerate(outs):
+
+        @pl.when(step == k)
+        def _():
+            out[0] = row
+            out[1] = slot_g
+
+
+def expert_kernel(owners, merged, *refs):
+    sent = refs[:owners]
+    weights = refs[owners : owners + 6]
+    backs = refs[owners + 6 : 2 * owners + 6]
+    grads = refs[2 * owners + 6 : -4]
+    r_all, s_all, out_acc, row_acc = refs[-4:]
+    step = pl.program_id(0)
+    steps = pl.num_programs(0)
+    stride, width = sent[0].shape[1:]
+    chunks, chunk_rows = weights[0].shape[:2]
+
+    @pl.when(step == 0)
+    def _():
+        for k, ref in enumerate(sent):
+            r_all[k * stride : (k + 1) * stride, :] = ref[0]
+            s_all[k * stride : (k + 1) * stride, :] = ref[1]
+        out_acc[...] = jnp.zeros_like(out_acc)
+        row_acc[...] = jnp.zeros_like(row_acc)
+
+    def tile_pair(a, b):
+        return jnp.concatenate([t[...].reshape(width, TILE) for t in (a, b)], axis=1)
+
+    def down_tile(ref):
+        parts = [ref[0, c * TILE : (c + 1) * TILE, :] for c in range(width // TILE)]
+        return jnp.concatenate(parts, axis=1)
+
+    r = r_all[...]
+    s = s_all[...]
+    gate = tile_pair(weights[0], weights[1])
+    up = tile_pair(weights[2], weights[3])
+    d = jnp.concatenate([down_tile(weights[4]), down_tile(weights[5])], axis=0)
+    gate_pre = mm(r, gate)
+    up_pre = mm(r, up)
     sig = jax.nn.sigmoid(gate_pre)
     silu = gate_pre * sig
     hid = (silu * up_pre).astype(BF16)
-    hidden[0] = hid
-    silu_out[0] = silu.astype(BF16)
-    slope[0] = (up_pre * (sig + silu * (1.0 - sig))).astype(BF16)
-    down_grad[...] = mm_tn(hid, s).astype(BF16).reshape(down_grad.shape)
-
-
-def expert_down_kernel(
-    rows, grads, gate, up, down, hidden, slope, silu, back, grad_out, out_acc, row_acc
-):
-    step = pl.program_id(0)
-    n_src, stride, width = rows.shape[0], rows.shape[3], rows.shape[4]
-    count = n_src * stride
-    ftile = gate.shape[-1]
-
-    @pl.when(step == 0)
+    hidden_g = mm_nt(s, d)
+    out_acc[...] += mm(hid, d)
+    gate_g = (hidden_g * (up_pre * (sig + silu * (1.0 - sig)))).astype(BF16)
+    up_g = (hidden_g * silu).astype(BF16)
+    row_acc[...] += mm_nt(gate_g, gate) + mm_nt(up_g, up)
+    down_grad = mm_tn(hid, s).astype(BF16)
+    gate_grad = mm_tn(r, gate_g).astype(BF16)
+    up_grad = mm_tn(r, up_g).astype(BF16)
+    base = 4 * steps * chunk_rows if merged else 0
+    for i in range(2):
+        tile = 2 * step + i
+        for index, value in enumerate((gate_grad, up_grad)):
+            start = pl.multiple_of((index * 2 * steps + tile) * chunk_rows, 16)
+            grads[0][:, pl.ds(start, chunk_rows), :] = value[:, i * TILE : (i + 1) * TILE].reshape(
+                chunks, chunk_rows, TILE
+            )
+        for c in range(width // TILE):
+            grads[-1][tile, base + c * TILE : base + (c + 1) * TILE, :] = down_grad[
+                i * TILE : (i + 1) * TILE, c * TILE : (c + 1) * TILE
+            ]
+
+    @pl.when(step == steps - 1)
     def _():
-        out_acc[...] = jnp.zeros_like(out_acc)
-        row_acc[...] = jnp.zeros_like(row_acc)
-
-    r = rows[...].reshape(count, width)
-    s = grads[...].reshape(count, width)
-    d = down[...].reshape(ftile, width)
-    hidden_g = mm_nt(s, d)
-    out_acc[...] += mm(hidden[0], d)
-    gate_g = (hidden_g * slope[0].astype(F32)).astype(BF16)
-    up_g = (hidden_g * silu[0].astype(F32)).astype(BF16)
-    row_acc[...] += mm_nt(gate_g, gate[...].reshape(width, ftile)) + mm_nt(
-        up_g, up[...].reshape(width, ftile)
-    )
-    shape = (grad_out.shape[0], grad_out.shape[2], ftile)
-    grad_out[:, 0] = mm_tn(r, gate_g).astype(BF16).reshape(shape)
-    grad_out[:, 1] = mm_tn(r, up_g).astype(BF16).reshape(shape)
-
-    @pl.when(step == pl.num_programs(0) - 1)
-    def _():
-        back[:, 0] = out_acc[...].astype(BF16).reshape(n_src, stride, width)
-        back[:, 1] = row_acc[...].astype(BF16).reshape(n_src, stride, width)
-
-
-def combine_kernel(
-    experts, eo0, rg0, eo1, rg1, residual, normed, grad, tok, routes, dest, mix, wo, small_t,
-    mixed_out, prev_out, resg_out, headg_out, delta_out, wo_out, small_out, wo_acc, small_acc, second_acc,
-):
+        for k, ref in enumerate(backs):
+            ref[0] = out_acc[k * stride : (k + 1) * stride, :].astype(BF16)
+            ref[1] = row_acc[k * stride : (k + 1) * stride, :].astype(BF16)
+
+
+def combine_kernel(experts, owners, local_experts, me, *refs):
+    backs = refs[: owners * local_experts]
+    (
+        residual, normed, grad, tok, routes, dest, mix, wo, small_t,
+        mixed_out, prev_out, resg_out, headg_out, delta_out, wo_out, small_out,
+        wo_acc, small_acc, second_acc, eo_all, rg_all,
+    ) = refs[owners * local_experts :]
     step = pl.program_id(0)
     block, width = residual.shape
-    n_src, stride = eo0.shape[0], eo0.shape[2]
-    local = n_src * stride
+    stride = backs[0].shape[1]
+    local = owners * stride
 
     @pl.when(step == 0)
     def _():
         wo_acc[...] = jnp.zeros_like(wo_acc)
         small_acc[...] = jnp.zeros_like(small_acc)
         second_acc[...] = jnp.zeros_like(second_acc)
-
-    slot = iota((block, local), 1)
-    owner_slot = slot // stride * (2 * stride) + slot % stride
+        for l in range(local_experts):
+            for k in range(owners):
+                place = slice(k * stride, (k + 1) * stride)
+                eo_all[l, place, :] = backs[l * owners + k][0]
+                rg_all[l, place, :] = backs[l * owners + k][1]
+
+    slot = iota((1, local), 1)
+    owner_slot = ((slot // stride) ^ me[0]) * (local_experts * stride) + slot % stride
 
     ep = [None, None]
     back = None
-    for l, (eo_ref, rg_ref) in enumerate(((eo0, rg0), (eo1, rg1))):
+    for l in range(local_experts):
         ident = owner_slot + l * stride
         t0 = jnp.where(dest[:, 0:1] == ident, 1.0, 0.0)
         t1 = jnp.where(dest[:, 1:2] == ident, 1.0, 0.0)
-        eo = eo_ref[...].reshape(local, width)
-        rg = rg_ref[...].reshape(local, width)
+        eo = eo_all[l]
+        rg = rg_all[l]
         e0 = mm(t0.astype(BF16), eo)
         e1 = mm(t1.astype(BF16), eo)
         b = mm((t0 + t1).astype(BF16), rg)
@@ -513,10 +576,9 @@
     kinds = experts + ZC
     capacity = count * TOP // kinds // 8 * 8
     stride = -(-capacity // 16) * 16
-    ftile = FTILE
-    fsteps = ff // ftile
+    tiles = ff // TILE
     down_rows = down_weight.shape[1]
-    per_tile = ftile // down_rows
+    me = lax.axis_index("expert").astype(jnp.int32).reshape(1)
     packed_width = 3 * width + LANES
     cosine, sine = (jnp.asarray(t) for t in rotary_tables())
     struct = jax.ShapeDtypeStruct
@@ -536,9 +598,36 @@
     )
     qkv_full = lax.all_gather(packed, "shard", axis=0, tiled=True)
     output_full = lax.all_gather(output_weight, "shard", axis=0, tiled=True)
-    gate_up = jnp.stack([gate_weight, up_weight], axis=1)
-    gate_up_full = lax.all_gather(gate_up, "shard", axis=0, tiled=False)
-    down_full = lax.all_gather(down_weight, "shard", axis=0, tiled=False)
+    aligned = shard_rows % 16 == 0 and down_rows == TILE
+    expert_rows = 2 * tiles * shard_rows + width // TILE * down_rows
+
+    def gather_expert(l):
+        if aligned:
+            one = call(
+                pack_expert_kernel, "pack_expert", (1,),
+                [pl.BlockSpec((1,) + w.shape[1:], lambda i: (l, 0, 0))
+                 for w in (gate_weight, up_weight, down_weight)],
+                whole((expert_rows, TILE)), struct((expert_rows, TILE), BF16), traffic=5 << 20,
+            )(gate_weight, up_weight, down_weight)
+        else:
+            one = jnp.concatenate([
+                w[l].reshape(w.shape[1], -1, TILE).transpose(1, 0, 2).reshape(-1, TILE)
+                for w in (gate_weight, up_weight, down_weight)
+            ])
+        full = lax.all_gather(one, "shard", axis=0, tiled=True)
+        full = full.reshape(shards, expert_rows, TILE)
+        if aligned:
+            return full, full
+        split = 2 * tiles * shard_rows
+        gate_up = full[:, :split].reshape(shards, 2 * tiles, shard_rows, TILE)
+        down = full[:, split:].reshape(shards, width // TILE, down_rows, TILE)
+        down = down.transpose(1, 0, 2, 3).reshape(width // TILE, tiles, TILE, TILE)
+        return (
+            gate_up.transpose(1, 0, 2, 3).reshape(1, -1, TILE),
+            down.transpose(1, 0, 2, 3).reshape(tiles, width, TILE),
+        )
+
+    expert_full = [gather_expert(l) for l in range(local_experts)]
 
     dest_col, dest_row = call(
         functools.partial(slots_kernel, experts, capacity, stride), "slots", (1,),
@@ -577,104 +666,89 @@
     )(prefix, queries, keys, values, tokens, output_full, qkv_full, small_t,
       previous_logits, routes)
 
-    send = call(
-        dispatch_kernel, "dispatch", (experts,),
-        [whole((count, width)), whole((count, width)), whole((count, LANES)),
-         whole((count, TOP)), whole((8, count))],
-        pl.BlockSpec(
-            (1, 2, 1, stride, width),
-            lambda e: (e // local_experts, 0, e % local_experts, 0, 0),
-        ),
-        struct((owners, 2, local_experts, stride, width), BF16),
-        scratch=[pltpu.VMEM((count, LANES), BF16)],
-        flops=4 * experts * stride * count * width, traffic=8 << 20,
-    )(normed_two, cotangent, tok, routes, dest_row)
-    received = lax.all_to_all(send, "expert", split_axis=0, concat_axis=0, tiled=True)
-
-    aligned = shard_rows % 16 == 0
-    if aligned:
-        chunks, chunk_rows = shards, shard_rows
-        gate_up_kernel = gate_up_full
-    else:
-        chunks, chunk_rows = 1, width
-        gate_up_kernel = gate_up_full.transpose(1, 2, 0, 3, 4).reshape(
-            1, local_experts, 2, width, ff
+    def exchange(parts):
+        return [parts[0]] + [
+            lax.ppermute(part, "expert", [(i, i ^ k) for i in range(owners)])
+            for k, part in list(enumerate(parts))[1:]
+        ]
+
+    pair = whole((2, stride, width))
+    pair_shape = struct((2, stride, width), BF16)
+
+    def dispatch(l):
+        parts = call(
+            functools.partial(dispatch_kernel, local_experts, l), "dispatch", (owners,),
+            [whole((count, width)), whole((count, width)), whole((count, LANES)),
+             whole((count, TOP)), whole((8, count))],
+            [pair] * owners, [pair_shape] * owners,
+            scratch=[pltpu.VMEM((count, LANES), BF16)],
+            flops=4 * owners * stride * count * width, traffic=6 << 20, prefetch=1,
+        )(me, normed_two, cotangent, tok, routes, dest_row)
+        return exchange(parts)
+
+    received = [dispatch(l) for l in range(local_experts)]
+
+    chunks, chunk_rows = (shards, shard_rows) if aligned else (1, width)
+    local = owners * stride
+
+    def run_expert(l):
+        gate_up, down = expert_full[l]
+        weights = [
+            pl.BlockSpec((chunks, chunk_rows, TILE), lambda f, j=j: (0, j // 2 * tiles + 2 * f + j % 2, 0))
+            for j in range(4)
+        ] + [
+            pl.BlockSpec((1, width, TILE), lambda f, j=j: (2 * f + j, 2 if aligned else 0, 0))
+            for j in range(2)
+        ]
+        if aligned:
+            grad_shapes = [(shards, expert_rows, TILE)]
+        else:
+            grad_shapes = [(1, 2 * tiles * width, TILE), (tiles, width, TILE)]
+        outs = call(
+            functools.partial(expert_kernel, owners, aligned), "expert", (tiles // 2,),
+            [pair] * owners + weights,
+            [pair] * owners + [whole(g) for g in grad_shapes],
+            [pair_shape] * owners + [struct(g, BF16) for g in grad_shapes],
+            scratch=[pltpu.VMEM((local, width), BF16)] * 2 + [pltpu.VMEM((local, width), F32)] * 2,
+            flops=16 * local * width * ff, traffic=24 << 20, trans=local * ff,
+        )(*received[l], gate_up, gate_up, gate_up, gate_up, down, down)
+        grads = outs[owners:]
+        if aligned:
+            grad = grads[0]
+        else:
+            gate_up_g = grads[0].reshape(2 * tiles, shards, shard_rows, TILE).transpose(1, 0, 2, 3)
+            down_g = grads[1].reshape(tiles, width // TILE, TILE, TILE).transpose(1, 0, 2, 3)
+            down_g = down_g.reshape(width // TILE, shards, down_rows, TILE).transpose(1, 0, 2, 3)
+            grad = jnp.concatenate(
+                [gate_up_g.reshape(shards, -1, TILE), down_g.reshape(shards, -1, TILE)], axis=1
+            )
+        total = lax.psum_scatter(
+            grad.reshape(shards * expert_rows, TILE), "shard", scatter_dimension=0, tiled=True
         )
-    local = owners * stride
-
-    def part(kind, pick):
-        return pl.BlockSpec(
-            (owners, 1, 1, stride, width), lambda *idx: (0, kind, pick(*idx), 0, 0)
-        )
-
-    expert_flops = 2 * local * width * ff
-    hidden_block = pl.BlockSpec((1, local, ftile), lambda l, f: (l, 0, f))
-    hidden_shape = struct((local_experts, local, ff), BF16)
-    hidden, slope, silu, down_grad = call(
-        expert_up_kernel, "expert_up", (local_experts, fsteps),
-        [part(0, lambda l, f: l), part(1, lambda l, f: l)]
-        + [
-            pl.BlockSpec((chunks, 1, 1, chunk_rows, ftile), lambda l, f, j=j: (0, l, j, 0, f))
-            for j in range(2)
-        ],
-        [hidden_block] * 3
-        + [pl.BlockSpec((per_tile, 1, down_rows, width), lambda l, f: (f, l, 0, 0))],
-        [hidden_shape] * 3 + [struct((shards, local_experts, down_rows, width), BF16)],
-        flops=3 * local_experts * expert_flops, traffic=35 << 20,
-        trans=local_experts * local * ff,
-    )(received, received, gate_up_kernel, gate_up_kernel)
-    down_sum = lax.psum_scatter(down_grad, "shard", scatter_dimension=0, tiled=False)
+        return exchange(outs[:owners]), total
 
     returned = []
-    gate_up_sums = []
+    expert_sums = []
     for l in range(local_experts):
-        pick = lambda f, l=l: l
-        hid = pl.BlockSpec((1, local, ftile), lambda f, l=l: (l, 0, f))
-        back, gu_grad = call(
-            expert_down_kernel, "expert_down", (fsteps,),
-            [part(0, pick), part(1, pick)]
-            + [
-                pl.BlockSpec(
-                    (chunks, 1, 1, chunk_rows, ftile), lambda f, j=j, l=l: (0, l, j, 0, f)
-                )
-                for j in range(2)
-            ]
-            + [pl.BlockSpec((per_tile, 1, down_rows, width), lambda f, l=l: (f, l, 0, 0))]
-            + [hid] * 3,
-            [whole((owners, 2, stride, width)),
-             pl.BlockSpec((chunks, 2, chunk_rows, ftile), lambda f: (0, 0, 0, f))],
-            [struct((owners, 2, stride, width), BF16),
-             struct((chunks, 2, chunk_rows, ff), BF16)],
-            scratch=[pltpu.VMEM((local, width), F32)] * 2,
-            flops=6 * expert_flops, traffic=30 << 20,
-        )(received, received, gate_up_kernel, gate_up_kernel, down_full, hidden, slope, silu)
-        if not aligned:
-            gu_grad = gu_grad.reshape(2, shards, shard_rows, ff).transpose(1, 0, 2, 3)
-        gate_up_sums.append(
-            lax.psum_scatter(gu_grad, "shard", scatter_dimension=0, tiled=False)
-        )
-        returned.append(
-            lax.all_to_all(back, "expert", split_axis=0, concat_axis=0, tiled=True)
-        )
-
-    def kind_block(kind):
-        return pl.BlockSpec((owners, 1, stride, width), lambda i: (0, kind, 0, 0))
+        back, total = run_expert(l)
+        returned += back
+        expert_sums.append(total)
 
     mixed, previous_grad, residual_grad, heads_grad, delta, output_grad, small_grad = call(
-        functools.partial(combine_kernel, experts), "combine", (steps,),
-        [kind_block(0), kind_block(1)] * 2
+        functools.partial(combine_kernel, experts, owners, local_experts), "combine", (steps,),
+        [pair] * len(returned)
         + [wide, wide, wide, table, rows_of(BLOCK, TOP), table, wide, whole((width, width)),
            whole((LANES, width))],
-        [wide, rows_of(BLOCK, kinds), wide, wide, pl.BlockSpec((16, BLOCK), lambda i: (0, i)),
+        [wide, rows_of(BLOCK, kinds), wide, wide, pl.BlockSpec((16, BLOCK), lambda i, *rest: (0, i)),
          whole((width, width)), whole((width, LANES))],
         [act, struct((count, kinds), F32), struct((count, width), F32), act,
          struct((16, count), F32), struct((width, width), BF16), struct((width, LANES), F32)],
         scratch=[pltpu.VMEM((width, width), F32), pltpu.VMEM((width, LANES), F32),
-                 pltpu.VMEM((8, width), F32)],
-        flops=6 * count * 2 * local * width + 4 * count * width * width, traffic=24 << 20,
-    )(returned[0], returned[0], returned[1], returned[1], residual, normed_two, cotangent, tok,
+                 pltpu.VMEM((8, width), F32)]
+        + [pltpu.VMEM((local_experts, local, width), BF16)] * 2,
+        flops=6 * count * 2 * local * width + 4 * count * width * width, traffic=24 << 20, prefetch=1,
+    )(me, *returned, residual, normed_two, cotangent, tok,
       routes, dest_col, attn_mix, output_full, small_t)
-    output_sum = lax.psum_scatter(output_grad, "shard", scatter_dimension=0, tiled=True)
 
     pair_block = pl.BlockSpec((count, LANES), lambda i, *rest: (0, i))
     dq, dk, dv = call(
@@ -697,14 +771,37 @@
         flops=12 * count * width * width, traffic=24 << 20,
     )(tokens, normed_one, dq, dk, dv, residual_grad, qkv_full, qkv_full, qkv_full, small_t,
       small_grad)
+    dense_grad = jnp.concatenate([dense_grad, output_grad], axis=1)
+    dense_grad, expert_sums = lax.optimization_barrier((dense_grad, expert_sums))
     dense_sum = lax.psum_scatter(dense_grad, "shard", scatter_dimension=0, tiled=True)
-    dense_all = lax.all_gather(
-        jnp.concatenate([dense_sum, output_sum], axis=1), "expert", axis=0, tiled=False
-    )
-    dense = jnp.sum(dense_all.astype(F32), axis=0)
+    half = shard_rows // 2
+    parts = [dense_sum[:half], dense_sum[half:]]
+    moves = [[(i, i ^ k) for i in range(owners)] for k in (1, 2)]
+    for turn in range(2):
+        other = [lax.ppermute(parts[j], "expert", moves[(turn + j) % 2]) for j in range(2)]
+        parts = [(a.astype(F32) + b.astype(F32)).astype(F32 if turn else BF16)
+                 for a, b in zip(parts, other)]
+    dense = jnp.concatenate(parts, axis=0)
     small = dense[:, 3 * width : 3 * width + LANES]
-    gate_sum = jnp.stack([s[0] for s in gate_up_sums]).astype(F32)
-    up_sum = jnp.stack([s[1] for s in gate_up_sums]).astype(F32)
+    if aligned:
+        out_shapes = [w.shape for w in (gate_weight, up_weight, down_weight)]
+        gate_sum, up_sum, down_sum = call(
+            unpack_expert_kernel, "unpack", (1,),
+            [whole((expert_rows, TILE))] * local_experts,
+            [whole(o) for o in out_shapes], [struct(o, F32) for o in out_shapes],
+            traffic=8 << 20,
+        )(*expert_sums)
+    else:
+        split = 2 * tiles * shard_rows
+        total = jnp.stack(expert_sums).astype(F32)
+        gate_sum, up_sum = (
+            part.reshape(local_experts, tiles, shard_rows, TILE).transpose(0, 2, 1, 3).reshape(
+                local_experts, shard_rows, ff
+            )
+            for part in (total[:, : split // 2], total[:, split // 2 : split])
+        )
+        down_sum = total[:, split:].reshape(local_experts, width // TILE, down_rows, TILE)
+        down_sum = down_sum.transpose(0, 2, 1, 3).reshape(local_experts, down_rows, width)
     return (
         mixed,
         tokens_grad,
@@ -720,7 +817,7 @@
         small[:, 17],
         gate_sum,
         up_sum,
-        down_sum.astype(F32),
+        down_sum,
     )
 
 

time: 740 us -> 557 us (0.75)
  waiting for transfers between devices: 433 us -> 270 us
  blocking collectives: 30.5 us -> 0 us
  Pallas kernels: 218 us -> 232 us
  local copies, waits for them, and re-layouts: 24.1 us -> 11.7 us
  starting transfers between devices: 9.06 us -> 21.1 us
    reduce_scatter x4 -> x2, waiting for transfers between devices: 205 us -> 23.1 us  [run_expert(): lax.psum_scatter(grad.reshape(shards * expert_rows, TILE), 'shard', scatt...]
    ppermute x0 -> x16, waiting for transfers between devices: none -> 101 us  [the longest x12 89.3 us: exchange(): lax.ppermute(part, 'expert', [(i, i ^ k) for i in range(owners)])]
    all_gather x3 -> x2, waiting for transfers between devices: 131 us -> 42.8 us  [gather_expert(): full = lax.all_gather(one, 'shard', axis=0, tiled=True)]
    all_to_all x1 -> x0, blocking collectives: 30.5 us -> none  [body(): lax.all_to_all(back, 'expert', split_axis=0, concat_axis=0, tiled=True)]
    ppermute x0 -> x16, starting transfers between devices: none -> 20.9 us  [the longest x12 15.8 us: exchange(): lax.ppermute(part, 'expert', [(i, i ^ k) for i in range(owners)])]
    reduce_scatter x1, waiting for transfers between devices: 40.4 us -> 57.5 us  [body(): lax.psum_scatter(dense_grad, 'shard', scatter_dimension=0, tiled=True)]
    pallas_call x5 -> x8, Pallas kernels: 99.8 us -> 113 us  [the longest x2 60.9 us: run_expert(): call(functools.partial(expert_kernel, owners, aligned), 'expert', (tiles...]
    all_gather x1 -> x0, local copies, waits for them, and re-layouts: 11 us -> none  [body(): gate_up_full = lax.all_gather(gate_up, 'shard', axis=0, tiled=False)]
  transfers between devices with their start and end apart: 12 -> 23, of which waited for: 10 -> 18; matrix products, arithmetic and copies ran while one was open for 3% -> 2% of each run, Pallas kernels for 23% -> 41%
where the time goes in v2:
time: 557 us; the launch traced here: 556 us
  waiting for transfers between devices  270 us (48%)
  Pallas kernels  232 us (42%)
  starting transfers between devices  21.1 us (4%)
  between operations  15 us (3%)
  local copies, waits for them, and re-layouts  11.7 us (2%)
  other arithmetic  6.81 us (1%)
    ppermute x12, waiting for transfers between devices, exchange(): lax.ppermute(part, 'expert', [(i, i ^ k) for i in range(owners)])  89.3 us
    pallas_call x2, Pallas kernels, run_expert(): call(functools.partial(expert_kernel, owners, aligned), 'expert', (tiles...  60.9 us
    reduce_scatter x1, waiting for transfers between devices, body(): lax.psum_scatter(dense_grad, 'shard', scatter_dimension=0, tiled=True)  57.5 us
    pallas_call x1, Pallas kernels, body(): call(attend_back_kernel, 'attend_back', (width // LANES,), [pair_block] *...  46.4 us
    all_gather x2, waiting for transfers between devices, gather_expert(): full = lax.all_gather(one, 'shard', axis=0, tiled=True)  42.8 us
    pallas_call x1, Pallas kernels, body(): call(attend_kernel, 'attend', (steps,), [wide, whole((count, width)), who...  39 us
    all_gather x1, waiting for transfers between devices, body(): qkv_full = lax.all_gather(packed, 'shard', axis=0, tiled=True)  29.7 us
    pallas_call x1, Pallas kernels, body(): call(functools.partial(combine_kernel, experts, owners, local_experts), '...  27.7 us
  transfers between devices with their start and end apart: 23, of which 18 were waited for; matrix products, arithmetic and copies ran while one was open for 2% of the time, Pallas kernels for 41%

profile of v2, /device:TPU:0, one launch (start us, length us, event | category | flops | bytes accessed | tf_op | source)
XLA Modules:
  0.0 556.2 jit_solution(7774307037321893518)
XLA Ops:
  10.0 2.0 pack.1
  12.9 2.3 pack_expert.3
  15.3 2.3 pack_expert.2
  21.4 6.9 %slots.1 = (s32[1024,128]{1,0:T(8,128)}, s32[8,1024]{1,0:T(8,128)}) custom-call(s32[1024,2]{1,0:T(8,128)} %copy.50.routes.refs_12_, s32[1,1024]{1,0:T(1,128)} %order_row.1, s32[1024,1]{1,0:T(8,128)} %copy.52.order_col), custom_call_target="tpu_custom_call" | custom-call | flops 805306368 | bytes 1048576 | tf_op jit(solution)/shard_map/slots/pallas_call | solution.py:632
  28.3 29.7 %all-gather.5.cloned.1.call-done.wq.wk.wv.small = bf16[768,2432]{1,0:T(8,128)(2,1)} async-done(((bf16[96,2432]{1,0:T(8,128)(2,1)}), bf16[768,2432]{1,0:T(8,128)(2,1)}) %all-gather.5.cloned.1.call-update) | async-done | bytes 3735568 | tf_op jit(solution)/shard_map/all_gather | solution.py:599
  58.0 8.7 %project.1 = (bf16[1024,768]{1,0:T(8,128)(2,1)}, bf16[1024,768]{1,0:T(8,128)(2,1)}, bf16[1024,768]{1,0:T(8,128)(2,1)}, bf16[1024,768]{1,0:T(8,128)(2,1)}, f32[128,768]{1,0:T(8,128)}) custom-call(bf16[1024,768]{1,0:T(8,128)(2,1)} %x.5, bf16[768,2432]{1,0:T(8,128)(2,1)} %all-gather.5.cloned.1.call-done.wq.wk.wv.small, ...), custom_call_target="tpu_custom_call" | custom-call | flops 3623878656 | bytes 12582912 | tf_op jit(solution)/shard_map/project/pallas_call | solution.py:648
  66.7 14.6 %all-gather.7.cloned.1.call-done.wo.refs_15_ = bf16[768,768]{1,0:T(8,128)(2,1)} async-done(((bf16[96,768]{1,0:T(8,128)(2,1)}), bf16[768,768]{1,0:T(8,128)(2,1)}) %all-gather.7.cloned.1.call-update) | async-done | bytes 1179664 | tf_op jit(solution)/shard_map/all_gather | solution.py:600
  81.3 39.0 %attend.1 = (bf16[1024,768]{1,0:T(8,128)(2,1)}, f32[16,1024]{1,0:T(8,128)}, f32[1024,768]{1,0:T(8,128)}, bf16[1024,768]{1,0:T(8,128)(2,1)}, f32[1024,128]{1,0:T(8,128)}) custom-call(s32[1]{0:T(128)S(6)} %copy.60.prefix, bf16[1024,768]{1,0:T(8,128)(2,1)} %get-tuple-element.63.q, bf16[1024,768]{1,0:T(8,128)(2,1)} %get-tuple-element.64.k, ...), custom_call_target="tpu_custom_call" | custom-call | flops 32212254720 | bytes 16777216 | tf_op jit(solution)/shard_map/attend/pallas_call | solution.py:656
  120.3 7.9 %dispatch.3 = (bf16[2,176,768]{2,1,0:T(8,128)(2,1)}, bf16[2,176,768]{2,1,0:T(8,128)(2,1)}, bf16[2,176,768]{2,1,0:T(8,128)(2,1)}, bf16[2,176,768]{2,1,0:T(8,128)(2,1)}) custom-call(s32[1]{0:T(128)} %bitcast.me, bf16[1024,768]{1,0:T(8,128)(2,1)} %get-tuple-element.67.normed.refs_9_, bf16[1024,768]{1,0:T(8,128)(2,1)} %refs_10_.1, ...), custom_call_target="tpu_custom_call" | custom-call | flops 2214592512 | bytes 6291456 | tf_op jit(solution)/shard_map/dispatch/pallas_call | solution.py:679
  131.8 11.9 %collective-permute-done.6.refs_1_ = bf16[2,176,768]{2,1,0:T(8,128)(2,1)S(1)} collective-permute-done((bf16[2,176,768]{2,1,0:T(8,128)(2,1)}, bf16[2,176,768]{2,1,0:T(8,128)(2,1)S(1)}, u32[]{:S(2)}, u32[]{:S(2)}) %collective-permute-start.6) | collective-permute-done | bytes 540704 | tf_op jit(solution)/shard_map/ppermute | solution.py:671
  143.6 12.0 %collective-permute-done.7.refs_2_ = bf16[2,176,768]{2,1,0:T(8,128)(2,1)S(1)} collective-permute-done((bf16[2,176,768]{2,1,0:T(8,128)(2,1)}, bf16[2,176,768]{2,1,0:T(8,128)(2,1)S(1)}, u32[]{:S(2)}, u32[]{:S(2)}) %collective-permute-start.7) | collective-permute-done | bytes 540704 | tf_op jit(solution)/shard_map/ppermute | solution.py:671
  155.6 17.7 %all-gather.11.cloned.1.call-done = bf16[18432,256]{1,0:T(8,128)(2,1)} async-done(((bf16[2304,256]{1,0:T(8,128)(2,1)}), bf16[18432,256]{1,0:T(8,128)(2,1)}) %all-gather.11.cloned.1.call-update) | async-done | bytes 9437200 | tf_op jit(solution)/shard_map/all_gather | solution.py:617
  173.3 30.4 %expert.3 = (bf16[2,176,768]{2,1,0:T(8,128)(2,1)}, bf16[2,176,768]{2,1,0:T(8,128)(2,1)}, bf16[2,176,768]{2,1,0:T(8,128)(2,1)}, bf16[2,176,768]{2,1,0:T(8,128)(2,1)}, bf16[8,2304,256]{2,1,0:T(8,128)(2,1)}) custom-call(bf16[2,176,768]{2,1,0:T(8,128)(2,1)} %get-tuple-element.78.refs_0_, bf16[2,176,768]{2,1,0:T(8,128)(2,1)} %copy-done.18, ...), custom_call_target="tpu_custom_call" | custom-call | flops 17716740096 | bytes 25165824 | tf_op jit(solution)/shard_map/expert/pallas_call | solution.py:707
  203.9 8.1 %dispatch.2 = (bf16[2,176,768]{2,1,0:T(8,128)(2,1)}, bf16[2,176,768]{2,1,0:T(8,128)(2,1)}, bf16[2,176,768]{2,1,0:T(8,128)(2,1)}, bf16[2,176,768]{2,1,0:T(8,128)(2,1)}) custom-call(s32[1]{0:T(128)} %bitcast.me, bf16[1024,768]{1,0:T(8,128)(2,1)} %get-tuple-element.67.normed.refs_9_, bf16[1024,768]{1,0:T(8,128)(2,1)} %refs_10_.1, ...), custom_call_target="tpu_custom_call" | custom-call | flops 2214592512 | bytes 6291456 | tf_op jit(solution)/shard_map/dispatch/pallas_call | solution.py:679
  215.5 11.9 %collective-permute-done.refs_1_ = bf16[2,176,768]{2,1,0:T(8,128)(2,1)S(1)} collective-permute-done((bf16[2,176,768]{2,1,0:T(8,128)(2,1)}, bf16[2,176,768]{2,1,0:T(8,128)(2,1)S(1)}, u32[]{:S(2)}, u32[]{:S(2)}) %collective-permute-start) | collective-permute-done | bytes 540704 | tf_op jit(solution)/shard_map/ppermute | solution.py:671
  227.4 12.0 %collective-permute-done.1.refs_2_ = bf16[2,176,768]{2,1,0:T(8,128)(2,1)S(1)} collective-permute-done((bf16[2,176,768]{2,1,0:T(8,128)(2,1)}, bf16[2,176,768]{2,1,0:T(8,128)(2,1)S(1)}, u32[]{:S(2)}, u32[]{:S(2)}) %collective-permute-start.1) | collective-permute-done | bytes 540704 | tf_op jit(solution)/shard_map/ppermute | solution.py:671
  239.4 25.1 %all-gather.9.cloned.1.call-done = bf16[18432,256]{1,0:T(8,128)(2,1)} async-done(((bf16[2304,256]{1,0:T(8,128)(2,1)}), bf16[18432,256]{1,0:T(8,128)(2,1)}) %all-gather.9.cloned.1.call-update) | async-done | bytes 9437200 | tf_op jit(solution)/shard_map/all_gather | solution.py:617
  264.6 30.5 %expert.2 = (bf16[2,176,768]{2,1,0:T(8,128)(2,1)}, bf16[2,176,768]{2,1,0:T(8,128)(2,1)}, bf16[2,176,768]{2,1,0:T(8,128)(2,1)}, bf16[2,176,768]{2,1,0:T(8,128)(2,1)}, bf16[8,2304,256]{2,1,0:T(8,128)(2,1)}) custom-call(bf16[2,176,768]{2,1,0:T(8,128)(2,1)} %get-tuple-element.70.refs_0_, bf16[2,176,768]{2,1,0:T(8,128)(2,1)} %copy-done.19, ...), custom_call_target="tpu_custom_call" | custom-call | flops 17716740096 | bytes 25165824 | tf_op jit(solution)/shard_map/expert/pallas_call | solution.py:707
  302.5 8.7 %collective-permute-done.9.refs_5_ = bf16[2,176,768]{2,1,0:T(8,128)(2,1)S(1)} collective-permute-done((bf16[2,176,768]{2,1,0:T(8,128)(2,1)S(1)}, bf16[2,176,768]{2,1,0:T(8,128)(2,1)S(1)}, u32[]{:S(2)}, u32[]{:S(2)}) %collective-permute-start.9) | collective-permute-done | bytes 540704 | tf_op jit(solution)/shard_map/ppermute | solution.py:671
  311.2 2.4 collective-permute-start.5
  313.6 10.7 %collective-permute-done.10.refs_6_ = bf16[2,176,768]{2,1,0:T(8,128)(2,1)S(1)} collective-permute-done((bf16[2,176,768]{2,1,0:T(8,128)(2,1)S(1)}, bf16[2,176,768]{2,1,0:T(8,128)(2,1)S(1)}, u32[]{:S(2)}, u32[]{:S(2)}) %collective-permute-start.10) | collective-permute-done | bytes 540704 | tf_op jit(solution)/shard_map/ppermute | solution.py:671
  324.3 10.2 %collective-permute-done.3.refs_1_ = bf16[2,176,768]{2,1,0:T(8,128)(2,1)S(1)} collective-permute-done((bf16[2,176,768]{2,1,0:T(8,128)(2,1)S(1)}, bf16[2,176,768]{2,1,0:T(8,128)(2,1)S(1)}, u32[]{:S(2)}, u32[]{:S(2)}) %collective-permute-start.3) | collective-permute-done | bytes 540704 | tf_op jit(solution)/shard_map/ppermute | solution.py:671
  334.5 12.0 %collective-permute-done.4.refs_2_ = bf16[2,176,768]{2,1,0:T(8,128)(2,1)S(1)} collective-permute-done((bf16[2,176,768]{2,1,0:T(8,128)(2,1)S(1)}, bf16[2,176,768]{2,1,0:T(8,128)(2,1)S(1)}, u32[]{:S(2)}, u32[]{:S(2)}) %collective-permute-start.4) | collective-permute-done | bytes 540704 | tf_op jit(solution)/shard_map/ppermute | solution.py:671
  347.4 27.7 %combine.1 = (bf16[1024,768]{1,0:T(8,128)(2,1)}, f32[1024,12]{1,0:T(8,128)}, f32[1024,768]{1,0:T(8,128)}, bf16[1024,768]{1,0:T(8,128)(2,1)}, f32[16,1024]{1,0:T(...) custom-call(s32[1]{0:T(128)} %bitcast.me, bf16[2,176,768]{2,1,0:T(8,128)(2,1)} %get-tuple-element.74.refs_0_, ...), custom_call_target="tpu_custom_call" | custom-call | flops 9059696640 | bytes 25165824 | tf_op jit(solution)/shard_map/combine/pallas_call | solution.py:737
  375.1 46.4 %attend_back.1 = (bf16[1024,768]{1,0:T(8,128)(2,1)}, bf16[1024,768]{1,0:T(8,128)(2,1)}, bf16[1024,768]{1,0:T(8,128)(2,1)}) custom-call(s32[1]{0:T(128)S(6)} %copy.60.prefix, bf16[1024,768]{1,0:T(8,128)(2,1)} %get-tuple-element.63.q, bf16[1024,768]{1,0:T(8,128)(2,1)} %get-tuple-element.64.k, bf16[1024,768]{1,0:T(8,128)(2,1)} %get-tuple-element.65.v, ...), custom_call_target="tpu_custom_call" | custom-call | flops 64424509440 | bytes 12582912 | tf_op jit(solution)/shard_map/attend_back/pallas_call | solution.py:754
  421.6 15.4 %project_back.1 = (f32[1024,768]{1,0:T(8,128)}, bf16[768,2432]{1,0:T(8,128)(2,1)}) custom-call(bf16[1024,768]{1,0:T(8,128)(2,1)} %x.5, bf16[1024,768]{1,0:T(8,128)(2,1)} %get-tuple-element.90.normed, bf16[1024,768]{1,0:T(8,128)(2,1)} %get-tuple-element.94.dq, bf16[1024,768]{1,0:T(8,128)(2,1)} %get-tuple-element.95.dk, ...), custom_call_target="tpu_custom_call" | custom-call | flops 7247757312 | bytes 25165824 | tf_op jit(solution)/shard_map/project_back/pallas_call | solution.py:765
  436.9 4.6 pad_maximum_fusion
  441.6 23.1 %reduce-scatter.4.cloned.1.call-done.refs_0_ = bf16[2304,256]{1,0:T(8,128)(2,1)} async-done(((bf16[18432,256]{1,0:T(8,128)(2,1)}), bf16[2304,256]{1,0:T(8,128)(2,1)}) %reduce-scatter.4.cloned.1.call-update) | async-done | bytes 1179664 | tf_op jit(solution)/shard_map/reduce_scatter | solution.py:725
  464.7 57.5 %reduce-scatter.8.cloned.1.call-done = bf16[96,3200]{1,0:T(8,128)(2,1)} async-done(((bf16[768,3200]{1,0:T(8,128)(2,1)}), bf16[96,3200]{1,0:T(8,128)(2,1)}) %reduce-scatter.8.cloned.1.call-update) | async-done | bytes 614416 | tf_op jit(solution)/shard_map/reduce_scatter | solution.py:776
  526.4 4.2 collective-permute-done.14
  534.7 3.9 unpack.1
  539.3 6.1 %collective-permute-done.13 = bf16[48,3200]{1,0:T(8,128)(2,1)S(1)} collective-permute-done((bf16[48,3200]{1,0:T(8,128)(2,1)S(1)}, bf16[48,3200]{1,0:T(8,128)(2,1)S(1)}, u32[]{:S(2)}, u32[]{:S(2)}) %collective-permute-start.13) | collective-permute-done | bytes 307232 | tf_op jit(solution)/shard_map/ppermute | solution.py:781
  (102 shorter events, 35.2 us)
Async XLA Ops:
  7.2 50.8 %all-gather.5.cloned.1.call-start = ((), (), s32[]{:S(2)}) async-start(), calls=%async_computation.3 | async-start | bytes 4202496 | tf_op jit(solution)/shard_map/all_gather | solution.py:599
  12.1 69.2 %all-gather.7.cloned.1.call-start = ((), (), s32[]{:S(2)}) async-start(), calls=%async_computation.4 | async-start | bytes 1327104 | tf_op jit(solution)/shard_map/all_gather | solution.py:600
  12.8 160.5 %all-gather.11.cloned.1.call-start = ((), (), s32[]{:S(2)}) async-start(), calls=%async_computation.6 | async-start | bytes 10616832 | tf_op jit(solution)/shard_map/all_gather | solution.py:617
  15.2 249.3 %all-gather.9.cloned.1.call-start = ((), (), s32[]{:S(2)}) async-start(), calls=%async_computation.5 | async-start | bytes 10616832 | tf_op jit(solution)/shard_map/all_gather | solution.py:617
  17.7 423.9 %reduce-scatter.6.cloned.1.call-start = ((), (), s32[]{:S(2)}) async-start(), calls=%async_computation.8 | async-start | bytes 10616832 | tf_op jit(solution)/shard_map/reduce_scatter | solution.py:725
  128.3 15.4 %collective-permute-start.6 = (bf16[2,176,768]{2,1,0:T(8,128)(2,1)}, bf16[2,176,768]{2,1,0:T(8,128)(2,1)S(1)}, u32[]{:S(2)}, u32[]{:S(2)}) collective-permute-start(bf16[2,176,768]{2,1,0:T(8,128)(2,1)} %get-tuple-element.79), channel_id=1, source_target_pairs={{0,8},{8,0},{16,24},{24,16},{1,9},{9,1},{17,25},{25,17},{2,10},{10... | collective-permute-start | bytes 1622024 | tf_op jit(solution)/shard_map/ppermute | solution.py:671
  129.6 26.0 %collective-permute-start.7 = (bf16[2,176,768]{2,1,0:T(8,128)(2,1)}, bf16[2,176,768]{2,1,0:T(8,128)(2,1)S(1)}, u32[]{:S(2)}, u32[]{:S(2)}) collective-permute-start(bf16[2,176,768]{2,1,0:T(8,128)(2,1)} %get-tuple-element.80), channel_id=1, source_target_pairs={{0,16},{8,24},{16,0},{24,8},{1,17},{9,25},{17,1},{25,9},{2,18},{10... | collective-permute-start | bytes 1622024 | tf_op jit(solution)/shard_map/ppermute | solution.py:671
  131.1 24.5 %collective-permute-start.8 = (bf16[2,176,768]{2,1,0:T(8,128)(2,1)}, bf16[2,176,768]{2,1,0:T(8,128)(2,1)S(1)}, u32[]{:S(2)}, u32[]{:S(2)}) collective-permute-start(bf16[2,176,768]{2,1,0:T(8,128)(2,1)} %get-tuple-element.81), channel_id=1, source_target_pairs={{0,24},{8,16},{16,8},{24,0},{1,25},{9,17},{17,9},{25,1},{2,26},{10... | collective-permute-start | bytes 1622024 | tf_op jit(solution)/shard_map/ppermute | solution.py:671
  143.6 29.7 %copy-start.18 = (bf16[2,176,768]{2,1,0:T(8,128)(2,1)}, bf16[2,176,768]{2,1,0:T(8,128)(2,1)S(1)}, u32[]{:S(2)}) copy-start(bf16[2,176,768]{2,1,0:T(8,128)(2,1)S(1)} %collective-permute-done.6.refs_1_) | copy-start | bytes 1622020
  155.6 17.7 %copy-start.20 = (bf16[2,176,768]{2,1,0:T(8,128)(2,1)}, bf16[2,176,768]{2,1,0:T(8,128)(2,1)S(1)}, u32[]{:S(2)}) copy-start(bf16[2,176,768]{2,1,0:T(8,128)(2,1)S(1)} %collective-permute-done.7.refs_2_) | copy-start | bytes 1622020
  203.8 260.9 %reduce-scatter.4.cloned.1.call-start = ((), (), s32[]{:S(2)}) async-start(), calls=%async_computation.7 | async-start | bytes 10616832 | tf_op jit(solution)/shard_map/reduce_scatter | solution.py:725
  212.0 15.4 %collective-permute-start = (bf16[2,176,768]{2,1,0:T(8,128)(2,1)}, bf16[2,176,768]{2,1,0:T(8,128)(2,1)S(1)}, u32[]{:S(2)}, u32[]{:S(2)}) collective-permute-start(bf16[2,176,768]{2,1,0:T(8,128)(2,1)} %get-tuple-element.71), channel_id=1, source_target_pairs={{0,8},{8,0},{16,24},{24,16},{1,9},{9,1},{17,25},{25,17},{2,10},{10... | collective-permute-start | bytes 1622024 | tf_op jit(solution)/shard_map/ppermute | solution.py:671
  213.5 25.9 %collective-permute-start.1 = (bf16[2,176,768]{2,1,0:T(8,128)(2,1)}, bf16[2,176,768]{2,1,0:T(8,128)(2,1)S(1)}, u32[]{:S(2)}, u32[]{:S(2)}) collective-permute-start(bf16[2,176,768]{2,1,0:T(8,128)(2,1)} %get-tuple-element.72), channel_id=1, source_target_pairs={{0,16},{8,24},{16,0},{24,8},{1,17},{9,25},{17,1},{25,9},{2,18},{10... | collective-permute-start | bytes 1622024 | tf_op jit(solution)/shard_map/ppermute | solution.py:671
  214.9 24.5 %collective-permute-start.2 = (bf16[2,176,768]{2,1,0:T(8,128)(2,1)}, bf16[2,176,768]{2,1,0:T(8,128)(2,1)S(1)}, u32[]{:S(2)}, u32[]{:S(2)}) collective-permute-start(bf16[2,176,768]{2,1,0:T(8,128)(2,1)} %get-tuple-element.73), channel_id=1, source_target_pairs={{0,24},{8,16},{16,8},{24,0},{1,25},{9,17},{17,9},{25,1},{2,26},{10... | collective-permute-start | bytes 1622024 | tf_op jit(solution)/shard_map/ppermute | solution.py:671
  227.4 37.2 %copy-start.19 = (bf16[2,176,768]{2,1,0:T(8,128)(2,1)}, bf16[2,176,768]{2,1,0:T(8,128)(2,1)S(1)}, u32[]{:S(2)}) copy-start(bf16[2,176,768]{2,1,0:T(8,128)(2,1)S(1)} %collective-permute-done.refs_1_) | copy-start | bytes 1622020
  239.4 25.1 %copy-start.21 = (bf16[2,176,768]{2,1,0:T(8,128)(2,1)}, bf16[2,176,768]{2,1,0:T(8,128)(2,1)S(1)}, u32[]{:S(2)}) copy-start(bf16[2,176,768]{2,1,0:T(8,128)(2,1)S(1)} %collective-permute-done.1.refs_2_) | copy-start | bytes 1622020
  239.4 25.1 %copy-start.23 = (bf16[2,176,768]{2,1,0:T(8,128)(2,1)}, bf16[2,176,768]{2,1,0:T(8,128)(2,1)S(1)}, u32[]{:S(2)}) copy-start(bf16[2,176,768]{2,1,0:T(8,128)(2,1)S(1)} %collective-permute-done.2.refs_3_) | copy-start | bytes 1622020
  295.1 227.1 %reduce-scatter.8.cloned.1.call-start = ((), (), s32[]{:S(2)}) async-start(), calls=%async_computation.9 | async-start | bytes 5529600 | tf_op jit(solution)/shard_map/reduce_scatter | solution.py:776
  296.1 15.1 %collective-permute-start.9 = (bf16[2,176,768]{2,1,0:T(8,128)(2,1)S(1)}, bf16[2,176,768]{2,1,0:T(8,128)(2,1)S(1)}, u32[]{:S(2)}, u32[]{:S(2)}) collective-permute-start(bf16[2,176,768]{2,1,0:T(8,128)(2,1)S(1)} %copy-done.8), channel_id=1, source_target_pairs={{0,8},{8,0},{16,24},{24,16},{1,9},{9,1},{17,25},{25,17},{2,10},{10... | collective-permute-start | bytes 1622024 | tf_op jit(solution)/shard_map/ppermute | solution.py:671
  297.6 26.7 %collective-permute-start.10 = (bf16[2,176,768]{2,1,0:T(8,128)(2,1)S(1)}, bf16[2,176,768]{2,1,0:T(8,128)(2,1)S(1)}, u32[]{:S(2)}, u32[]{:S(2)}) collective-permute-start(bf16[2,176,768]{2,1,0:T(8,128)(2,1)S(1)} %copy-done.7), channel_id=1, source_target_pairs={{0,16},{8,24},{16,0},{24,8},{1,17},{9,25},{17,1},{25,9},{2,18},{10... | collective-permute-start | bytes 1622024 | tf_op jit(solution)/shard_map/ppermute | solution.py:671
  299.0 25.3 %collective-permute-start.11 = (bf16[2,176,768]{2,1,0:T(8,128)(2,1)S(1)}, bf16[2,176,768]{2,1,0:T(8,128)(2,1)S(1)}, u32[]{:S(2)}, u32[]{:S(2)}) collective-permute-start(bf16[2,176,768]{2,1,0:T(8,128)(2,1)S(1)} %copy-done.6), channel_id=1, source_target_pairs={{0,24},{8,16},{16,8},{24,0},{1,25},{9,17},{17,9},{25,1},{2,26},{10... | collective-permute-start | bytes 1622024 | tf_op jit(solution)/shard_map/ppermute | solution.py:671
  299.6 34.9 %collective-permute-start.3 = (bf16[2,176,768]{2,1,0:T(8,128)(2,1)S(1)}, bf16[2,176,768]{2,1,0:T(8,128)(2,1)S(1)}, u32[]{:S(2)}, u32[]{:S(2)}) collective-permute-start(bf16[2,176,768]{2,1,0:T(8,128)(2,1)S(1)} %copy-done.14), channel_id=1, source_target_pairs={{0,8},{8,0},{16,24},{24,16},{1,9},{9,1},{17,25},{25,17},{2,10},{10... | collective-permute-start | bytes 1622024 | tf_op jit(solution)/shard_map/ppermute | solution.py:671
  301.1 45.4 %collective-permute-start.4 = (bf16[2,176,768]{2,1,0:T(8,128)(2,1)S(1)}, bf16[2,176,768]{2,1,0:T(8,128)(2,1)S(1)}, u32[]{:S(2)}, u32[]{:S(2)}) collective-permute-start(bf16[2,176,768]{2,1,0:T(8,128)(2,1)S(1)} %copy-done.12), channel_id=1, source_target_pairs={{0,16},{8,24},{16,0},{24,8},{1,17},{9,25},{17,1},{25,9},{2,18},{10... | collective-permute-start | bytes 1622024 | tf_op jit(solution)/shard_map/ppermute | solution.py:671
  311.2 35.2 %copy-start.9 = (bf16[2,176,768]{2,1,0:T(8,128)(2,1)}, bf16[2,176,768]{2,1,0:T(8,128)(2,1)S(1)}, u32[]{:S(2)}) copy-start(bf16[2,176,768]{2,1,0:T(8,128)(2,1)S(1)} %collective-permute-done.9.refs_5_) | copy-start | bytes 1622020
  311.2 35.2 %collective-permute-start.5 = (bf16[2,176,768]{2,1,0:T(8,128)(2,1)S(1)}, bf16[2,176,768]{2,1,0:T(8,128)(2,1)S(1)}, u32[]{:S(2)}, u32[]{:S(2)}) collective-permute-start(bf16[2,176,768]{2,1,0:T(8,128)(2,1)S(1)} %copy-done.10), channel_id=1, source_target_pairs={{0,24},{8,16},{16,8},{24,0},{1,25},{9,17},{17,9},{25,1},{2,26},{10... | collective-permute-start | bytes 1622024 | tf_op jit(solution)/shard_map/ppermute | solution.py:671
  324.3 22.2 %copy-start.11 = (bf16[2,176,768]{2,1,0:T(8,128)(2,1)}, bf16[2,176,768]{2,1,0:T(8,128)(2,1)S(1)}, u32[]{:S(2)}) copy-start(bf16[2,176,768]{2,1,0:T(8,128)(2,1)S(1)} %collective-permute-done.10.refs_6_) | copy-start | bytes 1622020
  324.3 22.2 %copy-start.13 = (bf16[2,176,768]{2,1,0:T(8,128)(2,1)}, bf16[2,176,768]{2,1,0:T(8,128)(2,1)S(1)}, u32[]{:S(2)}) copy-start(bf16[2,176,768]{2,1,0:T(8,128)(2,1)S(1)} %collective-permute-done.11.refs_7_) | copy-start | bytes 1622020
  464.7 69.2 %copy-start.2 = (f32[1024,12]{1,0:T(8,128)S(1)}, f32[1024,12]{1,0:T(8,128)}, u32[]{:S(2)}) copy-start(f32[1024,12]{1,0:T(8,128)} %get-tuple-element.128) | copy-start | bytes 147460
  523.4 7.2 %collective-permute-start.14 = (bf16[48,3200]{1,0:T(8,128)(2,1)S(1)}, bf16[48,3200]{1,0:T(8,128)(2,1)S(1)}, u32[]{:S(2)}, u32[]{:S(2)}) collective-permute-start(bf16[48,3200]{1,0:T(8,128)(2,1)S(1)} %get-tuple-element.149), channel_id=1, source_target_pairs={{0,16},{8,24},{16,0},{24,8},{1,17},{9,25},{17,1},{25,9},{2,18},{10... | collective-permute-start | bytes 921608 | tf_op jit(solution)/shard_map/ppermute | solution.py:781
  524.9 7.2 %collective-permute-start.12 = (bf16[48,3200]{1,0:T(8,128)(2,1)S(1)}, bf16[48,3200]{1,0:T(8,128)(2,1)S(1)}, u32[]{:S(2)}, u32[]{:S(2)}) collective-permute-start(bf16[48,3200]{1,0:T(8,128)(2,1)S(1)} %get-tuple-element.150), channel_id=1, source_target_pairs={{0,8},{8,0},{16,24},{24,16},{1,9},{9,1},{17,25},{25,17},{2,10},{10... | collective-permute-start | bytes 921608 | tf_op jit(solution)/shard_map/ppermute | solution.py:781
  532.3 6.9 %collective-permute-start.15 = (bf16[48,3200]{1,0:T(8,128)(2,1)S(1)}, bf16[48,3200]{1,0:T(8,128)(2,1)S(1)}, u32[]{:S(2)}, u32[]{:S(2)}) collective-permute-start(bf16[48,3200]{1,0:T(8,128)(2,1)S(1)} %get-tuple-element.147), channel_id=1, source_target_pairs={{0,8},{8,0},{16,24},{24,16},{1,9},{9,1},{17,25},{25,17},{2,10},{10... | collective-permute-start | bytes 921608 | tf_op jit(solution)/shard_map/ppermute | solution.py:781
  538.6 6.9 %collective-permute-start.13 = (bf16[48,3200]{1,0:T(8,128)(2,1)S(1)}, bf16[48,3200]{1,0:T(8,128)(2,1)S(1)}, u32[]{:S(2)}, u32[]{:S(2)}) collective-permute-start(bf16[48,3200]{1,0:T(8,128)(2,1)S(1)} %get-tuple-element.148), channel_id=1, source_target_pairs={{0,16},{8,24},{16,0},{24,8},{1,17},{9,25},{17,1},{25,9},{2,18},{10... | collective-permute-start | bytes 921608 | tf_op jit(solution)/shard_map/ppermute | solution.py:781
  (15 other events, 98.7 us)
Sparse Core Ops, SparseCore 0:
  12.2 45.7 all-gather.4
  59.7 21.5 all-gather.6
  82.9 90.3 all-gather.10
  175.4 89.1 all-gather.8
  266.7 97.8 reduce-scatter.5
  366.7 97.8 reduce-scatter.3
  467.0 55.1 reduce-scatter.7

commit v3 on v2

--- a/solution.py
+++ b/solution.py
@@ -519,7 +519,8 @@
 
 
 def project_back_kernel(
-    x, normed, dq, dk, dv, resg, wq, wk, wv, small_t, small_g, tok_out, grad_out, acc, first_acc
+    me, x, normed, dq, dk, dv, resg, wq, wk, wv, small_t, small_g, output_g,
+    tok_out, grad_out, acc, first_acc,
 ):
     step = pl.program_id(0)
     block, width = x.shape
@@ -545,11 +546,14 @@
 
     @pl.when(step == pl.num_programs(0) - 1)
     def _():
-        grad_out[:, 0 : 3 * width] = acc[...].astype(BF16)
+        for j in range(3):
+            grad_out[me[0] ^ j, :, 0:width] = acc[:, j * width : (j + 1) * width].astype(BF16)
+            grad_out[me[0] ^ j, :, width : width + LANES] = jnp.zeros((width, LANES), BF16)
         first = jnp.sum(first_acc[...], axis=0, keepdims=True)
         row = iota((LANES, width), 0)
         extra = small_g[...] + jnp.where(row == 16, first, 0.0).T
-        grad_out[:, 3 * width : 3 * width + LANES] = extra.astype(BF16)
+        grad_out[me[0] ^ 3, :, 0:width] = output_g[...]
+        grad_out[me[0] ^ 3, :, width : width + LANES] = extra.astype(BF16)
 
 
 def rotary_tables():
@@ -684,14 +688,15 @@
             scratch=[pltpu.VMEM((count, LANES), BF16)],
             flops=4 * owners * stride * count * width, traffic=6 << 20, prefetch=1,
         )(me, normed_two, cotangent, tok, routes, dest_row)
-        return exchange(parts)
-
-    received = [dispatch(l) for l in range(local_experts)]
+        return parts
+
+    dispatched = [dispatch(l) for l in range(local_experts)]
+    received = [exchange(parts) for parts in dispatched]
 
     chunks, chunk_rows = (shards, shard_rows) if aligned else (1, width)
     local = owners * stride
 
-    def run_expert(l):
+    def run_expert(l, rows):
         gate_up, down = expert_full[l]
         weights = [
             pl.BlockSpec((chunks, chunk_rows, TILE), lambda f, j=j: (0, j // 2 * tiles + 2 * f + j % 2, 0))
@@ -711,7 +716,7 @@
             [pair_shape] * owners + [struct(g, BF16) for g in grad_shapes],
             scratch=[pltpu.VMEM((local, width), BF16)] * 2 + [pltpu.VMEM((local, width), F32)] * 2,
             flops=16 * local * width * ff, traffic=24 << 20, trans=local * ff,
-        )(*received[l], gate_up, gate_up, gate_up, gate_up, down, down)
+        )(*rows, gate_up, gate_up, gate_up, gate_up, down, down)
         grads = outs[owners:]
         if aligned:
             grad = grads[0]
@@ -730,8 +735,10 @@
     returned = []
     expert_sums = []
     for l in range(local_experts):
-        back, total = run_expert(l)
-        returned += back
+        rows, ahead = lax.optimization_barrier((received[l], returned or dispatched[-1]))
+        returned = ahead if returned else returned
+        back, total = run_expert(l, rows)
+        returned = returned + back
         expert_sums.append(total)
 
     mixed, previous_grad, residual_grad, heads_grad, delta, output_grad, small_grad = call(
@@ -764,25 +771,30 @@
 
     tokens_grad, dense_grad = call(
         project_back_kernel, "project_back", (steps,),
-        [wide] * 6 + weight_block + [whole((LANES, width)), whole((width, LANES))],
-        [wide, whole((width, packed_width))],
-        [struct((count, width), F32), struct((width, packed_width), BF16)],
+        [wide] * 6 + weight_block + [whole((LANES, width)), whole((width, LANES)), whole((width, width))],
+        [wide, whole((owners, width, width + LANES))],
+        [struct((count, width), F32), struct((owners, width, width + LANES), BF16)],
         scratch=[pltpu.VMEM((width, 3 * width), F32), pltpu.VMEM((8, width), F32)],
-        flops=12 * count * width * width, traffic=24 << 20,
-    )(tokens, normed_one, dq, dk, dv, residual_grad, qkv_full, qkv_full, qkv_full, small_t,
-      small_grad)
-    dense_grad = jnp.concatenate([dense_grad, output_grad], axis=1)
-    dense_grad, expert_sums = lax.optimization_barrier((dense_grad, expert_sums))
-    dense_sum = lax.psum_scatter(dense_grad, "shard", scatter_dimension=0, tiled=True)
-    half = shard_rows // 2
-    parts = [dense_sum[:half], dense_sum[half:]]
-    moves = [[(i, i ^ k) for i in range(owners)] for k in (1, 2)]
-    for turn in range(2):
-        other = [lax.ppermute(parts[j], "expert", moves[(turn + j) % 2]) for j in range(2)]
-        parts = [(a.astype(F32) + b.astype(F32)).astype(F32 if turn else BF16)
-                 for a, b in zip(parts, other)]
-    dense = jnp.concatenate(parts, axis=0)
-    small = dense[:, 3 * width : 3 * width + LANES]
+        flops=12 * count * width * width, traffic=24 << 20, prefetch=1,
+    )(me, tokens, normed_one, dq, dk, dv, residual_grad, qkv_full, qkv_full, qkv_full, small_t,
+      small_grad, output_grad)
+
+    def send(part, k):
+        return lax.ppermute(part, "expert", [(i, i ^ k) for i in range(owners)])
+
+    def add(a, b):
+        return (a.astype(F32) + b.astype(F32)).astype(BF16)
+
+    half = width // 2
+    top, low = dense_grad[:, :half], dense_grad[:, half:]
+    top_in, low_in = send(top[1::2], 1), send(low[2:], 2)
+    top, low = add(top[0::2], top_in), add(low[:2], low_in)
+    top_in, low_in = send(top[1], 2), send(low[1], 1)
+    quarter = jnp.concatenate([add(top[0], top_in), add(low[0], low_in)], axis=0)
+    quarter, expert_sums = lax.optimization_barrier((quarter, expert_sums))
+    quarter = lax.psum_scatter(quarter, "shard", scatter_dimension=0, tiled=True)
+    dense = lax.all_gather(quarter, "expert", axis=0, tiled=False).astype(F32)
+    small = dense[3, :, width:]
     if aligned:
         out_shapes = [w.shape for w in (gate_weight, up_weight, down_weight)]
         gate_sum, up_sum, down_sum = call(
@@ -806,10 +818,10 @@
         mixed,
         tokens_grad,
         previous_grad,
-        dense[:, 0:width],
-        dense[:, width : 2 * width],
-        dense[:, 2 * width : 3 * width],
-        dense[:, packed_width:],
+        dense[0, :, :width],
+        dense[1, :, :width],
+        dense[2, :, :width],
+        dense[3, :, :width],
         small[:, 0:kinds],
         small[:, kinds : kinds + 4],
         small[:, 18:20].T,

time: 557 us -> 530 us (0.952); the launches traced: 556 us -> 522 us
  waiting for transfers between devices: 270 us -> 222 us
  blocking collectives: 0 us -> 11.2 us
    reduce_scatter x1, waiting for transfers between devices: 57.5 us -> 26.6 us  [body(): lax.psum_scatter(quarter, 'shard', scatter_dimension=0, tiled=True)]
    ppermute x4, waiting for transfers between devices: 12 us -> 42.6 us  [send(): return lax.ppermute(part, 'expert', [(i, i ^ k) for i in range(owners)])]
    reduce_scatter x2, waiting for transfers between devices: 23.1 us -> 0.01 us  [run_expert(): lax.psum_scatter(grad.reshape(shards * expert_rows, TILE), 'shard', scatt...]
    all_gather x2, waiting for transfers between devices: 42.8 us -> 26.9 us  [gather_expert(): full = lax.all_gather(one, 'shard', axis=0, tiled=True)]
    all_gather x0 -> x1, blocking collectives: none -> 11.2 us  [body(): dense = lax.all_gather(quarter, 'expert', axis=0, tiled=False).astype(F32)]
    ppermute x12, waiting for transfers between devices: 89.3 us -> 81.2 us  [exchange(): lax.ppermute(part, 'expert', [(i, i ^ k) for i in range(owners)])]
  transfers between devices with their start and end apart: 23 -> 23, of which waited for: 18 -> 17; matrix products, arithmetic and copies ran while one was open for 2% -> 2% of each run, Pallas kernels for 41% -> 44%
where the time goes in v3:
time: 530 us; the launch traced here: 522 us
  Pallas kernels  233 us (44%)
  waiting for transfers between devices  222 us (42%)
  starting transfers between devices  19.8 us (4%)
  local copies, waits for them, and re-layouts  16.7 us (3%)
  between operations  15.5 us (3%)
  blocking collectives  11.2 us (2%)
    ppermute x12, waiting for transfers between devices, exchange(): lax.ppermute(part, 'expert', [(i, i ^ k) for i in range(owners)])  81.2 us
    pallas_call x2, Pallas kernels, run_expert(): call(functools.partial(expert_kernel, owners, aligned), 'expert', (tiles...  61.1 us
    pallas_call x1, Pallas kernels, body(): call(attend_back_kernel, 'attend_back', (width // LANES,), [pair_block] *...  46.4 us
    ppermute x4, waiting for transfers between devices, send(): return lax.ppermute(part, 'expert', [(i, i ^ k) for i in range(owners)])  42.6 us
    pallas_call x1, Pallas kernels, body(): call(attend_kernel, 'attend', (steps,), [wide, whole((count, width)), who...  39 us
    all_gather x1, waiting for transfers between devices, body(): qkv_full = lax.all_gather(packed, 'shard', axis=0, tiled=True)  29.7 us
    pallas_call x1, Pallas kernels, body(): call(functools.partial(combine_kernel, experts, owners, local_experts), '...  27.6 us
    all_gather x2, waiting for transfers between devices, gather_expert(): full = lax.all_gather(one, 'shard', axis=0, tiled=True)  26.9 us
  transfers between devices with their start and end apart: 23, of which 17 were waited for; matrix products, arithmetic and copies ran while one was open for 2% of the time, Pallas kernels for 44%

profile of v3, /device:TPU:0, one launch (start us, length us, event | category | flops | bytes accessed | tf_op | source)
XLA Modules:
  0.0 522.1 jit_solution(14858167899193361966)
XLA Ops:
  10.0 2.0 pack.1
  12.9 2.3 pack_expert.2
  15.3 2.3 pack_expert.3
  21.4 6.9 %slots.1 = (s32[1024,128]{1,0:T(8,128)}, s32[8,1024]{1,0:T(8,128)}) custom-call(s32[1024,2]{1,0:T(8,128)} %copy.48.routes.refs_12_, s32[1,1024]{1,0:T(1,128)} %order_row.1, s32[1024,1]{1,0:T(8,128)} %copy.50.order_col), custom_call_target="tpu_custom_call" | custom-call | flops 805306368 | bytes 1048576 | tf_op jit(solution)/shard_map/slots/pallas_call | solution.py:636
  28.3 29.7 %all-gather.6.cloned.1.call-done.wq.wk.wv.small = bf16[768,2432]{1,0:T(8,128)(2,1)} async-done(((bf16[96,2432]{1,0:T(8,128)(2,1)}), bf16[768,2432]{1,0:T(8,128)(2,1)}) %all-gather.6.cloned.1.call-update) | async-done | bytes 3735568 | tf_op jit(solution)/shard_map/all_gather | solution.py:603
  58.0 8.7 %project.1 = (bf16[1024,768]{1,0:T(8,128)(2,1)}, bf16[1024,768]{1,0:T(8,128)(2,1)}, bf16[1024,768]{1,0:T(8,128)(2,1)}, bf16[1024,768]{1,0:T(8,128)(2,1)}, f32[128,768]{1,0:T(8,128)}) custom-call(bf16[1024,768]{1,0:T(8,128)(2,1)} %x.5, bf16[768,2432]{1,0:T(8,128)(2,1)} %all-gather.6.cloned.1.call-done.wq.wk.wv.small, ...), custom_call_target="tpu_custom_call" | custom-call | flops 3623878656 | bytes 12582912 | tf_op jit(solution)/shard_map/project/pallas_call | solution.py:652
  66.7 14.6 %all-gather.8.cloned.1.call-done.wo.refs_15_ = bf16[768,768]{1,0:T(8,128)(2,1)} async-done(((bf16[96,768]{1,0:T(8,128)(2,1)}), bf16[768,768]{1,0:T(8,128)(2,1)}) %all-gather.8.cloned.1.call-update) | async-done | bytes 1179664 | tf_op jit(solution)/shard_map/all_gather | solution.py:604
  81.3 39.0 %attend.1 = (bf16[1024,768]{1,0:T(8,128)(2,1)}, f32[16,1024]{1,0:T(8,128)}, f32[1024,768]{1,0:T(8,128)}, bf16[1024,768]{1,0:T(8,128)(2,1)}, f32[1024,128]{1,0:T(8,128)}) custom-call(s32[1]{0:T(128)S(6)} %copy.57.prefix, bf16[1024,768]{1,0:T(8,128)(2,1)} %get-tuple-element.75.q, bf16[1024,768]{1,0:T(8,128)(2,1)} %get-tuple-element.76.k, ...), custom_call_target="tpu_custom_call" | custom-call | flops 32212254720 | bytes 16777216 | tf_op jit(solution)/shard_map/attend/pallas_call | solution.py:660
  120.3 7.9 %dispatch.3 = (bf16[2,176,768]{2,1,0:T(8,128)(2,1)}, bf16[2,176,768]{2,1,0:T(8,128)(2,1)}, bf16[2,176,768]{2,1,0:T(8,128)(2,1)}, bf16[2,176,768]{2,1,0:T(8,128)(2,1)}) custom-call(s32[1]{0:T(128)} %bitcast.me, bf16[1024,768]{1,0:T(8,128)(2,1)} %get-tuple-element.79.normed.refs_9_, bf16[1024,768]{1,0:T(8,128)(2,1)} %refs_10_.1, ...), custom_call_target="tpu_custom_call" | custom-call | flops 2214592512 | bytes 6291456 | tf_op jit(solution)/shard_map/dispatch/pallas_call | solution.py:683
  131.7 7.9 %dispatch.2 = (bf16[2,176,768]{2,1,0:T(8,128)(2,1)}, bf16[2,176,768]{2,1,0:T(8,128)(2,1)}, bf16[2,176,768]{2,1,0:T(8,128)(2,1)}, bf16[2,176,768]{2,1,0:T(8,128)(2,1)}) custom-call(s32[1]{0:T(128)} %bitcast.me, bf16[1024,768]{1,0:T(8,128)(2,1)} %get-tuple-element.79.normed.refs_9_, bf16[1024,768]{1,0:T(8,128)(2,1)} %refs_10_.1, ...), custom_call_target="tpu_custom_call" | custom-call | flops 2214592512 | bytes 6291456 | tf_op jit(solution)/shard_map/dispatch/pallas_call | solution.py:683
  139.6 4.0 collective-permute-done.3.refs_1_
  143.6 12.0 %collective-permute-done.4.refs_2_ = bf16[2,176,768]{2,1,0:T(8,128)(2,1)S(1)} collective-permute-done((bf16[2,176,768]{2,1,0:T(8,128)(2,1)}, bf16[2,176,768]{2,1,0:T(8,128)(2,1)S(1)}, u32[]{:S(2)}, u32[]{:S(2)}) %collective-permute-start.4) | collective-permute-done | bytes 540704 | tf_op jit(solution)/shard_map/ppermute | solution.py:675
  155.6 18.3 %all-gather.10.cloned.1.call-done = bf16[18432,256]{1,0:T(8,128)(2,1)} async-done(((bf16[2304,256]{1,0:T(8,128)(2,1)}), bf16[18432,256]{1,0:T(8,128)(2,1)}) %all-gather.10.cloned.1.call-update) | async-done | bytes 9437200 | tf_op jit(solution)/shard_map/all_gather | solution.py:621
  173.9 30.7 %expert.2 = (bf16[2,176,768]{2,1,0:T(8,128)(2,1)}, bf16[2,176,768]{2,1,0:T(8,128)(2,1)}, bf16[2,176,768]{2,1,0:T(8,128)(2,1)}, bf16[2,176,768]{2,1,0:T(8,128)(2,1)}, bf16[8,2304,256]{2,1,0:T(8,128)(2,1)}) custom-call(bf16[2,176,768]{2,1,0:T(8,128)(2,1)} %get-tuple-element.90.refs_0_, bf16[2,176,768]{2,1,0:T(8,128)(2,1)} %copy-done.15, ...), custom_call_target="tpu_custom_call" | custom-call | flops 17716740096 | bytes 25165824 | tf_op jit(solution)/shard_map/expert/pallas_call | solution.py:712
  212.1 8.7 %collective-permute-done.refs_1_ = bf16[2,176,768]{2,1,0:T(8,128)(2,1)S(1)} collective-permute-done((bf16[2,176,768]{2,1,0:T(8,128)(2,1)S(1)}, bf16[2,176,768]{2,1,0:T(8,128)(2,1)S(1)}, u32[]{:S(2)}, u32[]{:S(2)}) %collective-permute-start) | collective-permute-done | bytes 540704 | tf_op jit(solution)/shard_map/ppermute | solution.py:675
  220.8 2.4 collective-permute-start.8
  223.2 10.7 %collective-permute-done.1.refs_2_ = bf16[2,176,768]{2,1,0:T(8,128)(2,1)S(1)} collective-permute-done((bf16[2,176,768]{2,1,0:T(8,128)(2,1)S(1)}, bf16[2,176,768]{2,1,0:T(8,128)(2,1)S(1)}, u32[]{:S(2)}, u32[]{:S(2)}) %collective-permute-start.1) | collective-permute-done | bytes 540704 | tf_op jit(solution)/shard_map/ppermute | solution.py:675
  233.9 10.1 %collective-permute-done.6.refs_1_ = bf16[2,176,768]{2,1,0:T(8,128)(2,1)S(1)} collective-permute-done((bf16[2,176,768]{2,1,0:T(8,128)(2,1)}, bf16[2,176,768]{2,1,0:T(8,128)(2,1)S(1)}, u32[]{:S(2)}, u32[]{:S(2)}) %collective-permute-start.6) | collective-permute-done | bytes 540704 | tf_op jit(solution)/shard_map/ppermute | solution.py:675
  244.0 12.0 %collective-permute-done.7.refs_2_ = bf16[2,176,768]{2,1,0:T(8,128)(2,1)S(1)} collective-permute-done((bf16[2,176,768]{2,1,0:T(8,128)(2,1)}, bf16[2,176,768]{2,1,0:T(8,128)(2,1)S(1)}, u32[]{:S(2)}, u32[]{:S(2)}) %collective-permute-start.7) | collective-permute-done | bytes 540704 | tf_op jit(solution)/shard_map/ppermute | solution.py:675
  256.1 8.5 %all-gather.12.cloned.1.call-done = bf16[18432,256]{1,0:T(8,128)(2,1)} async-done(((bf16[2304,256]{1,0:T(8,128)(2,1)}), bf16[18432,256]{1,0:T(8,128)(2,1)}) %all-gather.12.cloned.1.call-update) | async-done | bytes 9437200 | tf_op jit(solution)/shard_map/all_gather | solution.py:621
  264.6 30.4 %expert.3 = (bf16[2,176,768]{2,1,0:T(8,128)(2,1)}, bf16[2,176,768]{2,1,0:T(8,128)(2,1)}, bf16[2,176,768]{2,1,0:T(8,128)(2,1)}, bf16[2,176,768]{2,1,0:T(8,128)(2,1)}, bf16[8,2304,256]{2,1,0:T(8,128)(2,1)}) custom-call(bf16[2,176,768]{2,1,0:T(8,128)(2,1)} %get-tuple-element.102.refs_0_, bf16[2,176,768]{2,1,0:T(8,128)(2,1)} %copy-done.11, ...), custom_call_target="tpu_custom_call" | custom-call | flops 17716740096 | bytes 25165824 | tf_op jit(solution)/shard_map/expert/pallas_call | solution.py:712
  299.6 11.7 %collective-permute-done.9.refs_5_ = bf16[2,176,768]{2,1,0:T(8,128)(2,1)S(1)} collective-permute-done((bf16[2,176,768]{2,1,0:T(8,128)(2,1)S(1)}, bf16[2,176,768]{2,1,0:T(8,128)(2,1)S(1)}, u32[]{:S(2)}, u32[]{:S(2)}) %collective-permute-start.9) | collective-permute-done | bytes 540704 | tf_op jit(solution)/shard_map/ppermute | solution.py:675
  311.3 12.0 %collective-permute-done.10.refs_6_ = bf16[2,176,768]{2,1,0:T(8,128)(2,1)S(1)} collective-permute-done((bf16[2,176,768]{2,1,0:T(8,128)(2,1)S(1)}, bf16[2,176,768]{2,1,0:T(8,128)(2,1)S(1)}, u32[]{:S(2)}, u32[]{:S(2)}) %collective-permute-start.10) | collective-permute-done | bytes 540704 | tf_op jit(solution)/shard_map/ppermute | solution.py:675
  324.3 27.6 %combine.1 = (bf16[1024,768]{1,0:T(8,128)(2,1)}, f32[1024,12]{1,0:T(8,128)}, f32[1024,768]{1,0:T(8,128)}, bf16[1024,768]{1,0:T(8,128)(2,1)}, f32[16,1024]{1,0:T(...) custom-call(s32[1]{0:T(128)} %bitcast.me, bf16[2,176,768]{2,1,0:T(8,128)(2,1)} %get-tuple-element.98.refs_0_, ...), custom_call_target="tpu_custom_call" | custom-call | flops 9059696640 | bytes 25165824 | tf_op jit(solution)/shard_map/combine/pallas_call | solution.py:744
  351.9 46.4 %attend_back.1 = (bf16[1024,768]{1,0:T(8,128)(2,1)}, bf16[1024,768]{1,0:T(8,128)(2,1)}, bf16[1024,768]{1,0:T(8,128)(2,1)}) custom-call(s32[1]{0:T(128)S(6)} %copy.57.prefix, bf16[1024,768]{1,0:T(8,128)(2,1)} %get-tuple-element.75.q, bf16[1024,768]{1,0:T(8,128)(2,1)} %get-tuple-element.76.k, bf16[1024,768]{1,0:T(8,128)(2,1)} %get-tuple-element.77.v, ...), custom_call_target="tpu_custom_call" | custom-call | flops 64424509440 | bytes 12582912 | tf_op jit(solution)/shard_map/attend_back/pallas_call | solution.py:761
  398.3 16.7 %project_back.1 = (f32[1024,768]{1,0:T(8,128)}, bf16[4,768,896]{2,1,0:T(8,128)(2,1)}) custom-call(s32[1]{0:T(128)} %bitcast.me, bf16[1024,768]{1,0:T(8,128)(2,1)} %x.5, bf16[1024,768]{1,0:T(8,128)(2,1)} %get-tuple-element.114.normed, bf16[1024,768]{1,0:T(8,128)(2,1)} %get-tuple-element.118.dq, bf16[1024,768]{1,0:T(8,128)(2,1)} %get-tuple-element.119.dk, ...), custom_call_target="tpu_custom_call" | custom-call | flops 7247757312 | bytes 25165824 | tf_op jit(solution)/shard_map/project_back/pallas_call | solution.py:772
  418.1 2.0 slice.60
  420.8 26.9 %collective-permute-done.14 = bf16[2,384,896]{2,1,0:T(8,128)(2,1)S(1)} collective-permute-done((bf16[2,384,896]{2,1,0:T(8,128)(2,1)S(1)}, bf16[2,384,896]{2,1,0:T(8,128)(2,1)S(1)}, u32[]{:S(2)}, u32[]{:S(2)}) %collective-permute-start.14) | collective-permute-done | bytes 1376288 | tf_op jit(solution)/shard_map/ppermute | solution.py:783
  452.5 13.5 %collective-permute-done.15 = bf16[384,896]{1,0:T(8,128)(2,1)S(1)} collective-permute-done((bf16[384,896]{1,0:T(8,128)(2,1)S(1)}, bf16[384,896]{1,0:T(8,128)(2,1)S(1)}, u32[]{:S(2)}, u32[]{:S(2)}) %collective-permute-start.15) | collective-permute-done | bytes 688160 | tf_op jit(solution)/shard_map/ppermute | solution.py:783
  469.6 3.9 unpack.1
  473.5 26.6 %reduce-scatter.8.cloned.1.call-done = bf16[96,896]{1,0:T(8,128)(2,1)} async-done(((bf16[768,896]{1,0:T(8,128)(2,1)}), bf16[96,896]{1,0:T(8,128)(2,1)}) %reduce-scatter.8.cloned.1.call-update) | async-done | bytes 172048 | tf_op jit(solution)/shard_map/reduce_scatter | solution.py:795
  500.1 11.2 %all-gather = bf16[384,896]{1,0:T(8,128)(2,1)S(1)} all-gather(bf16[96,896]{1,0:T(8,128)(2,1)} %reduce-scatter.8.cloned.1.call-done), channel_id=2, replica_groups=mesh['expert'=4,'shard'=8] {'expert'}, dimensions={0}, use_global_device_ids=true | all-gather | bytes 860160 | tf_op jit(solution)/shard_map/all_gather | solution.py:796
  (106 shorter events, 38.8 us)
Async XLA Ops:
  7.2 50.8 %all-gather.6.cloned.1.call-start = ((), (), s32[]{:S(2)}) async-start(), calls=%async_computation.3 | async-start | bytes 4202496 | tf_op jit(solution)/shard_map/all_gather | solution.py:603
  12.1 69.2 %all-gather.8.cloned.1.call-start = ((), (), s32[]{:S(2)}) async-start(), calls=%async_computation.4 | async-start | bytes 1327104 | tf_op jit(solution)/shard_map/all_gather | solution.py:604
  12.8 161.1 %all-gather.10.cloned.1.call-start = ((), (), s32[]{:S(2)}) async-start(), calls=%async_computation.5 | async-start | bytes 10616832 | tf_op jit(solution)/shard_map/all_gather | solution.py:621
  15.2 249.4 %all-gather.12.cloned.1.call-start = ((), (), s32[]{:S(2)}) async-start(), calls=%async_computation.6 | async-start | bytes 10616832 | tf_op jit(solution)/shard_map/all_gather | solution.py:621
  17.6 451.1 %reduce-scatter.4.cloned.1.call-start = ((), (), s32[]{:S(2)}) async-start(), calls=%async_computation.7 | async-start | bytes 10616832 | tf_op jit(solution)/shard_map/reduce_scatter | solution.py:730
  128.2 15.4 %collective-permute-start.3 = (bf16[2,176,768]{2,1,0:T(8,128)(2,1)}, bf16[2,176,768]{2,1,0:T(8,128)(2,1)S(1)}, u32[]{:S(2)}, u32[]{:S(2)}) collective-permute-start(bf16[2,176,768]{2,1,0:T(8,128)(2,1)} %get-tuple-element.87), channel_id=1, source_target_pairs={{0,8},{8,0},{16,24},{24,16},{1,9},{9,1},{17,25},{25,17},{2,10},{10... | collective-permute-start | bytes 1622024 | tf_op jit(solution)/shard_map/ppermute | solution.py:675
  129.6 26.0 %collective-permute-start.4 = (bf16[2,176,768]{2,1,0:T(8,128)(2,1)}, bf16[2,176,768]{2,1,0:T(8,128)(2,1)S(1)}, u32[]{:S(2)}, u32[]{:S(2)}) collective-permute-start(bf16[2,176,768]{2,1,0:T(8,128)(2,1)} %get-tuple-element.88), channel_id=1, source_target_pairs={{0,16},{8,24},{16,0},{24,8},{1,17},{9,25},{17,1},{25,9},{2,18},{10... | collective-permute-start | bytes 1622024 | tf_op jit(solution)/shard_map/ppermute | solution.py:675
  131.0 24.5 %collective-permute-start.5 = (bf16[2,176,768]{2,1,0:T(8,128)(2,1)}, bf16[2,176,768]{2,1,0:T(8,128)(2,1)S(1)}, u32[]{:S(2)}, u32[]{:S(2)}) collective-permute-start(bf16[2,176,768]{2,1,0:T(8,128)(2,1)} %get-tuple-element.89), channel_id=1, source_target_pairs={{0,24},{8,16},{16,8},{24,0},{1,25},{9,17},{17,9},{25,1},{2,26},{10... | collective-permute-start | bytes 1622024 | tf_op jit(solution)/shard_map/ppermute | solution.py:675
  143.6 30.3 %copy-start.15 = (bf16[2,176,768]{2,1,0:T(8,128)(2,1)}, bf16[2,176,768]{2,1,0:T(8,128)(2,1)S(1)}, u32[]{:S(2)}) copy-start(bf16[2,176,768]{2,1,0:T(8,128)(2,1)S(1)} %collective-permute-done.3.refs_1_) | copy-start | bytes 1622020
  155.5 18.4 %copy-start.18 = (bf16[2,176,768]{2,1,0:T(8,128)(2,1)}, bf16[2,176,768]{2,1,0:T(8,128)(2,1)S(1)}, u32[]{:S(2)}) copy-start(bf16[2,176,768]{2,1,0:T(8,128)(2,1)S(1)} %collective-permute-done.4.refs_2_) | copy-start | bytes 1622020
  155.5 18.4 %copy-start.21 = (bf16[2,176,768]{2,1,0:T(8,128)(2,1)}, bf16[2,176,768]{2,1,0:T(8,128)(2,1)S(1)}, u32[]{:S(2)}) copy-start(bf16[2,176,768]{2,1,0:T(8,128)(2,1)S(1)} %collective-permute-done.5.refs_3_) | copy-start | bytes 1622020
  204.7 264.0 %reduce-scatter.6.cloned.1.call-start = ((), (), s32[]{:S(2)}) async-start(), calls=%async_computation.8 | async-start | bytes 10616832 | tf_op jit(solution)/shard_map/reduce_scatter | solution.py:730
  205.6 15.1 %collective-permute-start = (bf16[2,176,768]{2,1,0:T(8,128)(2,1)S(1)}, bf16[2,176,768]{2,1,0:T(8,128)(2,1)S(1)}, u32[]{:S(2)}, u32[]{:S(2)}) collective-permute-start(bf16[2,176,768]{2,1,0:T(8,128)(2,1)S(1)} %copy-done.9), channel_id=1, source_target_pairs={{0,8},{8,0},{16,24},{24,16},{1,9},{9,1},{17,25},{25,17},{2,10},{10... | collective-permute-start | bytes 1622024 | tf_op jit(solution)/shard_map/ppermute | solution.py:675
  207.1 26.7 %collective-permute-start.1 = (bf16[2,176,768]{2,1,0:T(8,128)(2,1)S(1)}, bf16[2,176,768]{2,1,0:T(8,128)(2,1)S(1)}, u32[]{:S(2)}, u32[]{:S(2)}) collective-permute-start(bf16[2,176,768]{2,1,0:T(8,128)(2,1)S(1)} %copy-done.8), channel_id=1, source_target_pairs={{0,16},{8,24},{16,0},{24,8},{1,17},{9,25},{17,1},{25,9},{2,18},{10... | collective-permute-start | bytes 1622024 | tf_op jit(solution)/shard_map/ppermute | solution.py:675
  208.6 25.3 %collective-permute-start.2 = (bf16[2,176,768]{2,1,0:T(8,128)(2,1)S(1)}, bf16[2,176,768]{2,1,0:T(8,128)(2,1)S(1)}, u32[]{:S(2)}, u32[]{:S(2)}) collective-permute-start(bf16[2,176,768]{2,1,0:T(8,128)(2,1)S(1)} %copy-done.7), channel_id=1, source_target_pairs={{0,24},{8,16},{16,8},{24,0},{1,25},{9,17},{17,9},{25,1},{2,26},{10... | collective-permute-start | bytes 1622024 | tf_op jit(solution)/shard_map/ppermute | solution.py:675
  209.1 34.9 %collective-permute-start.6 = (bf16[2,176,768]{2,1,0:T(8,128)(2,1)}, bf16[2,176,768]{2,1,0:T(8,128)(2,1)S(1)}, u32[]{:S(2)}, u32[]{:S(2)}) collective-permute-start(bf16[2,176,768]{2,1,0:T(8,128)(2,1)} %get-tuple-element.95), channel_id=1, source_target_pairs={{0,8},{8,0},{16,24},{24,16},{1,9},{9,1},{17,25},{25,17},{2,10},{10... | collective-permute-start | bytes 1622024 | tf_op jit(solution)/shard_map/ppermute | solution.py:675
  210.6 45.4 %collective-permute-start.7 = (bf16[2,176,768]{2,1,0:T(8,128)(2,1)}, bf16[2,176,768]{2,1,0:T(8,128)(2,1)S(1)}, u32[]{:S(2)}, u32[]{:S(2)}) collective-permute-start(bf16[2,176,768]{2,1,0:T(8,128)(2,1)} %get-tuple-element.96), channel_id=1, source_target_pairs={{0,16},{8,24},{16,0},{24,8},{1,17},{9,25},{17,1},{25,9},{2,18},{10... | collective-permute-start | bytes 1622024 | tf_op jit(solution)/shard_map/ppermute | solution.py:675
  220.8 35.2 %copy-start.11 = (bf16[2,176,768]{2,1,0:T(8,128)(2,1)}, bf16[2,176,768]{2,1,0:T(8,128)(2,1)S(1)}, u32[]{:S(2)}) copy-start(bf16[2,176,768]{2,1,0:T(8,128)(2,1)S(1)} %collective-permute-done.refs_1_) | copy-start | bytes 1622020
  220.8 35.2 %collective-permute-start.8 = (bf16[2,176,768]{2,1,0:T(8,128)(2,1)S(1)}, bf16[2,176,768]{2,1,0:T(8,128)(2,1)S(1)}, u32[]{:S(2)}, u32[]{:S(2)}) collective-permute-start(bf16[2,176,768]{2,1,0:T(8,128)(2,1)S(1)} %copy-done.10), channel_id=1, source_target_pairs={{0,24},{8,16},{16,8},{24,0},{1,25},{9,17},{17,9},{25,1},{2,26},{10... | collective-permute-start | bytes 1622024 | tf_op jit(solution)/shard_map/ppermute | solution.py:675
  233.9 22.2 %copy-start.12 = (bf16[2,176,768]{2,1,0:T(8,128)(2,1)}, bf16[2,176,768]{2,1,0:T(8,128)(2,1)S(1)}, u32[]{:S(2)}) copy-start(bf16[2,176,768]{2,1,0:T(8,128)(2,1)S(1)} %collective-permute-done.1.refs_2_) | copy-start | bytes 1622020
  233.9 22.2 %copy-start.13 = (bf16[2,176,768]{2,1,0:T(8,128)(2,1)}, bf16[2,176,768]{2,1,0:T(8,128)(2,1)S(1)}, u32[]{:S(2)}) copy-start(bf16[2,176,768]{2,1,0:T(8,128)(2,1)S(1)} %collective-permute-done.2.refs_3_) | copy-start | bytes 1622020
  244.0 51.0 %copy-start.4 = (bf16[2,176,768]{2,1,0:T(8,128)(2,1)}, bf16[2,176,768]{2,1,0:T(8,128)(2,1)S(1)}, u32[]{:S(2)}) copy-start(bf16[2,176,768]{2,1,0:T(8,128)(2,1)S(1)} %collective-permute-done.6.refs_1_) | copy-start | bytes 1622020
  256.0 39.0 %copy-start.5 = (bf16[2,176,768]{2,1,0:T(8,128)(2,1)}, bf16[2,176,768]{2,1,0:T(8,128)(2,1)S(1)}, u32[]{:S(2)}) copy-start(bf16[2,176,768]{2,1,0:T(8,128)(2,1)S(1)} %collective-permute-done.7.refs_2_) | copy-start | bytes 1622020
  256.1 39.0 %copy-start.6 = (bf16[2,176,768]{2,1,0:T(8,128)(2,1)}, bf16[2,176,768]{2,1,0:T(8,128)(2,1)S(1)}, u32[]{:S(2)}) copy-start(bf16[2,176,768]{2,1,0:T(8,128)(2,1)S(1)} %collective-permute-done.8.refs_3_) | copy-start | bytes 1622020
  295.1 205.0 %reduce-scatter.8.cloned.1.call-start = ((), (), s32[]{:S(2)}) async-start(), calls=%async_computation.9 | async-start | bytes 1548288 | tf_op jit(solution)/shard_map/reduce_scatter | solution.py:795
  296.1 15.1 %collective-permute-start.9 = (bf16[2,176,768]{2,1,0:T(8,128)(2,1)S(1)}, bf16[2,176,768]{2,1,0:T(8,128)(2,1)S(1)}, u32[]{:S(2)}, u32[]{:S(2)}) collective-permute-start(bf16[2,176,768]{2,1,0:T(8,128)(2,1)S(1)} %copy-done.22), channel_id=1, source_target_pairs={{0,8},{8,0},{16,24},{24,16},{1,9},{9,1},{17,25},{25,17},{2,10},{10... | collective-permute-start | bytes 1622024 | tf_op jit(solution)/shard_map/ppermute | solution.py:675
  297.6 25.7 %collective-permute-start.10 = (bf16[2,176,768]{2,1,0:T(8,128)(2,1)S(1)}, bf16[2,176,768]{2,1,0:T(8,128)(2,1)S(1)}, u32[]{:S(2)}, u32[]{:S(2)}) collective-permute-start(bf16[2,176,768]{2,1,0:T(8,128)(2,1)S(1)} %copy-done.20), channel_id=1, source_target_pairs={{0,16},{8,24},{16,0},{24,8},{1,17},{9,25},{17,1},{25,9},{2,18},{10... | collective-permute-start | bytes 1622024 | tf_op jit(solution)/shard_map/ppermute | solution.py:675
  299.1 24.2 %collective-permute-start.11 = (bf16[2,176,768]{2,1,0:T(8,128)(2,1)S(1)}, bf16[2,176,768]{2,1,0:T(8,128)(2,1)S(1)}, u32[]{:S(2)}, u32[]{:S(2)}) collective-permute-start(bf16[2,176,768]{2,1,0:T(8,128)(2,1)S(1)} %copy-done.17), channel_id=1, source_target_pairs={{0,24},{8,16},{16,8},{24,0},{1,25},{9,17},{17,9},{25,1},{2,26},{10... | collective-permute-start | bytes 1622024 | tf_op jit(solution)/shard_map/ppermute | solution.py:675
  416.5 31.2 %collective-permute-start.14 = (bf16[2,384,896]{2,1,0:T(8,128)(2,1)S(1)}, bf16[2,384,896]{2,1,0:T(8,128)(2,1)S(1)}, u32[]{:S(2)}, u32[]{:S(2)}) collective-permute-start(bf16[2,384,896]{2,1,0:T(8,128)(2,1)S(1)} %slice.66), channel_id=1, source_target_pairs={{0,16},{8,24},{16,0},{24,8},{1,17},{9,25},{17,1},{25,9},{2,18},{10... | collective-permute-start | bytes 4128776 | tf_op jit(solution)/shard_map/ppermute | solution.py:783
  420.2 31.8 %collective-permute-start.12 = (bf16[2,384,896]{2,1,0:T(8,128)(2,1)S(1)}, bf16[2,384,896]{2,1,0:T(8,128)(2,1)S(1)}, u32[]{:S(2)}, u32[]{:S(2)}) collective-permute-start(bf16[2,384,896]{2,1,0:T(8,128)(2,1)S(1)} %slice.62), channel_id=1, source_target_pairs={{0,8},{8,0},{16,24},{24,16},{1,9},{9,1},{17,25},{25,17},{2,10},{10... | collective-permute-start | bytes 4128776 | tf_op jit(solution)/shard_map/ppermute | solution.py:783
  449.5 16.5 %collective-permute-start.15 = (bf16[384,896]{1,0:T(8,128)(2,1)S(1)}, bf16[384,896]{1,0:T(8,128)(2,1)S(1)}, u32[]{:S(2)}, u32[]{:S(2)}) collective-permute-start(bf16[384,896]{1,0:T(8,128)(2,1)S(1)} %slice_bitcast_fusion), channel_id=1, source_target_pairs={{0,8},{8,0},{16,24},{24,16},{1,9},{9,1},{17,25},{25,17},{2,10},{10... | collective-permute-start | bytes 2064392 | tf_op jit(solution)/shard_map/ppermute | solution.py:783
  452.5 14.9 %collective-permute-start.13 = (bf16[384,896]{1,0:T(8,128)(2,1)S(1)}, bf16[384,896]{1,0:T(8,128)(2,1)S(1)}, u32[]{:S(2)}, u32[]{:S(2)}) collective-permute-start(bf16[384,896]{1,0:T(8,128)(2,1)S(1)} %slice_bitcast_fusion.2), channel_id=1, source_target_pairs={{0,16},{8,24},{16,0},{24,8},{1,17},{9,25},{17,1},{25,9},{2,18},{10... | collective-permute-start | bytes 2064392 | tf_op jit(solution)/shard_map/ppermute | solution.py:783
  (14 other events, 54.1 us)
Sparse Core Ops, SparseCore 0:
  12.2 45.7 all-gather.5
  59.7 21.5 all-gather.7
  83.5 90.3 all-gather.9
  175.4 89.1 all-gather.11
  266.7 97.8 reduce-scatter.3
  366.8 97.8 reduce-scatter.5
  468.8 31.2 reduce-scatter.7

commit v4 on v3

--- a/solution.py
+++ b/solution.py
@@ -71,12 +71,15 @@
     return high, low
 
 
-def pack_kernel(q, k, v, gain1, gain2, router, mix, vectors, out, scratch):
+def pack_kernel(me, q, k, v, o, gain1, gain2, router, mix, vectors, out, scratch):
     rows, width = q.shape
-    out[:, 0:width] = q[...]
-    out[:, width : 2 * width] = k[...]
-    out[:, 2 * width : 3 * width] = v[...]
-    base = 3 * width
+    for j, weight in enumerate((q, k, v, o)):
+
+        @pl.when(me[0] == j)
+        def _():
+            out[:, 0:width] = weight[...]
+
+    base = width
     out[:, base : base + LANES] = jnp.zeros((rows, LANES), BF16)
     scratch[...] = jnp.zeros_like(scratch)
     scratch[0:1, 0:rows] = gain1[...].astype(F32)
@@ -122,7 +125,7 @@
     )
 
 
-def project_kernel(x, wq, wk, wv, small, cosine, sine, q_out, k_out, v_out, n_out, small_t):
+def project_kernel(me, x, wq, wk, wv, small, cosine, sine, q_out, k_out, v_out, n_out, small_t):
     @pl.when(pl.program_id(0) == 0)
     def _():
         small_t[...] = small[...].astype(F32).T
@@ -135,18 +138,18 @@
     cos = cosine[...]
     sin = sine[...]
     for weight, out, factor in ((wq, q_out, HEAD_DIM**-0.5), (wk, k_out, None)):
-        lin = mm(normed, weight[...])
+        lin = mm(normed, weight[0])
         for c in range(width // LANES):
             part = lin[:, c * LANES : (c + 1) * LANES]
             turned = part * cos + half_swap(part) * sin
             if factor is not None:
                 turned = turned * factor
             out[:, c * LANES : (c + 1) * LANES] = turned.astype(BF16)
-    v_out[...] = mm(normed, wv[...]).astype(BF16)
+    v_out[...] = mm(normed, wv[0]).astype(BF16)
 
 
 def attend_kernel(
-    prefix, q, k, v, x, wo, small, small_t, prev, routes,
+    me, prefix, q, k, v, x, wo, small, small_t, prev, routes,
     mix_out, lse_out, res_out, n_out, tok_out, bias, mixed, lse,
 ):
     block, width = q.shape
@@ -179,7 +182,7 @@
     lax.fori_loop(0, width // LANES, one_pair, 0)
     mix_out[...] = mixed[...]
     lse_out[...] = lse[...].T[0:16, :]
-    residual = x[...].astype(F32) + mm(mixed[...], wo[...])
+    residual = x[...].astype(F32) + mm(mixed[...], wo[0])
     res_out[...] = residual
     scale = lax.rsqrt(jnp.mean(residual * residual, axis=1, keepdims=True) + EPS)
     normed = (residual * scale * small_t[17:18, :]).astype(BF16)
@@ -441,7 +444,7 @@
     attn_g = resg.astype(BF16)
     am = mix[...]
     wo_acc[...] += mm_tn(am, attn_g)
-    heads_g = mm_nt(attn_g, wo[...]).astype(BF16)
+    heads_g = mm_nt(attn_g, wo[0]).astype(BF16)
     headg_out[...] = heads_g
     product = heads_g.astype(F32) * am.astype(F32)
     p_high, p_low = split_high_low(product)
@@ -532,7 +535,7 @@
 
     rows = x[...].astype(F32)
     scale = lax.rsqrt(jnp.mean(rows * rows, axis=1, keepdims=True) + EPS)
-    normed_g = mm_nt(dq[...], wq[...]) + mm_nt(dk[...], wk[...]) + mm_nt(dv[...], wv[...])
+    normed_g = mm_nt(dq[...], wq[0]) + mm_nt(dk[...], wk[0]) + mm_nt(dv[...], wv[0])
     n_low = normed[...]
     for index, part in enumerate((dq, dk, dv)):
         acc[:, index * width : (index + 1) * width] += mm_tn(n_low, part[...])
@@ -583,25 +586,37 @@
     tiles = ff // TILE
     down_rows = down_weight.shape[1]
     me = lax.axis_index("expert").astype(jnp.int32).reshape(1)
-    packed_width = 3 * width + LANES
+    packed_width = width + LANES
     cosine, sine = (jnp.asarray(t) for t in rotary_tables())
     struct = jax.ShapeDtypeStruct
 
     packed = call(
         pack_kernel, "pack", (1,),
-        [whole((shard_rows, width))] * 3
+        [whole((shard_rows, width))] * 4
         + [whole((1, shard_rows))] * 2
         + [whole((shard_rows, kinds)), whole((shard_rows, 4)), whole((2, shard_rows))],
         whole((shard_rows, packed_width)),
         struct((shard_rows, packed_width), BF16),
         scratch=[pltpu.VMEM((8, LANES), F32)],
-        traffic=1 << 20,
+        traffic=1 << 20, prefetch=1,
     )(
-        query_weight, key_weight, value_weight, first_gain[None], second_gain[None],
+        me, query_weight, key_weight, value_weight, output_weight, first_gain[None], second_gain[None],
         router_weight, constant_mix, constant_vectors,
     )
-    qkv_full = lax.all_gather(packed, "shard", axis=0, tiled=True)
-    output_full = lax.all_gather(output_weight, "shard", axis=0, tiled=True)
+
+    def send(part, k):
+        return lax.ppermute(part, "expert", [(i, i ^ k) for i in range(owners)])
+
+    half = width // 2
+    own = lax.all_gather(packed, "shard", axis=0, tiled=True)
+    top, low = own[None, :half, :width], own[None, half:, :width]
+    top = jnp.concatenate([top, send(top, 1)])
+    low = jnp.concatenate([low, send(low, 2)])
+    top_in, low_in = send(top, 2), send(low, 1)
+    weights = jnp.concatenate([
+        jnp.concatenate([top, top_in]),
+        jnp.stack([low[0], low_in[0], low[1], low_in[1]]),
+    ], axis=1)
     aligned = shard_rows % 16 == 0 and down_rows == TILE
     expert_rows = 2 * tiles * shard_rows + width // TILE * down_rows
 
@@ -643,9 +658,11 @@
 
     steps = count // BLOCK
     weight_block = [
-        pl.BlockSpec((width, width), lambda i, *rest, j=j: (0, j)) for j in range(3)
+        pl.BlockSpec((1, width, width), lambda i, me, *rest, j=j: (me[0] ^ j, 0, 0))
+        for j in range(4)
     ]
-    small_block = pl.BlockSpec((width, LANES), lambda i, *rest: (0, 3 * width // LANES))
+    output_block = weight_block.pop()
+    small_block = pl.BlockSpec((width, LANES), lambda i, *rest: (0, width // LANES))
     wide = rows_of(BLOCK, width)
     table = rows_of(BLOCK, LANES)
     act = struct((count, width), BF16)
@@ -654,20 +671,20 @@
         [wide] + weight_block + [small_block, table, table],
         [wide] * 4 + [whole((LANES, width))],
         [act] * 4 + [struct((LANES, width), F32)],
-        flops=6 * count * width * width, traffic=12 << 20,
-    )(tokens, qkv_full, qkv_full, qkv_full, qkv_full, cosine, sine)
+        flops=6 * count * width * width, traffic=12 << 20, prefetch=1,
+    )(me, tokens, weights, weights, weights, own, cosine, sine)
 
     attn_mix, lse, residual, normed_two, tok = call(
         attend_kernel, "attend", (steps,),
-        [wide, whole((count, width)), whole((count, width)), wide, whole((width, width)),
+        [wide, whole((count, width)), whole((count, width)), wide, output_block,
          small_block, whole((LANES, width)), rows_of(BLOCK, kinds), rows_of(BLOCK, TOP)],
         [wide, pl.BlockSpec((16, BLOCK), lambda i, *rest: (0, i)), wide, wide, table],
         [act, struct((16, count), F32), struct((count, width), F32), act,
          struct((count, LANES), F32)],
         scratch=[pltpu.VMEM((BLOCK, count), F32), pltpu.VMEM((BLOCK, width), BF16),
                  pltpu.VMEM((BLOCK, LANES), F32)],
-        flops=30 << 30, traffic=16 << 20, trans=HEADS * count * count, prefetch=1,
-    )(prefix, queries, keys, values, tokens, output_full, qkv_full, small_t,
+        flops=30 << 30, traffic=16 << 20, trans=HEADS * count * count, prefetch=2,
+    )(me, prefix, queries, keys, values, tokens, weights, own, small_t,
       previous_logits, routes)
 
     def exchange(parts):
@@ -696,7 +713,7 @@
     chunks, chunk_rows = (shards, shard_rows) if aligned else (1, width)
     local = owners * stride
 
-    def run_expert(l, rows):
+    def run_expert(l, rows, after):
         gate_up, down = expert_full[l]
         weights = [
             pl.BlockSpec((chunks, chunk_rows, TILE), lambda f, j=j: (0, j // 2 * tiles + 2 * f + j % 2, 0))
@@ -727,24 +744,25 @@
             grad = jnp.concatenate(
                 [gate_up_g.reshape(shards, -1, TILE), down_g.reshape(shards, -1, TILE)], axis=1
             )
+        grad, after = lax.optimization_barrier((grad, after))
         total = lax.psum_scatter(
             grad.reshape(shards * expert_rows, TILE), "shard", scatter_dimension=0, tiled=True
         )
-        return exchange(outs[:owners]), total
+        return outs[:owners], total, after
 
     returned = []
     expert_sums = []
     for l in range(local_experts):
         rows, ahead = lax.optimization_barrier((received[l], returned or dispatched[-1]))
         returned = ahead if returned else returned
-        back, total = run_expert(l, rows)
-        returned = returned + back
+        back, total, received[l + 1 :] = run_expert(l, rows, received[l + 1 :])
+        returned = returned + exchange(back)
         expert_sums.append(total)
 
     mixed, previous_grad, residual_grad, heads_grad, delta, output_grad, small_grad = call(
         functools.partial(combine_kernel, experts, owners, local_experts), "combine", (steps,),
         [pair] * len(returned)
-        + [wide, wide, wide, table, rows_of(BLOCK, TOP), table, wide, whole((width, width)),
+        + [wide, wide, wide, table, rows_of(BLOCK, TOP), table, wide, output_block,
            whole((LANES, width))],
         [wide, rows_of(BLOCK, kinds), wide, wide, pl.BlockSpec((16, BLOCK), lambda i, *rest: (0, i)),
          whole((width, width)), whole((width, LANES))],
@@ -755,7 +773,7 @@
         + [pltpu.VMEM((local_experts, local, width), BF16)] * 2,
         flops=6 * count * 2 * local * width + 4 * count * width * width, traffic=24 << 20, prefetch=1,
     )(me, *returned, residual, normed_two, cotangent, tok,
-      routes, dest_col, attn_mix, output_full, small_t)
+      routes, dest_col, attn_mix, weights, small_t)
 
     pair_block = pl.BlockSpec((count, LANES), lambda i, *rest: (0, i))
     dq, dk, dv = call(
@@ -776,16 +794,12 @@
         [struct((count, width), F32), struct((owners, width, width + LANES), BF16)],
         scratch=[pltpu.VMEM((width, 3 * width), F32), pltpu.VMEM((8, width), F32)],
         flops=12 * count * width * width, traffic=24 << 20, prefetch=1,
-    )(me, tokens, normed_one, dq, dk, dv, residual_grad, qkv_full, qkv_full, qkv_full, small_t,
+    )(me, tokens, normed_one, dq, dk, dv, residual_grad, weights, weights, weights, small_t,
       small_grad, output_grad)
-
-    def send(part, k):
-        return lax.ppermute(part, "expert", [(i, i ^ k) for i in range(owners)])
 
     def add(a, b):
         return (a.astype(F32) + b.astype(F32)).astype(BF16)
 
-    half = width // 2
     top, low = dense_grad[:, :half], dense_grad[:, half:]
     top_in, low_in = send(top[1::2], 1), send(low[2:], 2)
     top, low = add(top[0::2], top_in), add(low[:2], low_in)

time: 530 us -> 488 us (0.921)
  waiting for transfers between devices: 222 us -> 159 us
  starting transfers between devices: 19.8 us -> 28.7 us
    ppermute x12, waiting for transfers between devices: 81.2 us -> 48.2 us  [exchange(): lax.ppermute(part, 'expert', [(i, i ^ k) for i in range(owners)])]
    all_gather x2, waiting for transfers between devices: 26.9 us -> 0.02 us  [gather_expert(): full = lax.all_gather(one, 'shard', axis=0, tiled=True)]
    all_gather x2 -> x1, waiting for transfers between devices: 44.3 us -> 21.9 us  [body(): own = lax.all_gather(packed, 'shard', axis=0, tiled=True)]
    ppermute x4 -> x8, waiting for transfers between devices: 42.6 us -> 57.5 us  [send(): return lax.ppermute(part, 'expert', [(i, i ^ k) for i in range(owners)])]
    ppermute x4 -> x8, starting transfers between devices: 3.72 us -> 14.9 us  [send(): return lax.ppermute(part, 'expert', [(i, i ^ k) for i in range(owners)])]
    unnamed x52 -> x48, local copies, waits for them, and re-layouts: 8.73 us -> 10.8 us
  transfers between devices with their start and end apart: 23 -> 26, of which waited for: 17 -> 17; matrix products, arithmetic and copies ran while one was open for 2% -> 4% of each run, Pallas kernels for 44% -> 49%
where the time goes in v4:
time: 488 us; the launch traced here: 479 us
  Pallas kernels  235 us (48%)
  waiting for transfers between devices  159 us (33%)
  starting transfers between devices  28.7 us (6%)
  local copies, waits for them, and re-layouts  21.5 us (4%)
  between operations  15.5 us (3%)
  blocking collectives  11.3 us (2%)
  other arithmetic  8.61 us (2%)
    pallas_call x2, Pallas kernels, run_expert(): call(functools.partial(expert_kernel, owners, aligned), 'expert', (tiles...  62.1 us
    ppermute x8, waiting for transfers between devices, send(): return lax.ppermute(part, 'expert', [(i, i ^ k) for i in range(owners)])  57.5 us
    ppermute x12, waiting for transfers between devices, exchange(): lax.ppermute(part, 'expert', [(i, i ^ k) for i in range(owners)])  48.2 us
    pallas_call x1, Pallas kernels, body(): call(attend_back_kernel, 'attend_back', (width // LANES,), [pair_block] *...  46.4 us
    pallas_call x1, Pallas kernels, body(): call(attend_kernel, 'attend', (steps,), [wide, whole((count, width)), who...  39.2 us
    reduce_scatter x1, waiting for transfers between devices, body(): lax.psum_scatter(quarter, 'shard', scatter_dimension=0, tiled=True)  29.5 us
    pallas_call x1, Pallas kernels, body(): call(functools.partial(combine_kernel, experts, owners, local_experts), '...  27.6 us
    all_gather x1, waiting for transfers between devices, body(): own = lax.all_gather(packed, 'shard', axis=0, tiled=True)  21.9 us
  transfers between devices with their start and end apart: 26, of which 17 were waited for; matrix products, arithmetic and copies ran while one was open for 4% of the time, Pallas kernels for 49%

profile of v4, /device:TPU:0, one launch (start us, length us, event | category | flops | bytes accessed | tf_op | source)
XLA Modules:
  0.0 478.8 jit_solution(11760380407952213056)
XLA Ops:
  10.0 2.0 pack.1
  12.1 2.3 pack_expert.2
  14.5 2.3 pack_expert.3
  16.9 21.9 %all-gather.5.cloned.1.call-done.small = bf16[768,896]{1,0:T(8,128)(2,1)} async-done(((bf16[96,896]{1,0:T(8,128)(2,1)}), bf16[768,896]{1,0:T(8,128)(2,1)}) %all-gather.5.cloned.1.call-update) | async-done | bytes 1376272 | tf_op jit(solution)/shard_map/all_gather | solution.py:611
  43.1 12.5 %collective-permute-done.2 = bf16[1,384,768]{2,1,0:T(8,128)(2,1)S(1)} collective-permute-done((bf16[1,384,768]{2,1,0:T(8,128)(2,1)S(1)}, bf16[1,384,768]{2,1,0:T(8,128)(2,1)S(1)}, u32[]{:S(2)}, u32[]{:S(2)}) %collective-permute-start.2) | collective-permute-done | bytes 589856 | tf_op jit(solution)/shard_map/ppermute | solution.py:608
  65.5 6.8 %slots.1 = (s32[1024,128]{1,0:T(8,128)}, s32[8,1024]{1,0:T(8,128)}) custom-call(s32[1024,2]{1,0:T(8,128)} %copy.48.routes.refs_12_, s32[1,1024]{1,0:T(1,128)} %order_row.1, s32[1024,1]{1,0:T(8,128)} %copy.50.order_col), custom_call_target="tpu_custom_call" | custom-call | flops 805306368 | bytes 1048576 | tf_op jit(solution)/shard_map/slots/pallas_call | solution.py:651
  72.3 12.1 %collective-permute-done.3 = bf16[2,384,768]{2,1,0:T(8,128)(2,1)} collective-permute-done((bf16[2,384,768]{2,1,0:T(8,128)(2,1)}, bf16[2,384,768]{2,1,0:T(8,128)(2,1)}, u32[]{:S(2)}, u32[]{:S(2)}) %collective-permute-start.3) | collective-permute-done | bytes 1179680 | tf_op jit(solution)/shard_map/ppermute | solution.py:608
  86.6 2.8 maximum_maximum_fusion.wq.wk.wv.wo.refs_15_
  89.4 8.7 %project.1 = (bf16[1024,768]{1,0:T(8,128)(2,1)}, bf16[1024,768]{1,0:T(8,128)(2,1)}, bf16[1024,768]{1,0:T(8,128)(2,1)}, bf16[1024,768]{1,0:T(8,128)(2,1)}, f32[128,768]{1,0:T(8,128)}) custom-call(s32[1]{0:T(128)} %bitcast.me, bf16[1024,768]{1,0:T(8,128)(2,1)} %x.5, bf16[4,768,768]{2,1,0:T(8,128)(2,1)} %maximum_maximum_fusion.wq.wk.wv.wo.refs_15_, ...), custom_call_target="tpu_custom_call" | custom-call | flops 3623878656 | bytes 12582912 | tf_op jit(solution)/shard_map/project/pallas_call | solution.py:669
  98.1 39.2 %attend.1 = (bf16[1024,768]{1,0:T(8,128)(2,1)}, f32[16,1024]{1,0:T(8,128)}, f32[1024,768]{1,0:T(8,128)}, bf16[1024,768]{1,0:T(8,128)(2,1)}, f32[1024,128]{1,0:T(8,128)}) custom-call(s32[1]{0:T(128)} %bitcast.me, s32[1]{0:T(128)S(6)} %copy.57.prefix, bf16[1024,768]{1,0:T(8,128)(2,1)} %get-tuple-element.80.q, bf16[1024,768]{1,0:T(8,128)(2,1)} %get-tuple-element.81.k, ...), custom_call_target="tpu_custom_call" | custom-call | flops 32212254720 | bytes 16777216 | tf_op jit(solution)/shard_map/attend/pallas_call | solution.py:677
  137.3 8.5 %dispatch.2 = (bf16[2,176,768]{2,1,0:T(8,128)(2,1)}, bf16[2,176,768]{2,1,0:T(8,128)(2,1)}, bf16[2,176,768]{2,1,0:T(8,128)(2,1)}, bf16[2,176,768]{2,1,0:T(8,128)(2,1)}) custom-call(s32[1]{0:T(128)} %bitcast.me, bf16[1024,768]{1,0:T(8,128)(2,1)} %get-tuple-element.84.normed.refs_9_, bf16[1024,768]{1,0:T(8,128)(2,1)} %refs_10_.1, ...), custom_call_target="tpu_custom_call" | custom-call | flops 2214592512 | bytes 6291456 | tf_op jit(solution)/shard_map/dispatch/pallas_call | solution.py:700
  149.3 7.9 %dispatch.3 = (bf16[2,176,768]{2,1,0:T(8,128)(2,1)}, bf16[2,176,768]{2,1,0:T(8,128)(2,1)}, bf16[2,176,768]{2,1,0:T(8,128)(2,1)}, bf16[2,176,768]{2,1,0:T(8,128)(2,1)}) custom-call(s32[1]{0:T(128)} %bitcast.me, bf16[1024,768]{1,0:T(8,128)(2,1)} %get-tuple-element.84.normed.refs_9_, bf16[1024,768]{1,0:T(8,128)(2,1)} %refs_10_.1, ...), custom_call_target="tpu_custom_call" | custom-call | flops 2214592512 | bytes 6291456 | tf_op jit(solution)/shard_map/dispatch/pallas_call | solution.py:700
  159.0 2.1 collective-permute-done.4.refs_1_
  162.4 8.2 %collective-permute-done.5.refs_2_ = bf16[2,176,768]{2,1,0:T(8,128)(2,1)S(1)} collective-permute-done((bf16[2,176,768]{2,1,0:T(8,128)(2,1)}, bf16[2,176,768]{2,1,0:T(8,128)(2,1)S(1)}, u32[]{:S(2)}, u32[]{:S(2)}) %collective-permute-start.5) | collective-permute-done | bytes 540704 | tf_op jit(solution)/shard_map/ppermute | solution.py:692
  170.6 3.0 collective-permute-done.6.refs_3_
  174.5 30.7 %expert.2 = (bf16[2,176,768]{2,1,0:T(8,128)(2,1)}, bf16[2,176,768]{2,1,0:T(8,128)(2,1)}, bf16[2,176,768]{2,1,0:T(8,128)(2,1)}, bf16[2,176,768]{2,1,0:T(8,128)(2,1)}, bf16[8,2304,256]{2,1,0:T(8,128)(2,1)}) custom-call(bf16[2,176,768]{2,1,0:T(8,128)(2,1)} %get-tuple-element.95.refs_0_, bf16[2,176,768]{2,1,0:T(8,128)(2,1)} %copy-done.9, ...), custom_call_target="tpu_custom_call" | custom-call | flops 17716740096 | bytes 25165824 | tf_op jit(solution)/shard_map/expert/pallas_call | solution.py:729
  210.2 10.9 %collective-permute-done.10.refs_1_ = bf16[2,176,768]{2,1,0:T(8,128)(2,1)S(1)} collective-permute-done((bf16[2,176,768]{2,1,0:T(8,128)(2,1)S(1)}, bf16[2,176,768]{2,1,0:T(8,128)(2,1)S(1)}, u32[]{:S(2)}, u32[]{:S(2)}) %collective-permute-start.10) | collective-permute-done | bytes 540704 | tf_op jit(solution)/shard_map/ppermute | solution.py:692
  221.0 6.6 %collective-permute-done.11.refs_2_ = bf16[2,176,768]{2,1,0:T(8,128)(2,1)S(1)} collective-permute-done((bf16[2,176,768]{2,1,0:T(8,128)(2,1)S(1)}, bf16[2,176,768]{2,1,0:T(8,128)(2,1)S(1)}, u32[]{:S(2)}, u32[]{:S(2)}) %collective-permute-start.11) | collective-permute-done | bytes 540704 | tf_op jit(solution)/shard_map/ppermute | solution.py:692
  227.6 31.5 %expert.3 = (bf16[2,176,768]{2,1,0:T(8,128)(2,1)}, bf16[2,176,768]{2,1,0:T(8,128)(2,1)}, bf16[2,176,768]{2,1,0:T(8,128)(2,1)}, bf16[2,176,768]{2,1,0:T(8,128)(2,1)}, bf16[8,2304,256]{2,1,0:T(8,128)(2,1)}) custom-call(bf16[2,176,768]{2,1,0:T(8,128)(2,1)} %get-tuple-element.112.refs_0_, bf16[2,176,768]{2,1,0:T(8,128)(2,1)} %copy-done.3, ...), custom_call_target="tpu_custom_call" | custom-call | flops 17716740096 | bytes 25165824 | tf_op jit(solution)/shard_map/expert/pallas_call | solution.py:729
  263.7 10.3 %collective-permute-done.13.refs_5_ = bf16[2,176,768]{2,1,0:T(8,128)(2,1)S(1)} collective-permute-done((bf16[2,176,768]{2,1,0:T(8,128)(2,1)S(1)}, bf16[2,176,768]{2,1,0:T(8,128)(2,1)S(1)}, u32[]{:S(2)}, u32[]{:S(2)}) %collective-permute-start.13) | collective-permute-done | bytes 540704 | tf_op jit(solution)/shard_map/ppermute | solution.py:692
  274.0 7.1 %collective-permute-done.14.refs_6_ = bf16[2,176,768]{2,1,0:T(8,128)(2,1)S(1)} collective-permute-done((bf16[2,176,768]{2,1,0:T(8,128)(2,1)S(1)}, bf16[2,176,768]{2,1,0:T(8,128)(2,1)S(1)}, u32[]{:S(2)}, u32[]{:S(2)}) %collective-permute-start.14) | collective-permute-done | bytes 540704 | tf_op jit(solution)/shard_map/ppermute | solution.py:692
  282.0 27.6 %combine.1 = (bf16[1024,768]{1,0:T(8,128)(2,1)}, f32[1024,12]{1,0:T(8,128)}, f32[1024,768]{1,0:T(8,128)}, bf16[1024,768]{1,0:T(8,128)(2,1)}, f32[16,1024]{1,0:T(...) custom-call(s32[1]{0:T(128)} %bitcast.me, bf16[2,176,768]{2,1,0:T(8,128)(2,1)} %get-tuple-element.108.refs_0_, ...), custom_call_target="tpu_custom_call" | custom-call | flops 9059696640 | bytes 25165824 | tf_op jit(solution)/shard_map/combine/pallas_call | solution.py:762
  309.7 46.4 %attend_back.1 = (bf16[1024,768]{1,0:T(8,128)(2,1)}, bf16[1024,768]{1,0:T(8,128)(2,1)}, bf16[1024,768]{1,0:T(8,128)(2,1)}) custom-call(s32[1]{0:T(128)S(6)} %copy.57.prefix, bf16[1024,768]{1,0:T(8,128)(2,1)} %get-tuple-element.80.q, bf16[1024,768]{1,0:T(8,128)(2,1)} %get-tuple-element.81.k, bf16[1024,768]{1,0:T(8,128)(2,1)} %get-tuple-element.82.v, ...), custom_call_target="tpu_custom_call" | custom-call | flops 64424509440 | bytes 12582912 | tf_op jit(solution)/shard_map/attend_back/pallas_call | solution.py:779
  356.0 16.8 %project_back.1 = (f32[1024,768]{1,0:T(8,128)}, bf16[4,768,896]{2,1,0:T(8,128)(2,1)}) custom-call(s32[1]{0:T(128)} %bitcast.me, bf16[1024,768]{1,0:T(8,128)(2,1)} %x.5, bf16[1024,768]{1,0:T(8,128)(2,1)} %get-tuple-element.124.normed, bf16[1024,768]{1,0:T(8,128)(2,1)} %get-tuple-element.128.dq, bf16[1024,768]{1,0:T(8,128)(2,1)} %get-tuple-element.129.dk, ...), custom_call_target="tpu_custom_call" | custom-call | flops 7247757312 | bytes 25165824 | tf_op jit(solution)/shard_map/project_back/pallas_call | solution.py:790
  378.5 21.8 %collective-permute-done.18 = bf16[2,384,896]{2,1,0:T(8,128)(2,1)S(1)} collective-permute-done((bf16[2,384,896]{2,1,0:T(8,128)(2,1)S(1)}, bf16[2,384,896]{2,1,0:T(8,128)(2,1)S(1)}, u32[]{:S(2)}, u32[]{:S(2)}) %collective-permute-start.18) | collective-permute-done | bytes 1376288 | tf_op jit(solution)/shard_map/ppermute | solution.py:608
  402.0 3.4 collective-permute-start.19
  407.2 3.5 collective-permute-start.17
  410.7 5.9 %collective-permute-done.19 = bf16[384,896]{1,0:T(8,128)(2,1)S(1)} collective-permute-done((bf16[384,896]{1,0:T(8,128)(2,1)S(1)}, bf16[384,896]{1,0:T(8,128)(2,1)S(1)}, u32[]{:S(2)}, u32[]{:S(2)}) %collective-permute-start.19) | collective-permute-done | bytes 688160 | tf_op jit(solution)/shard_map/ppermute | solution.py:608
  416.8 2.8 collective-permute-done.17
  423.2 3.9 unpack.1
  427.1 29.5 %reduce-scatter.8.cloned.1.call-done = bf16[96,896]{1,0:T(8,128)(2,1)} async-done(((bf16[768,896]{1,0:T(8,128)(2,1)}), bf16[96,896]{1,0:T(8,128)(2,1)}) %reduce-scatter.8.cloned.1.call-update) | async-done | bytes 172048 | tf_op jit(solution)/shard_map/reduce_scatter | solution.py:809
  456.7 11.3 %all-gather = bf16[384,896]{1,0:T(8,128)(2,1)S(1)} all-gather(bf16[96,896]{1,0:T(8,128)(2,1)} %reduce-scatter.8.cloned.1.call-done), channel_id=2, replica_groups=mesh['expert'=4,'shard'=8] {'expert'}, dimensions={0}, use_global_device_ids=true | all-gather | bytes 860160 | tf_op jit(solution)/shard_map/all_gather | solution.py:810
  (112 shorter events, 53.0 us)
Async XLA Ops:
  7.2 31.6 %all-gather.5.cloned.1.call-start = ((), (), s32[]{:S(2)}) async-start(), calls=%async_computation.3 | async-start | bytes 1548288 | tf_op jit(solution)/shard_map/all_gather | solution.py:611
  12.1 161.6 %all-gather.7.cloned.1.call-start = ((), (), s32[]{:S(2)}) async-start(), calls=%async_computation.4 | async-start | bytes 10616832 | tf_op jit(solution)/shard_map/all_gather | solution.py:636
  14.5 213.2 %all-gather.9.cloned.1.call-start = ((), (), s32[]{:S(2)}) async-start(), calls=%async_computation.5 | async-start | bytes 10616832 | tf_op jit(solution)/shard_map/all_gather | solution.py:636
  16.9 404.2 %reduce-scatter.4.cloned.1.call-start = ((), (), s32[]{:S(2)}) async-start(), calls=%async_computation.6 | async-start | bytes 10616832 | tf_op jit(solution)/shard_map/reduce_scatter | solution.py:748
  40.1 15.5 %collective-permute-start.2 = (bf16[1,384,768]{2,1,0:T(8,128)(2,1)S(1)}, bf16[1,384,768]{2,1,0:T(8,128)(2,1)S(1)}, u32[]{:S(2)}, u32[]{:S(2)}) collective-permute-start(bf16[1,384,768]{2,1,0:T(8,128)(2,1)S(1)} %get-tuple-element.180), channel_id=1, source_target_pairs={{0,16},{8,24},{16,0},{24,8},{1,17},{9,25},{17,1},{25,9},{2,18},{10... | collective-permute-start | bytes 1769480 | tf_op jit(solution)/shard_map/ppermute | solution.py:608
  41.6 16.6 %collective-permute-start = (bf16[1,384,768]{2,1,0:T(8,128)(2,1)S(1)}, bf16[1,384,768]{2,1,0:T(8,128)(2,1)S(1)}, u32[]{:S(2)}, u32[]{:S(2)}) collective-permute-start(bf16[1,384,768]{2,1,0:T(8,128)(2,1)S(1)} %get-tuple-element.179), channel_id=1, source_target_pairs={{0,8},{8,0},{16,24},{24,16},{1,9},{9,1},{17,25},{25,17},{2,10},{10... | collective-permute-start | bytes 1769480 | tf_op jit(solution)/shard_map/ppermute | solution.py:608
  56.7 7.7 %copy-start.2 = (s32[1,1024]{1,0:T(1,128)S(1)}, s32[1,1024]{1,0:T(1,128)}, u32[]{:S(2)}) copy-start(s32[1,1024]{1,0:T(1,128)} %order_row.1) | copy-start | bytes 12292
  56.7 27.7 %collective-permute-start.3 = (bf16[2,384,768]{2,1,0:T(8,128)(2,1)}, bf16[2,384,768]{2,1,0:T(8,128)(2,1)}, u32[]{:S(2)}, u32[]{:S(2)}) collective-permute-start(bf16[2,384,768]{2,1,0:T(8,128)(2,1)} %pad_maximum_fusion.2), channel_id=1, source_target_pairs={{0,8},{8,0},{16,24},{24,16},{1,9},{9,1},{17,25},{25,17},{2,10},{10... | collective-permute-start | bytes 3538952 | tf_op jit(solution)/shard_map/ppermute | solution.py:608
  59.3 27.3 %collective-permute-start.1 = (bf16[2,384,768]{2,1,0:T(8,128)(2,1)}, bf16[2,384,768]{2,1,0:T(8,128)(2,1)S(1)}, u32[]{:S(2)}, u32[]{:S(2)}) collective-permute-start(bf16[2,384,768]{2,1,0:T(8,128)(2,1)} %pad_maximum_fusion.1), channel_id=1, source_target_pairs={{0,16},{8,24},{16,0},{24,8},{1,17},{9,25},{17,1},{25,9},{2,18},{10... | collective-permute-start | bytes 3538952 | tf_op jit(solution)/shard_map/ppermute | solution.py:608
  145.8 15.4 %collective-permute-start.4 = (bf16[2,176,768]{2,1,0:T(8,128)(2,1)}, bf16[2,176,768]{2,1,0:T(8,128)(2,1)S(1)}, u32[]{:S(2)}, u32[]{:S(2)}) collective-permute-start(bf16[2,176,768]{2,1,0:T(8,128)(2,1)} %get-tuple-element.88), channel_id=1, source_target_pairs={{0,8},{8,0},{16,24},{24,16},{1,9},{9,1},{17,25},{25,17},{2,10},{10... | collective-permute-start | bytes 1622024 | tf_op jit(solution)/shard_map/ppermute | solution.py:692
  146.1 24.5 %collective-permute-start.5 = (bf16[2,176,768]{2,1,0:T(8,128)(2,1)}, bf16[2,176,768]{2,1,0:T(8,128)(2,1)S(1)}, u32[]{:S(2)}, u32[]{:S(2)}) collective-permute-start(bf16[2,176,768]{2,1,0:T(8,128)(2,1)} %get-tuple-element.89), channel_id=1, source_target_pairs={{0,16},{8,24},{16,0},{24,8},{1,17},{9,25},{17,1},{25,9},{2,18},{10... | collective-permute-start | bytes 1622024 | tf_op jit(solution)/shard_map/ppermute | solution.py:692
  147.6 26.0 %collective-permute-start.6 = (bf16[2,176,768]{2,1,0:T(8,128)(2,1)}, bf16[2,176,768]{2,1,0:T(8,128)(2,1)S(1)}, u32[]{:S(2)}, u32[]{:S(2)}) collective-permute-start(bf16[2,176,768]{2,1,0:T(8,128)(2,1)} %get-tuple-element.90), channel_id=1, source_target_pairs={{0,24},{8,16},{16,8},{24,0},{1,25},{9,17},{17,9},{25,1},{2,26},{10... | collective-permute-start | bytes 1622024 | tf_op jit(solution)/shard_map/ppermute | solution.py:692
  157.1 48.0 %collective-permute-start.7 = (bf16[2,176,768]{2,1,0:T(8,128)(2,1)}, bf16[2,176,768]{2,1,0:T(8,128)(2,1)S(1)}, u32[]{:S(2)}, u32[]{:S(2)}) collective-permute-start(bf16[2,176,768]{2,1,0:T(8,128)(2,1)} %get-tuple-element.92), channel_id=1, source_target_pairs={{0,8},{8,0},{16,24},{24,16},{1,9},{9,1},{17,25},{25,17},{2,10},{10... | collective-permute-start | bytes 1622024 | tf_op jit(solution)/shard_map/ppermute | solution.py:692
  157.5 47.6 %collective-permute-start.8 = (bf16[2,176,768]{2,1,0:T(8,128)(2,1)}, bf16[2,176,768]{2,1,0:T(8,128)(2,1)S(1)}, u32[]{:S(2)}, u32[]{:S(2)}) collective-permute-start(bf16[2,176,768]{2,1,0:T(8,128)(2,1)} %get-tuple-element.93), channel_id=1, source_target_pairs={{0,16},{8,24},{16,0},{24,8},{1,17},{9,25},{17,1},{25,9},{2,18},{10... | collective-permute-start | bytes 1622024 | tf_op jit(solution)/shard_map/ppermute | solution.py:692
  161.1 12.5 %copy-start.9 = (bf16[2,176,768]{2,1,0:T(8,128)(2,1)}, bf16[2,176,768]{2,1,0:T(8,128)(2,1)S(1)}, u32[]{:S(2)}) copy-start(bf16[2,176,768]{2,1,0:T(8,128)(2,1)S(1)} %collective-permute-done.4.refs_1_) | copy-start | bytes 1622020
  161.1 44.0 %collective-permute-start.9 = (bf16[2,176,768]{2,1,0:T(8,128)(2,1)}, bf16[2,176,768]{2,1,0:T(8,128)(2,1)S(1)}, u32[]{:S(2)}, u32[]{:S(2)}) collective-permute-start(bf16[2,176,768]{2,1,0:T(8,128)(2,1)} %get-tuple-element.94), channel_id=1, source_target_pairs={{0,24},{8,16},{16,8},{24,0},{1,25},{9,17},{17,9},{25,1},{2,26},{10... | collective-permute-start | bytes 1622024 | tf_op jit(solution)/shard_map/ppermute | solution.py:692
  206.3 216.1 %reduce-scatter.6.cloned.1.call-start = ((), (), s32[]{:S(2)}) async-start(), calls=%async_computation.7 | async-start | bytes 10616832 | tf_op jit(solution)/shard_map/reduce_scatter | solution.py:748
  206.7 14.4 %collective-permute-start.10 = (bf16[2,176,768]{2,1,0:T(8,128)(2,1)S(1)}, bf16[2,176,768]{2,1,0:T(8,128)(2,1)S(1)}, u32[]{:S(2)}, u32[]{:S(2)}) collective-permute-start(bf16[2,176,768]{2,1,0:T(8,128)(2,1)S(1)} %copy-done.14), channel_id=1, source_target_pairs={{0,8},{8,0},{16,24},{24,16},{1,9},{9,1},{17,25},{25,17},{2,10},{10... | collective-permute-start | bytes 1622024 | tf_op jit(solution)/shard_map/ppermute | solution.py:692
  207.0 20.6 %collective-permute-start.11 = (bf16[2,176,768]{2,1,0:T(8,128)(2,1)S(1)}, bf16[2,176,768]{2,1,0:T(8,128)(2,1)S(1)}, u32[]{:S(2)}, u32[]{:S(2)}) collective-permute-start(bf16[2,176,768]{2,1,0:T(8,128)(2,1)S(1)} %copy-done.12), channel_id=1, source_target_pairs={{0,16},{8,24},{16,0},{24,8},{1,17},{9,25},{17,1},{25,9},{2,18},{10... | collective-permute-start | bytes 1622024 | tf_op jit(solution)/shard_map/ppermute | solution.py:692
  208.5 19.1 %collective-permute-start.12 = (bf16[2,176,768]{2,1,0:T(8,128)(2,1)S(1)}, bf16[2,176,768]{2,1,0:T(8,128)(2,1)S(1)}, u32[]{:S(2)}, u32[]{:S(2)}) collective-permute-start(bf16[2,176,768]{2,1,0:T(8,128)(2,1)S(1)} %copy-done.10), channel_id=1, source_target_pairs={{0,24},{8,16},{16,8},{24,0},{1,25},{9,17},{17,9},{25,1},{2,26},{10... | collective-permute-start | bytes 1622024 | tf_op jit(solution)/shard_map/ppermute | solution.py:692
  221.0 38.1 %copy-start.5 = (bf16[2,176,768]{2,1,0:T(8,128)(2,1)}, bf16[2,176,768]{2,1,0:T(8,128)(2,1)S(1)}, u32[]{:S(2)}) copy-start(bf16[2,176,768]{2,1,0:T(8,128)(2,1)S(1)} %collective-permute-done.10.refs_1_) | copy-start | bytes 1622020
  227.6 31.5 %copy-start.7 = (bf16[2,176,768]{2,1,0:T(8,128)(2,1)}, bf16[2,176,768]{2,1,0:T(8,128)(2,1)S(1)}, u32[]{:S(2)}) copy-start(bf16[2,176,768]{2,1,0:T(8,128)(2,1)S(1)} %collective-permute-done.11.refs_2_) | copy-start | bytes 1622020
  227.6 31.5 %copy-start.8 = (bf16[2,176,768]{2,1,0:T(8,128)(2,1)}, bf16[2,176,768]{2,1,0:T(8,128)(2,1)S(1)}, u32[]{:S(2)}) copy-start(bf16[2,176,768]{2,1,0:T(8,128)(2,1)S(1)} %collective-permute-done.12.refs_3_) | copy-start | bytes 1622020
  259.2 197.5 %reduce-scatter.8.cloned.1.call-start = ((), (), s32[]{:S(2)}) async-start(), calls=%async_computation.8 | async-start | bytes 1548288 | tf_op jit(solution)/shard_map/reduce_scatter | solution.py:809
  260.2 13.8 %collective-permute-start.13 = (bf16[2,176,768]{2,1,0:T(8,128)(2,1)S(1)}, bf16[2,176,768]{2,1,0:T(8,128)(2,1)S(1)}, u32[]{:S(2)}, u32[]{:S(2)}) collective-permute-start(bf16[2,176,768]{2,1,0:T(8,128)(2,1)S(1)} %copy-done.20), channel_id=1, source_target_pairs={{0,8},{8,0},{16,24},{24,16},{1,9},{9,1},{17,25},{25,17},{2,10},{10... | collective-permute-start | bytes 1622024 | tf_op jit(solution)/shard_map/ppermute | solution.py:692
  261.2 19.8 %collective-permute-start.14 = (bf16[2,176,768]{2,1,0:T(8,128)(2,1)S(1)}, bf16[2,176,768]{2,1,0:T(8,128)(2,1)S(1)}, u32[]{:S(2)}, u32[]{:S(2)}) collective-permute-start(bf16[2,176,768]{2,1,0:T(8,128)(2,1)S(1)} %copy-done.18), channel_id=1, source_target_pairs={{0,16},{8,24},{16,0},{24,8},{1,17},{9,25},{17,1},{25,9},{2,18},{10... | collective-permute-start | bytes 1622024 | tf_op jit(solution)/shard_map/ppermute | solution.py:692
  262.0 19.1 %collective-permute-start.15 = (bf16[2,176,768]{2,1,0:T(8,128)(2,1)S(1)}, bf16[2,176,768]{2,1,0:T(8,128)(2,1)S(1)}, u32[]{:S(2)}, u32[]{:S(2)}) collective-permute-start(bf16[2,176,768]{2,1,0:T(8,128)(2,1)S(1)} %copy-done.16), channel_id=1, source_target_pairs={{0,24},{8,16},{16,8},{24,0},{1,25},{9,17},{17,9},{25,1},{2,26},{10... | collective-permute-start | bytes 1622024 | tf_op jit(solution)/shard_map/ppermute | solution.py:692
  274.0 7.1 %copy-start.15 = (bf16[2,176,768]{2,1,0:T(8,128)(2,1)}, bf16[2,176,768]{2,1,0:T(8,128)(2,1)S(1)}, u32[]{:S(2)}) copy-start(bf16[2,176,768]{2,1,0:T(8,128)(2,1)S(1)} %collective-permute-done.13.refs_5_) | copy-start | bytes 1622020
  374.3 26.0 %collective-permute-start.18 = (bf16[2,384,896]{2,1,0:T(8,128)(2,1)S(1)}, bf16[2,384,896]{2,1,0:T(8,128)(2,1)S(1)}, u32[]{:S(2)}, u32[]{:S(2)}) collective-permute-start(bf16[2,384,896]{2,1,0:T(8,128)(2,1)S(1)} %slice.82), channel_id=1, source_target_pairs={{0,16},{8,24},{16,0},{24,8},{1,17},{9,25},{17,1},{25,9},{2,18},{10... | collective-permute-start | bytes 4128776 | tf_op jit(solution)/shard_map/ppermute | solution.py:608
  377.7 29.1 %collective-permute-start.16 = (bf16[2,384,896]{2,1,0:T(8,128)(2,1)S(1)}, bf16[2,384,896]{2,1,0:T(8,128)(2,1)S(1)}, u32[]{:S(2)}, u32[]{:S(2)}) collective-permute-start(bf16[2,384,896]{2,1,0:T(8,128)(2,1)S(1)} %slice.78), channel_id=1, source_target_pairs={{0,8},{8,0},{16,24},{24,16},{1,9},{9,1},{17,25},{25,17},{2,10},{10... | collective-permute-start | bytes 4128776 | tf_op jit(solution)/shard_map/ppermute | solution.py:608
  402.0 14.6 %collective-permute-start.19 = (bf16[384,896]{1,0:T(8,128)(2,1)S(1)}, bf16[384,896]{1,0:T(8,128)(2,1)S(1)}, u32[]{:S(2)}, u32[]{:S(2)}) collective-permute-start(bf16[384,896]{1,0:T(8,128)(2,1)S(1)} %slice_bitcast_fusion), channel_id=1, source_target_pairs={{0,8},{8,0},{16,24},{24,16},{1,9},{9,1},{17,25},{25,17},{2,10},{10... | collective-permute-start | bytes 2064392 | tf_op jit(solution)/shard_map/ppermute | solution.py:608
  407.2 12.4 %collective-permute-start.17 = (bf16[384,896]{1,0:T(8,128)(2,1)S(1)}, bf16[384,896]{1,0:T(8,128)(2,1)S(1)}, u32[]{:S(2)}, u32[]{:S(2)}) collective-permute-start(bf16[384,896]{1,0:T(8,128)(2,1)S(1)} %slice_bitcast_fusion.2), channel_id=1, source_target_pairs={{0,16},{8,24},{16,0},{24,8},{1,17},{9,25},{17,1},{25,9},{2,18},{10... | collective-permute-start | bytes 2064392 | tf_op jit(solution)/shard_map/ppermute | solution.py:608
  (15 other events, 28.4 us)
Sparse Core Ops, SparseCore 0:
  12.2 26.5 all-gather.4
  41.0 90.3 all-gather.6
  133.0 89.1 all-gather.8
  224.4 97.8 reduce-scatter.3
  324.4 97.9 reduce-scatter.5
  424.5 32.0 reduce-scatter.7

commit v5 on v4

--- a/solution.py
+++ b/solution.py
@@ -17,6 +17,7 @@
 LANES = 128
 BLOCK = 256
 TILE = 256
+STRIDE = 32
 F32 = jnp.float32
 BF16 = jnp.bfloat16
 VMEM_LIMIT = 56 << 20
@@ -134,7 +135,7 @@
     rows = x[...].astype(F32)
     scale = lax.rsqrt(jnp.mean(rows * rows, axis=1, keepdims=True) + EPS)
     normed = (rows * scale * small_t[16:17, :]).astype(BF16)
-    n_out[...] = normed
+    n_out[...] = normed.T
     cos = cosine[...]
     sin = sine[...]
     for weight, out, factor in ((wq, q_out, HEAD_DIM**-0.5), (wk, k_out, None)):
@@ -274,7 +275,7 @@
             out[1] = slot_g
 
 
-def expert_kernel(owners, merged, *refs):
+def expert_kernel(owners, merged, halves, core, *refs):
     sent = refs[:owners]
     weights = refs[owners : owners + 6]
     backs = refs[owners + 6 : 2 * owners + 6]
@@ -318,18 +319,29 @@
     down_grad = mm_tn(hid, s).astype(BF16)
     gate_grad = mm_tn(r, gate_g).astype(BF16)
     up_grad = mm_tn(r, up_g).astype(BF16)
-    base = 4 * steps * chunk_rows if merged else 0
+    even = core[0] == 0
     for i in range(2):
         tile = 2 * step + i
         for index, value in enumerate((gate_grad, up_grad)):
             start = pl.multiple_of((index * 2 * steps + tile) * chunk_rows, 16)
-            grads[0][:, pl.ds(start, chunk_rows), :] = value[:, i * TILE : (i + 1) * TILE].reshape(
-                chunks, chunk_rows, TILE
-            )
-        for c in range(width // TILE):
-            grads[-1][tile, base + c * TILE : base + (c + 1) * TILE, :] = down_grad[
-                i * TILE : (i + 1) * TILE, c * TILE : (c + 1) * TILE
-            ]
+            place = pl.ds(start, chunk_rows)
+            value = value[:, i * TILE : (i + 1) * TILE]
+            if halves:
+                value = value.reshape(chunks // 2, 2, chunk_rows, TILE)
+                for out, flag in zip(grads, (even, jnp.logical_not(even))):
+                    out[:, place, :] = jnp.where(flag, value[:, 0], value[:, 1])
+            else:
+                grads[0][:, place, :] = value.reshape(chunks, chunk_rows, TILE)
+    base = 4 * steps * chunk_rows if merged else 0
+    for c in range(width // TILE):
+        pair = [down_grad[i * TILE : (i + 1) * TILE, c * TILE : (c + 1) * TILE] for i in range(2)]
+        place = slice(base + c * TILE, base + (c + 1) * TILE)
+        if halves:
+            for out, flag in zip(grads, (even, jnp.logical_not(even))):
+                out[step, place, :] = jnp.where(flag, pair[0], pair[1])
+        else:
+            for i in range(2):
+                grads[-1][2 * step + i, place, :] = pair[i]
 
     @pl.when(step == steps - 1)
     def _():
@@ -466,18 +478,21 @@
 
 
 def attend_back_kernel(
-    prefix, q, k, v, grad, lse, delta, cosine, sine, dq_out, dk_out, dv_out, bias, dq_acc
+    start, me, prefix, q, k, v, grad, lse, delta, cosine, sine, normed, output_g,
+    dq_out, dk_out, dv_out, grad_out, bias, dq_acc,
 ):
     length = q.shape[0]
-    pair = pl.program_id(0)
+    step = pl.program_id(0)
+    pair = step + start
     block = BLOCK
     lane_all = iota((length, LANES), 1)
     lane = iota((block, LANES), 1)
 
-    @pl.when(pair == 0)
+    @pl.when(step == 0)
     def _():
         limit = jnp.maximum(iota((1, length), 1) + 1, prefix[0])
         bias[...] = jnp.where(iota((length, length), 0) < limit, 0.0, NEG).astype(BF16)
+        grad_out[me[0] ^ 3] = output_g[...]
 
     q_pair = q[...]
     g_pair = grad[...]
@@ -519,26 +534,28 @@
     lax.fori_loop(0, length // block, one_block, 0)
     dq = dq_acc[...] * (HEAD_DIM**-0.5)
     dq_out[...] = (dq * cosine[...] - half_swap(dq) * sine[...]).astype(BF16)
-
-
-def project_back_kernel(
-    me, x, normed, dq, dk, dv, resg, wq, wk, wv, small_t, small_g, output_g,
-    tok_out, grad_out, acc, first_acc,
-):
+    columns = pl.ds(pl.multiple_of(step * LANES, LANES), LANES)
+    for j, part in enumerate((dq_out, dk_out, dv_out)):
+        grad_out[me[0] ^ j, :, columns] = mm(normed[...], part[...]).astype(BF16)
+
+
+def project_back_kernel(me, x, *refs):
+    parts = refs[:-9]
+    resg, wq, wk, wv, small_t, small_g, tok_out, small_out, first_acc = refs[-9:]
     step = pl.program_id(0)
     block, width = x.shape
 
     @pl.when(step == 0)
     def _():
-        acc[...] = jnp.zeros_like(acc)
         first_acc[...] = jnp.zeros_like(first_acc)
 
     rows = x[...].astype(F32)
     scale = lax.rsqrt(jnp.mean(rows * rows, axis=1, keepdims=True) + EPS)
-    normed_g = mm_nt(dq[...], wq[0]) + mm_nt(dk[...], wk[0]) + mm_nt(dv[...], wv[0])
-    n_low = normed[...]
-    for index, part in enumerate((dq, dk, dv)):
-        acc[:, index * width : (index + 1) * width] += mm_tn(n_low, part[...])
+    normed_g = None
+    for j, weight in enumerate((wq, wk, wv)):
+        part = jnp.concatenate([p[...] for p in parts[j::3]], axis=1)
+        one = mm_nt(part, weight[0])
+        normed_g = one if normed_g is None else normed_g + one
     first_acc[...] += jnp.sum(
         (normed_g * rows * scale).reshape(block // 8, 8, width), axis=0
     )
@@ -549,25 +566,20 @@
 
     @pl.when(step == pl.num_programs(0) - 1)
     def _():
-        for j in range(3):
-            grad_out[me[0] ^ j, :, 0:width] = acc[:, j * width : (j + 1) * width].astype(BF16)
-            grad_out[me[0] ^ j, :, width : width + LANES] = jnp.zeros((width, LANES), BF16)
         first = jnp.sum(first_acc[...], axis=0, keepdims=True)
         row = iota((LANES, width), 0)
-        extra = small_g[...] + jnp.where(row == 16, first, 0.0).T
-        grad_out[me[0] ^ 3, :, 0:width] = output_g[...]
-        grad_out[me[0] ^ 3, :, width : width + LANES] = extra.astype(BF16)
+        small_out[...] = (small_g[...] + jnp.where(row == 16, first, 0.0).T).astype(BF16)
 
 
 def rotary_tables():
     half = HEAD_DIM // 2
-    frequency = np.float32(10000.0) ** (
-        -np.arange(half, dtype=np.float32) * np.float32(2.0) / np.float32(HEAD_DIM)
-    )
-    angles = np.arange(LEN, dtype=np.float32)[:, None] * frequency[None, :].astype(np.float32)
-    cos = np.cos(angles.astype(np.float64)).astype(np.float32)
-    sin = np.sin(angles.astype(np.float64)).astype(np.float32)
-    return np.tile(cos, (1, 4)), np.tile(np.concatenate([-sin, sin], axis=1), (1, 2))
+    frequency = 10000.0 ** (-np.arange(half) * 2.0 / HEAD_DIM)
+    sign = np.tile(np.repeat([-1.0, 1.0], half), LANES // HEAD_DIM)
+    tables = []
+    for positions in (np.arange(0, LEN, STRIDE), np.arange(STRIDE)):
+        angles = np.tile(positions[:, None] * frequency[None, :], (1, LANES // half))
+        tables += [np.cos(angles), np.sin(angles)]
+    return [t.astype(np.float32) for t in tables + [sign]]
 
 
 def body(
@@ -587,7 +599,11 @@
     down_rows = down_weight.shape[1]
     me = lax.axis_index("expert").astype(jnp.int32).reshape(1)
     packed_width = width + LANES
-    cosine, sine = (jnp.asarray(t) for t in rotary_tables())
+    cos_a, sin_a, cos_b, sin_b, sign = (jnp.asarray(t) for t in rotary_tables())
+    cos_a, sin_a, cos_b, sin_b, me = lax.optimization_barrier((cos_a, sin_a, cos_b, sin_b, me))
+    cos_a, sin_a, cos_b, sin_b = cos_a[:, None], sin_a[:, None], cos_b[None], sin_b[None]
+    cosine = (cos_a * cos_b - sin_a * sin_b).reshape(LEN, LANES)
+    sine = ((sin_a * cos_b + cos_a * sin_b) * sign).reshape(LEN, LANES)
     struct = jax.ShapeDtypeStruct
 
     packed = call(
@@ -607,6 +623,10 @@
     def send(part, k):
         return lax.ppermute(part, "expert", [(i, i ^ k) for i in range(owners)])
 
+    def add(a, b):
+        return (a.astype(F32) + b.astype(F32)).astype(BF16)
+
+    core = (lax.axis_index("shard") % 2).astype(jnp.int32).reshape(1)
     half = width // 2
     own = lax.all_gather(packed, "shard", axis=0, tiled=True)
     top, low = own[None, :half, :width], own[None, half:, :width]
@@ -669,8 +689,8 @@
     queries, keys, values, normed_one, small_t = call(
         project_kernel, "project", (steps,),
         [wide] + weight_block + [small_block, table, table],
-        [wide] * 4 + [whole((LANES, width))],
-        [act] * 4 + [struct((LANES, width), F32)],
+        [wide] * 3 + [pl.BlockSpec((width, BLOCK), lambda i, *rest: (0, i)), whole((LANES, width))],
+        [act] * 3 + [struct((width, count), BF16), struct((LANES, width), F32)],
         flops=6 * count * width * width, traffic=12 << 20, prefetch=1,
     )(me, tokens, weights, weights, weights, own, cosine, sine)
 
@@ -716,26 +736,31 @@
     def run_expert(l, rows, after):
         gate_up, down = expert_full[l]
         weights = [
-            pl.BlockSpec((chunks, chunk_rows, TILE), lambda f, j=j: (0, j // 2 * tiles + 2 * f + j % 2, 0))
+            pl.BlockSpec((chunks, chunk_rows, TILE), lambda f, *rest, j=j: (0, j // 2 * tiles + 2 * f + j % 2, 0))
             for j in range(4)
         ] + [
-            pl.BlockSpec((1, width, TILE), lambda f, j=j: (2 * f + j, 2 if aligned else 0, 0))
+            pl.BlockSpec((1, width, TILE), lambda f, *rest, j=j: (2 * f + j, 2 if aligned else 0, 0))
             for j in range(2)
         ]
-        if aligned:
+        halves = aligned and l + 1 == local_experts
+        if halves:
+            grad_shapes = [(shards // 2, expert_rows, TILE)] * 2
+        elif aligned:
             grad_shapes = [(shards, expert_rows, TILE)]
         else:
             grad_shapes = [(1, 2 * tiles * width, TILE), (tiles, width, TILE)]
         outs = call(
-            functools.partial(expert_kernel, owners, aligned), "expert", (tiles // 2,),
+            functools.partial(expert_kernel, owners, aligned, halves), "expert", (tiles // 2,),
             [pair] * owners + weights,
             [pair] * owners + [whole(g) for g in grad_shapes],
             [pair_shape] * owners + [struct(g, BF16) for g in grad_shapes],
             scratch=[pltpu.VMEM((local, width), BF16)] * 2 + [pltpu.VMEM((local, width), F32)] * 2,
-            flops=16 * local * width * ff, traffic=24 << 20, trans=local * ff,
-        )(*rows, gate_up, gate_up, gate_up, gate_up, down, down)
+            flops=16 * local * width * ff, traffic=24 << 20, trans=local * ff, prefetch=1,
+        )(core, *rows, gate_up, gate_up, gate_up, gate_up, down, down)
         grads = outs[owners:]
-        if aligned:
+        if halves:
+            keep, give = grads
+        elif aligned:
             grad = grads[0]
         else:
             gate_up_g = grads[0].reshape(2 * tiles, shards, shard_rows, TILE).transpose(1, 0, 2, 3)
@@ -744,20 +769,31 @@
             grad = jnp.concatenate(
                 [gate_up_g.reshape(shards, -1, TILE), down_g.reshape(shards, -1, TILE)], axis=1
             )
+        if halves:
+            grad = add(keep, lax.ppermute(give, "shard", [(i, i ^ 1) for i in range(shards)]))
         grad, after = lax.optimization_barrier((grad, after))
-        total = lax.psum_scatter(
-            grad.reshape(shards * expert_rows, TILE), "shard", scatter_dimension=0, tiled=True
+        return outs[:owners], grad.reshape(-1, TILE), after
+
+    def reduce_expert(grad):
+        return lax.psum_scatter(
+            grad, "shard", scatter_dimension=0, tiled=True,
+            axis_index_groups=(
+                None if len(grad) == shards * expert_rows
+                else [list(range(c, shards, 2)) for c in range(2)]
+            ),
         )
-        return outs[:owners], total, after
 
     returned = []
     expert_sums = []
     for l in range(local_experts):
         rows, ahead = lax.optimization_barrier((received[l], returned or dispatched[-1]))
         returned = ahead if returned else returned
-        back, total, received[l + 1 :] = run_expert(l, rows, received[l + 1 :])
-        returned = returned + exchange(back)
-        expert_sums.append(total)
+        back, grad, received[l + 1 :] = run_expert(l, rows, received[l + 1 :])
+        back = exchange(back)
+        if l + 1 == local_experts:
+            back, grad = lax.optimization_barrier((back, grad))
+        returned = returned + back
+        expert_sums.append(reduce_expert(grad))
 
     mixed, previous_grad, residual_grad, heads_grad, delta, output_grad, small_grad = call(
         functools.partial(combine_kernel, experts, owners, local_experts), "combine", (steps,),
@@ -775,40 +811,65 @@
     )(me, *returned, residual, normed_two, cotangent, tok,
       routes, dest_col, attn_mix, weights, small_t)
 
-    pair_block = pl.BlockSpec((count, LANES), lambda i, *rest: (0, i))
-    dq, dk, dv = call(
-        attend_back_kernel, "attend_back", (width // LANES,),
-        [pair_block] * 4
-        + [whole((16, count))] * 2
-        + [whole((count, LANES))] * 2,
-        [pair_block] * 3,
-        [act] * 3,
-        scratch=[pltpu.VMEM((count, count), BF16), pltpu.VMEM((count, LANES), F32)],
-        flops=60 << 30, traffic=12 << 20, trans=HEADS * count * count, prefetch=1,
-    )(prefix, queries, keys, values, heads_grad, lse, delta, cosine, sine)
-
-    tokens_grad, dense_grad = call(
+    def first_turn(grad):
+        return send(grad[1::2, :half], 1), send(grad[2:, half:], 2)
+
+    def second_turn(grad, came):
+        top, low = add(grad[0::2, :half], came[0]), add(grad[:2, half:], came[1])
+        return (top[0], low[0]), (send(top[1], 2), send(low[1], 1))
+
+    def join(mine, came):
+        return jnp.concatenate([add(a, b) for a, b in zip(mine, came)], axis=0)
+
+    pairs = width // LANES // 2
+    columns = pairs * LANES
+    half_out = pl.BlockSpec((count, LANES), lambda i, *rest: (0, i))
+    parts = []
+    dense_grads = []
+    moved = ()
+    for start in (0, pairs):
+        pair_block = pl.BlockSpec((count, LANES), lambda i, *rest, start=start: (0, i + start))
+        *three, dense_grad = call(
+            functools.partial(attend_back_kernel, start), "attend_back", (pairs,),
+            [pair_block] * 4
+            + [whole((16, count))] * 2
+            + [whole((count, LANES))] * 2
+            + [whole((width, count)),
+               pl.BlockSpec((width, columns), lambda i, *rest, start=start: (0, start // pairs))],
+            [half_out] * 3 + [whole((owners, width, columns))],
+            [struct((count, columns), BF16)] * 3 + [struct((owners, width, columns), BF16)],
+            scratch=[pltpu.VMEM((count, count), BF16), pltpu.VMEM((count, LANES), F32)],
+            flops=30 << 30, traffic=6 << 20, trans=HEADS // 2 * count * count, prefetch=2,
+        )(me, prefix, queries, keys, values, heads_grad, lse, delta, cosine, sine, normed_one,
+          output_grad)
+        if start:
+            three, moved, expert_sums[0] = lax.optimization_barrier((three, moved, expert_sums[0]))
+        parts += three
+        dense_grads.append(dense_grad)
+        if start == 0:
+            moved = first_turn(dense_grad)
+    mine_a, moved_a = second_turn(dense_grads[0], moved)
+    moved_b = first_turn(dense_grads[1])
+
+    half_wide = rows_of(BLOCK, columns)
+    tokens_grad, small_grad = call(
         project_back_kernel, "project_back", (steps,),
-        [wide] * 6 + weight_block + [whole((LANES, width)), whole((width, LANES)), whole((width, width))],
-        [wide, whole((owners, width, width + LANES))],
-        [struct((count, width), F32), struct((owners, width, width + LANES), BF16)],
-        scratch=[pltpu.VMEM((width, 3 * width), F32), pltpu.VMEM((8, width), F32)],
-        flops=12 * count * width * width, traffic=24 << 20, prefetch=1,
-    )(me, tokens, normed_one, dq, dk, dv, residual_grad, weights, weights, weights, small_t,
-      small_grad, output_grad)
-
-    def add(a, b):
-        return (a.astype(F32) + b.astype(F32)).astype(BF16)
-
-    top, low = dense_grad[:, :half], dense_grad[:, half:]
-    top_in, low_in = send(top[1::2], 1), send(low[2:], 2)
-    top, low = add(top[0::2], top_in), add(low[:2], low_in)
-    top_in, low_in = send(top[1], 2), send(low[1], 1)
-    quarter = jnp.concatenate([add(top[0], top_in), add(low[0], low_in)], axis=0)
+        [wide] + [half_wide] * 6 + [wide] + weight_block
+        + [whole((LANES, width)), whole((width, LANES))],
+        [wide, whole((width, LANES))],
+        [struct((count, width), F32), struct((width, LANES), BF16)],
+        scratch=[pltpu.VMEM((8, width), F32)],
+        flops=6 * count * width * width, traffic=18 << 20, prefetch=1,
+    )(me, tokens, *parts, residual_grad, weights, weights, weights, small_t, small_grad)
+    small_grad, moved_a, moved_b = lax.optimization_barrier((small_grad, moved_a, moved_b))
+    mine_b, moved_b = second_turn(dense_grads[1], moved_b)
+    quarters = [join(mine_a, moved_a), join(mine_b, moved_b)]
+    quarter = jnp.concatenate(quarters + [small_grad], axis=1)
     quarter, expert_sums = lax.optimization_barrier((quarter, expert_sums))
     quarter = lax.psum_scatter(quarter, "shard", scatter_dimension=0, tiled=True)
-    dense = lax.all_gather(quarter, "expert", axis=0, tiled=False).astype(F32)
-    small = dense[3, :, width:]
+    gathered = lax.all_gather(quarter, "expert", axis=0, tiled=False).astype(F32)
+    dense = gathered[:, :, :width]
+    small = jnp.sum(gathered[:, :, width:], axis=0)
     if aligned:
         out_shapes = [w.shape for w in (gate_weight, up_weight, down_weight)]
         gate_sum, up_sum, down_sum = call(
@@ -832,10 +893,10 @@
         mixed,
         tokens_grad,
         previous_grad,
-        dense[0, :, :width],
-        dense[1, :, :width],
-        dense[2, :, :width],
-        dense[3, :, :width],
+        dense[0],
+        dense[1],
+        dense[2],
+        dense[3],
         small[:, 0:kinds],
         small[:, kinds : kinds + 4],
         small[:, 18:20].T,

time: 488 us -> 476 us (0.975)
  waiting for transfers between devices: 159 us -> 133 us
  other arithmetic: 8.61 us -> 16.2 us
  Pallas kernels: 235 us -> 242 us
    ppermute x8 -> x12, waiting for transfers between devices: 57.5 us -> 34.6 us  [send(): return lax.ppermute(part, 'expert', [(i, i ^ k) for i in range(owners)])]
    pallas_call x4 -> x5, Pallas kernels: 125 us -> 133 us  [the longest x2 62.2 us: run_expert(): call(functools.partial(expert_kernel, owners, aligned, halves), 'expert',...]
    convert_element_type x4 -> x6, other arithmetic: 2.34 us -> 8.06 us  [add(): return (a.astype(F32) + b.astype(F32)).astype(BF16)]
    ppermute x12, waiting for transfers between devices: 48.2 us -> 42.9 us  [exchange(): lax.ppermute(part, 'expert', [(i, i ^ k) for i in range(owners)])]
    ppermute x0 -> x1, waiting for transfers between devices: none -> 5 us  [run_expert(): lax.ppermute(give, 'shard', [(i, i ^ 1) for i in range(shards)])]
    ppermute x8 -> x12, starting transfers between devices: 14.9 us -> 14.2 us  [send(): return lax.ppermute(part, 'expert', [(i, i ^ k) for i in range(owners)])]
    unnamed x48 -> x58, local copies, waits for them, and re-layouts: 10.8 us -> 11.3 us
  transfers between devices with their start and end apart: 26 -> 31, of which waited for: 17 -> 19; matrix products, arithmetic and copies ran while one was open for 4% -> 6% of each run, Pallas kernels for 49% -> 51%
where the time goes in v5:
time: 476 us; the launch traced here: 467 us
  Pallas kernels  242 us (51%)
  waiting for transfers between devices  133 us (28%)
  starting transfers between devices  28 us (6%)
  local copies, waits for them, and re-layouts  20.9 us (4%)
  other arithmetic  16.2 us (3%)
  between operations  15.5 us (3%)
  blocking collectives  11.6 us (2%)
    pallas_call x2, Pallas kernels, run_expert(): call(functools.partial(expert_kernel, owners, aligned, halves), 'expert',...  62.2 us
    pallas_call x2, Pallas kernels, body(): call(functools.partial(attend_back_kernel, start), 'attend_back', (pairs,...  60.2 us
    ppermute x12, waiting for transfers between devices, exchange(): lax.ppermute(part, 'expert', [(i, i ^ k) for i in range(owners)])  42.9 us
    pallas_call x1, Pallas kernels, body(): call(attend_kernel, 'attend', (steps,), [wide, whole((count, width)), who...  39.2 us
    ppermute x12, waiting for transfers between devices, send(): return lax.ppermute(part, 'expert', [(i, i ^ k) for i in range(owners)])  34.6 us
    reduce_scatter x1, waiting for transfers between devices, body(): lax.psum_scatter(quarter, 'shard', scatter_dimension=0, tiled=True)  28.5 us
    pallas_call x1, Pallas kernels, body(): call(functools.partial(combine_kernel, experts, owners, local_experts), '...  27.6 us
    all_gather x1, waiting for transfers between devices, body(): own = lax.all_gather(packed, 'shard', axis=0, tiled=True)  21.9 us
  transfers between devices with their start and end apart: 31, of which 19 were waited for; matrix products, arithmetic and copies ran while one was open for 6% of the time, Pallas kernels for 51%

profile of v5, /device:TPU:0, one launch (start us, length us, event | category | flops | bytes accessed | tf_op | source)
XLA Modules:
  0.0 467.1 jit_solution(3861284165502837261)
XLA Ops:
  12.1 2.3 pack_expert.2
  14.5 2.3 pack_expert.3
  16.9 21.9 %all-gather.5.cloned.1.call-done.small = bf16[768,896]{1,0:T(8,128)(2,1)} async-done(((bf16[96,896]{1,0:T(8,128)(2,1)}), bf16[768,896]{1,0:T(8,128)(2,1)}) %all-gather.5.cloned.1.call-update) | async-done | bytes 1376272 | tf_op jit(solution)/shard_map/all_gather | solution.py:631
  43.1 12.5 %collective-permute-done.2 = bf16[1,384,768]{2,1,0:T(8,128)(2,1)S(1)} collective-permute-done((bf16[1,384,768]{2,1,0:T(8,128)(2,1)S(1)}, bf16[1,384,768]{2,1,0:T(8,128)(2,1)S(1)}, u32[]{:S(2)}, u32[]{:S(2)}) %collective-permute-start.2) | collective-permute-done | bytes 589856 | tf_op jit(solution)/shard_map/ppermute | solution.py:624
  65.4 6.9 %slots.1 = (s32[1024,128]{1,0:T(8,128)}, s32[8,1024]{1,0:T(8,128)}) custom-call(s32[1024,2]{1,0:T(8,128)} %copy.73.routes.refs_12_, s32[1,1024]{1,0:T(1,128)} %order_row.1, s32[1024,1]{1,0:T(8,128)} %copy.75.order_col), custom_call_target="tpu_custom_call" | custom-call | flops 805306368 | bytes 1048576 | tf_op jit(solution)/shard_map/slots/pallas_call | solution.py:671
  74.1 10.3 %collective-permute-done.3 = bf16[2,384,768]{2,1,0:T(8,128)(2,1)} collective-permute-done((bf16[2,384,768]{2,1,0:T(8,128)(2,1)}, bf16[2,384,768]{2,1,0:T(8,128)(2,1)}, u32[]{:S(2)}, u32[]{:S(2)}) %collective-permute-start.3) | collective-permute-done | bytes 1179680 | tf_op jit(solution)/shard_map/ppermute | solution.py:624
  86.6 2.8 maximum_maximum_fusion.wq.wk.wv.wo.refs_15_.refs_7_.refs_8_.refs_9_
  89.4 8.6 %project.1 = (bf16[1024,768]{1,0:T(8,128)(2,1)}, bf16[1024,768]{1,0:T(8,128)(2,1)}, bf16[1024,768]{1,0:T(8,128)(2,1)}, bf16[768,1024]{1,0:T(8,128)(2,1)}, f32[128,768]{1,0:T(8,128)}) custom-call(s32[1]{0:T(128)} %bitcast.me, bf16[1024,768]{1,0:T(8,128)(2,1)} %x.5, bf16[4,768,768]{2,1,0:T(8,128)(2,1)} %maximum_maximum_fusion.wq.wk.wv.wo.refs_15_.refs_7_.refs_8_.refs_9_, ...), custom_call_target="tpu_custom_call" | custom-call | flops 3623878656 | bytes 12582912 | tf_op jit(solution)/shard_map/project/pallas_call | solution.py:689
  98.0 39.2 %attend.1 = (bf16[1024,768]{1,0:T(8,128)(2,1)}, f32[16,1024]{1,0:T(8,128)}, f32[1024,768]{1,0:T(8,128)}, bf16[1024,768]{1,0:T(8,128)(2,1)}, f32[1024,128]{1,0:T(8,128)}) custom-call(s32[1]{0:T(128)} %bitcast.me, s32[1]{0:T(128)S(6)} %copy.83.prefix, bf16[1024,768]{1,0:T(8,128)(2,1)} %get-tuple-element.112.q, bf16[1024,768]{1,0:T(8,128)(2,1)} %get-tuple-element.113.k, ...), custom_call_target="tpu_custom_call" | custom-call | flops 32212254720 | bytes 16777216 | tf_op jit(solution)/shard_map/attend/pallas_call | solution.py:697
  137.2 8.3 %dispatch.2 = (bf16[2,176,768]{2,1,0:T(8,128)(2,1)}, bf16[2,176,768]{2,1,0:T(8,128)(2,1)}, bf16[2,176,768]{2,1,0:T(8,128)(2,1)}, bf16[2,176,768]{2,1,0:T(8,128)(2,1)}) custom-call(s32[1]{0:T(128)} %bitcast.me, bf16[1024,768]{1,0:T(8,128)(2,1)} %get-tuple-element.116.normed.refs_9_, bf16[1024,768]{1,0:T(8,128)(2,1)} %refs_10_.1, ...), custom_call_target="tpu_custom_call" | custom-call | flops 2214592512 | bytes 6291456 | tf_op jit(solution)/shard_map/dispatch/pallas_call | solution.py:720
  149.0 7.9 %dispatch.3 = (bf16[2,176,768]{2,1,0:T(8,128)(2,1)}, bf16[2,176,768]{2,1,0:T(8,128)(2,1)}, bf16[2,176,768]{2,1,0:T(8,128)(2,1)}, bf16[2,176,768]{2,1,0:T(8,128)(2,1)}) custom-call(s32[1]{0:T(128)} %bitcast.me, bf16[1024,768]{1,0:T(8,128)(2,1)} %get-tuple-element.116.normed.refs_9_, bf16[1024,768]{1,0:T(8,128)(2,1)} %refs_10_.1, ...), custom_call_target="tpu_custom_call" | custom-call | flops 2214592512 | bytes 6291456 | tf_op jit(solution)/shard_map/dispatch/pallas_call | solution.py:720
  158.7 2.2 collective-permute-done.4.refs_1_
  162.1 8.3 %collective-permute-done.5.refs_2_ = bf16[2,176,768]{2,1,0:T(8,128)(2,1)S(1)} collective-permute-done((bf16[2,176,768]{2,1,0:T(8,128)(2,1)}, bf16[2,176,768]{2,1,0:T(8,128)(2,1)S(1)}, u32[]{:S(2)}, u32[]{:S(2)}) %collective-permute-start.5) | collective-permute-done | bytes 540704 | tf_op jit(solution)/shard_map/ppermute | solution.py:712
  170.4 3.0 collective-permute-done.6.refs_3_
  174.2 30.7 %expert.2 = (bf16[2,176,768]{2,1,0:T(8,128)(2,1)}, bf16[2,176,768]{2,1,0:T(8,128)(2,1)}, bf16[2,176,768]{2,1,0:T(8,128)(2,1)}, bf16[2,176,768]{2,1,0:T(8,128)(2,1)}, bf16[8,2304,256]{2,1,0:T(8,128)(2,1)}) custom-call(s32[1]{0:T(128)} %bitcast.1.core, bf16[2,176,768]{2,1,0:T(8,128)(2,1)} %get-tuple-element.127.refs_0_, bf16[2,176,768]{2,1,0:T(8,128)(2,1)} %copy-done.17, ...), custom_call_target="tpu_custom_call" | custom-call | flops 17716740096 | bytes 25165824 | tf_op jit(solution)/shard_map/expert/pallas_call | solution.py:752
  209.5 11.1 %collective-permute-done.10.refs_1_ = bf16[2,176,768]{2,1,0:T(8,128)(2,1)S(1)} collective-permute-done((bf16[2,176,768]{2,1,0:T(8,128)(2,1)}, bf16[2,176,768]{2,1,0:T(8,128)(2,1)S(1)}, u32[]{:S(2)}, u32[]{:S(2)}) %collective-permute-start.10) | collective-permute-done | bytes 540704 | tf_op jit(solution)/shard_map/ppermute | solution.py:712
  220.6 6.3 %collective-permute-done.11.refs_2_ = bf16[2,176,768]{2,1,0:T(8,128)(2,1)S(1)} collective-permute-done((bf16[2,176,768]{2,1,0:T(8,128)(2,1)S(1)}, bf16[2,176,768]{2,1,0:T(8,128)(2,1)S(1)}, u32[]{:S(2)}, u32[]{:S(2)}) %collective-permute-start.11) | collective-permute-done | bytes 540704 | tf_op jit(solution)/shard_map/ppermute | solution.py:712
  227.0 31.5 %expert.3 = (bf16[2,176,768]{2,1,0:T(8,128)(2,1)}, bf16[2,176,768]{2,1,0:T(8,128)(2,1)}, bf16[2,176,768]{2,1,0:T(8,128)(2,1)}, bf16[2,176,768]{2,1,0:T(8,128)(2,...) custom-call(s32[1]{0:T(128)} %bitcast.1.core, bf16[2,176,768]{2,1,0:T(8,128)(2,1)} %get-tuple-element.144.refs_0_, ...), custom_call_target="tpu_custom_call" | custom-call | flops 17716740096 | bytes 25165824 | tf_op jit(solution)/shard_map/expert/pallas_call | solution.py:752
  260.1 2.1 collective-permute-start.15
  262.2 5.0 %collective-permute-done.16 = bf16[4,2304,256]{2,1,0:T(8,128)(2,1)S(1)} collective-permute-done((bf16[4,2304,256]{2,1,0:T(8,128)(2,1)}, bf16[4,2304,256]{2,1,0:T(8,128)(2,1)S(1)}, u32[]{:S(2)}, u32[]{:S(2)}) %collective-permute-start.16) | collective-permute-done | bytes 4718624 | tf_op jit(solution)/shard_map/ppermute | solution.py:773
  267.2 6.0 %add_convert_fusion = bf16[4,2304,256]{2,1,0:T(8,128)(2,1)} fusion(bf16[4,2304,256]{2,1,0:T(8,128)(2,1)S(1)} %collective-permute-done.16, bf16[4,2304,256]{2,1,0:T(8,128)(2,1)} %get-tuple-element.152), kind=kLoop, calls=%fused_computation | loop fusion | flops 9437184 | bytes 14155776 | tf_op jit(solution)/shard_map/convert_element_type | solution.py:627
  274.0 11.0 %collective-permute-done.14.refs_6_ = bf16[2,176,768]{2,1,0:T(8,128)(2,1)S(1)} collective-permute-done((bf16[2,176,768]{2,1,0:T(8,128)(2,1)}, bf16[2,176,768]{2,1,0:T(8,128)(2,1)S(1)}, u32[]{:S(2)}, u32[]{:S(2)}) %collective-permute-start.14) | collective-permute-done | bytes 540704 | tf_op jit(solution)/shard_map/ppermute | solution.py:712
  286.1 27.6 %combine.1 = (bf16[1024,768]{1,0:T(8,128)(2,1)}, f32[1024,12]{1,0:T(8,128)}, f32[1024,768]{1,0:T(8,128)}, bf16[1024,768]{1,0:T(8,128)(2,1)}, f32[16,1024]{1,0:T(...) custom-call(s32[1]{0:T(128)} %bitcast.me, bf16[2,176,768]{2,1,0:T(8,128)(2,1)} %get-tuple-element.140.refs_0_, ...), custom_call_target="tpu_custom_call" | custom-call | flops 9059696640 | bytes 25165824 | tf_op jit(solution)/shard_map/combine/pallas_call | solution.py:798
  313.7 30.0 %attend_back.2 = (bf16[1024,384]{1,0:T(8,128)(2,1)}, bf16[1024,384]{1,0:T(8,128)(2,1)}, bf16[1024,384]{1,0:T(8,128)(2,1)}, bf16[4,768,384]{2,1,0:T(8,128)(2,1)}) custom-call(s32[1]{0:T(128)} %bitcast.me, s32[1]{0:T(128)S(6)} %copy.83.prefix, bf16[1024,768]{1,0:T(8,128)(2,1)} %get-tuple-element.112.q, bf16[1024,768]{1,0:T(8,128)(2,1)} %get-tuple-element.113.k, ...), custom_call_target="tpu_custom_call" | custom-call | flops 32212254720 | bytes 6291456 | tf_op jit(solution)/shard_map/attend_back/pallas_call | solution.py:832
  347.1 30.2 %attend_back.3 = (bf16[1024,384]{1,0:T(8,128)(2,1)}, bf16[1024,384]{1,0:T(8,128)(2,1)}, bf16[1024,384]{1,0:T(8,128)(2,1)}, bf16[4,768,384]{2,1,0:T(8,128)(2,1)}) custom-call(s32[1]{0:T(128)} %bitcast.me, s32[1]{0:T(128)S(6)} %copy.83.prefix, bf16[1024,768]{1,0:T(8,128)(2,1)} %get-tuple-element.112.q, bf16[1024,768]{1,0:T(8,128)(2,1)} %get-tuple-element.113.k, ...), custom_call_target="tpu_custom_call" | custom-call | flops 32212254720 | bytes 6291456 | tf_op jit(solution)/shard_map/attend_back/pallas_call | solution.py:832
  377.3 2.5 fusion.4
  385.7 10.4 %project_back.1 = (f32[1024,768]{1,0:T(8,128)}, bf16[768,128]{1,0:T(8,128)(2,1)}) custom-call(s32[1]{0:T(128)} %bitcast.me, bf16[1024,768]{1,0:T(8,128)(2,1)} %x.5, bf16[1024,384]{1,0:T(8,128)(2,1)} %get-tuple-element.167.refs_0_, bf16[1024,384]{1,0:T(8,128)(2,1)} %get-tuple-element.168.refs_1_, bf16[1024,384]{1,0:T(8,128)(2,1)} %get-tuple-element.169.refs_2_, ...), custom_call_target="tpu_custom_call" | custom-call | flops 3623878656 | bytes 18874368 | tf_op jit(solution)/shard_map/project_back/pallas_call | solution.py:855
  398.1 2.4 collective-permute-done.19
  404.4 4.6 collective-permute-done.24
  411.8 3.9 unpack.1
  415.7 28.5 %reduce-scatter.8.cloned.1.call-done = bf16[96,896]{1,0:T(8,128)(2,1)} async-done(((bf16[768,896]{1,0:T(8,128)(2,1)}), bf16[96,896]{1,0:T(8,128)(2,1)}) %reduce-scatter.8.cloned.1.call-update) | async-done | bytes 172048 | tf_op jit(solution)/shard_map/reduce_scatter | solution.py:869
  444.2 11.6 %all-gather = bf16[384,896]{1,0:T(8,128)(2,1)S(1)} all-gather(bf16[96,896]{1,0:T(8,128)(2,1)} %reduce-scatter.8.cloned.1.call-done), channel_id=2, replica_groups=mesh['expert'=4,'shard'=8] {'expert'}, dimensions={0}, use_global_device_ids=true | all-gather | bytes 860160 | tf_op jit(solution)/shard_map/all_gather | solution.py:870
  (137 shorter events, 59.6 us)
Async XLA Ops:
  7.2 31.6 %all-gather.5.cloned.1.call-start = ((), (), s32[]{:S(2)}) async-start(), calls=%async_computation.3 | async-start | bytes 1548288 | tf_op jit(solution)/shard_map/all_gather | solution.py:631
  12.1 161.3 %all-gather.7.cloned.1.call-start = ((), (), s32[]{:S(2)}) async-start(), calls=%async_computation.4 | async-start | bytes 10616832 | tf_op jit(solution)/shard_map/all_gather | solution.py:656
  14.5 212.5 %all-gather.9.cloned.1.call-start = ((), (), s32[]{:S(2)}) async-start(), calls=%async_computation.5 | async-start | bytes 10616832 | tf_op jit(solution)/shard_map/all_gather | solution.py:656
  16.9 365.1 %reduce-scatter.4.cloned.1.call-start = ((), (), s32[]{:S(2)}) async-start(), calls=%async_computation.6 | async-start | bytes 10616832 | tf_op jit(solution)/shard_map/reduce_scatter | solution.py:778
  40.1 15.5 %collective-permute-start.2 = (bf16[1,384,768]{2,1,0:T(8,128)(2,1)S(1)}, bf16[1,384,768]{2,1,0:T(8,128)(2,1)S(1)}, u32[]{:S(2)}, u32[]{:S(2)}) collective-permute-start(bf16[1,384,768]{2,1,0:T(8,128)(2,1)S(1)} %get-tuple-element.274), channel_id=1, source_target_pairs={{0,16},{8,24},{16,0},{24,8},{1,17},{9,25},{17,1},{25,9},{2,18},{10... | collective-permute-start | bytes 1769480 | tf_op jit(solution)/shard_map/ppermute | solution.py:624
  41.6 16.6 %collective-permute-start = (bf16[1,384,768]{2,1,0:T(8,128)(2,1)S(1)}, bf16[1,384,768]{2,1,0:T(8,128)(2,1)S(1)}, u32[]{:S(2)}, u32[]{:S(2)}) collective-permute-start(bf16[1,384,768]{2,1,0:T(8,128)(2,1)S(1)} %get-tuple-element.273), channel_id=1, source_target_pairs={{0,8},{8,0},{16,24},{24,16},{1,9},{9,1},{17,25},{25,17},{2,10},{10... | collective-permute-start | bytes 1769480 | tf_op jit(solution)/shard_map/ppermute | solution.py:624
  56.8 27.7 %collective-permute-start.3 = (bf16[2,384,768]{2,1,0:T(8,128)(2,1)}, bf16[2,384,768]{2,1,0:T(8,128)(2,1)}, u32[]{:S(2)}, u32[]{:S(2)}) collective-permute-start(bf16[2,384,768]{2,1,0:T(8,128)(2,1)} %pad_maximum_fusion.2), channel_id=1, source_target_pairs={{0,8},{8,0},{16,24},{24,16},{1,9},{9,1},{17,25},{25,17},{2,10},{10... | collective-permute-start | bytes 3538952 | tf_op jit(solution)/shard_map/ppermute | solution.py:624
  59.3 27.3 %collective-permute-start.1 = (bf16[2,384,768]{2,1,0:T(8,128)(2,1)}, bf16[2,384,768]{2,1,0:T(8,128)(2,1)S(1)}, u32[]{:S(2)}, u32[]{:S(2)}) collective-permute-start(bf16[2,384,768]{2,1,0:T(8,128)(2,1)} %pad_maximum_fusion.1), channel_id=1, source_target_pairs={{0,16},{8,24},{16,0},{24,8},{1,17},{9,25},{17,1},{25,9},{2,18},{10... | collective-permute-start | bytes 3538952 | tf_op jit(solution)/shard_map/ppermute | solution.py:624
  145.5 15.4 %collective-permute-start.4 = (bf16[2,176,768]{2,1,0:T(8,128)(2,1)}, bf16[2,176,768]{2,1,0:T(8,128)(2,1)S(1)}, u32[]{:S(2)}, u32[]{:S(2)}) collective-permute-start(bf16[2,176,768]{2,1,0:T(8,128)(2,1)} %get-tuple-element.120), channel_id=1, source_target_pairs={{0,8},{8,0},{16,24},{24,16},{1,9},{9,1},{17,25},{25,17},{2,10},{10... | collective-permute-start | bytes 1622024 | tf_op jit(solution)/shard_map/ppermute | solution.py:712
  145.8 24.6 %collective-permute-start.5 = (bf16[2,176,768]{2,1,0:T(8,128)(2,1)}, bf16[2,176,768]{2,1,0:T(8,128)(2,1)S(1)}, u32[]{:S(2)}, u32[]{:S(2)}) collective-permute-start(bf16[2,176,768]{2,1,0:T(8,128)(2,1)} %get-tuple-element.121), channel_id=1, source_target_pairs={{0,16},{8,24},{16,0},{24,8},{1,17},{9,25},{17,1},{25,9},{2,18},{10... | collective-permute-start | bytes 1622024 | tf_op jit(solution)/shard_map/ppermute | solution.py:712
  147.3 26.1 %collective-permute-start.6 = (bf16[2,176,768]{2,1,0:T(8,128)(2,1)}, bf16[2,176,768]{2,1,0:T(8,128)(2,1)S(1)}, u32[]{:S(2)}, u32[]{:S(2)}) collective-permute-start(bf16[2,176,768]{2,1,0:T(8,128)(2,1)} %get-tuple-element.122), channel_id=1, source_target_pairs={{0,24},{8,16},{16,8},{24,0},{1,25},{9,17},{17,9},{25,1},{2,26},{10... | collective-permute-start | bytes 1622024 | tf_op jit(solution)/shard_map/ppermute | solution.py:712
  156.9 48.0 %collective-permute-start.7 = (bf16[2,176,768]{2,1,0:T(8,128)(2,1)}, bf16[2,176,768]{2,1,0:T(8,128)(2,1)S(1)}, u32[]{:S(2)}, u32[]{:S(2)}) collective-permute-start(bf16[2,176,768]{2,1,0:T(8,128)(2,1)} %get-tuple-element.124), channel_id=1, source_target_pairs={{0,8},{8,0},{16,24},{24,16},{1,9},{9,1},{17,25},{25,17},{2,10},{10... | collective-permute-start | bytes 1622024 | tf_op jit(solution)/shard_map/ppermute | solution.py:712
  157.2 47.6 %collective-permute-start.8 = (bf16[2,176,768]{2,1,0:T(8,128)(2,1)}, bf16[2,176,768]{2,1,0:T(8,128)(2,1)S(1)}, u32[]{:S(2)}, u32[]{:S(2)}) collective-permute-start(bf16[2,176,768]{2,1,0:T(8,128)(2,1)} %get-tuple-element.125), channel_id=1, source_target_pairs={{0,16},{8,24},{16,0},{24,8},{1,17},{9,25},{17,1},{25,9},{2,18},{10... | collective-permute-start | bytes 1622024 | tf_op jit(solution)/shard_map/ppermute | solution.py:712
  160.9 44.0 %collective-permute-start.9 = (bf16[2,176,768]{2,1,0:T(8,128)(2,1)}, bf16[2,176,768]{2,1,0:T(8,128)(2,1)S(1)}, u32[]{:S(2)}, u32[]{:S(2)}) collective-permute-start(bf16[2,176,768]{2,1,0:T(8,128)(2,1)} %get-tuple-element.126), channel_id=1, source_target_pairs={{0,24},{8,16},{16,8},{24,0},{1,25},{9,17},{17,9},{25,1},{2,26},{10... | collective-permute-start | bytes 1622024 | tf_op jit(solution)/shard_map/ppermute | solution.py:712
  206.0 204.9 %reduce-scatter.6.cloned.1.call-start = ((), (), s32[]{:S(2)}) async-start(), calls=%async_computation.7 | async-start | bytes 5898240 | tf_op jit(solution)/shard_map/reduce_scatter | solution.py:778
  206.0 14.6 %collective-permute-start.10 = (bf16[2,176,768]{2,1,0:T(8,128)(2,1)}, bf16[2,176,768]{2,1,0:T(8,128)(2,1)S(1)}, u32[]{:S(2)}, u32[]{:S(2)}) collective-permute-start(bf16[2,176,768]{2,1,0:T(8,128)(2,1)} %get-tuple-element.137), channel_id=1, source_target_pairs={{0,8},{8,0},{16,24},{24,16},{1,9},{9,1},{17,25},{25,17},{2,10},{10... | collective-permute-start | bytes 1622024 | tf_op jit(solution)/shard_map/ppermute | solution.py:712
  206.4 20.6 %collective-permute-start.11 = (bf16[2,176,768]{2,1,0:T(8,128)(2,1)S(1)}, bf16[2,176,768]{2,1,0:T(8,128)(2,1)S(1)}, u32[]{:S(2)}, u32[]{:S(2)}) collective-permute-start(bf16[2,176,768]{2,1,0:T(8,128)(2,1)S(1)} %copy-done.24), channel_id=1, source_target_pairs={{0,16},{8,24},{16,0},{24,8},{1,17},{9,25},{17,1},{25,9},{2,18},{10... | collective-permute-start | bytes 1622024 | tf_op jit(solution)/shard_map/ppermute | solution.py:712
  207.8 19.1 %collective-permute-start.12 = (bf16[2,176,768]{2,1,0:T(8,128)(2,1)S(1)}, bf16[2,176,768]{2,1,0:T(8,128)(2,1)S(1)}, u32[]{:S(2)}, u32[]{:S(2)}) collective-permute-start(bf16[2,176,768]{2,1,0:T(8,128)(2,1)S(1)} %copy-done.23), channel_id=1, source_target_pairs={{0,24},{8,16},{16,8},{24,0},{1,25},{9,17},{17,9},{25,1},{2,26},{10... | collective-permute-start | bytes 1622024 | tf_op jit(solution)/shard_map/ppermute | solution.py:712
  220.6 37.9 %copy-start.11 = (bf16[2,176,768]{2,1,0:T(8,128)(2,1)}, bf16[2,176,768]{2,1,0:T(8,128)(2,1)S(1)}, u32[]{:S(2)}) copy-start(bf16[2,176,768]{2,1,0:T(8,128)(2,1)S(1)} %collective-permute-done.10.refs_1_) | copy-start | bytes 1622020
  258.5 8.6 %collective-permute-start.16 = (bf16[4,2304,256]{2,1,0:T(8,128)(2,1)}, bf16[4,2304,256]{2,1,0:T(8,128)(2,1)S(1)}, u32[]{:S(2)}, u32[]{:S(2)}) collective-permute-start(bf16[4,2304,256]{2,1,0:T(8,128)(2,1)} %get-tuple-element.153), channel_id=1, source_target_pairs={{0,1},{1,0},{2,3},{3,2},{4,5},{5,4},{6,7},{7,6},{8,9},{9,8},{10,11... | collective-permute-start | bytes 14155784 | tf_op jit(solution)/shard_map/ppermute | solution.py:773
  258.6 15.4 %collective-permute-start.13 = (bf16[2,176,768]{2,1,0:T(8,128)(2,1)}, bf16[2,176,768]{2,1,0:T(8,128)(2,1)S(1)}, u32[]{:S(2)}, u32[]{:S(2)}) collective-permute-start(bf16[2,176,768]{2,1,0:T(8,128)(2,1)} %get-tuple-element.149), channel_id=1, source_target_pairs={{0,8},{8,0},{16,24},{24,16},{1,9},{9,1},{17,25},{25,17},{2,10},{10... | collective-permute-start | bytes 1622024 | tf_op jit(solution)/shard_map/ppermute | solution.py:712
  259.0 26.1 %collective-permute-start.14 = (bf16[2,176,768]{2,1,0:T(8,128)(2,1)}, bf16[2,176,768]{2,1,0:T(8,128)(2,1)S(1)}, u32[]{:S(2)}, u32[]{:S(2)}) collective-permute-start(bf16[2,176,768]{2,1,0:T(8,128)(2,1)} %get-tuple-element.150), channel_id=1, source_target_pairs={{0,16},{8,24},{16,0},{24,8},{1,17},{9,25},{17,1},{25,9},{2,18},{10... | collective-permute-start | bytes 1622024 | tf_op jit(solution)/shard_map/ppermute | solution.py:712
  260.1 25.0 %collective-permute-start.15 = (bf16[2,176,768]{2,1,0:T(8,128)(2,1)}, bf16[2,176,768]{2,1,0:T(8,128)(2,1)S(1)}, u32[]{:S(2)}, u32[]{:S(2)}) collective-permute-start(bf16[2,176,768]{2,1,0:T(8,128)(2,1)} %get-tuple-element.151), channel_id=1, source_target_pairs={{0,24},{8,16},{16,8},{24,0},{1,25},{9,17},{17,9},{25,1},{2,26},{10... | collective-permute-start | bytes 1622024 | tf_op jit(solution)/shard_map/ppermute | solution.py:712
  286.1 158.1 %reduce-scatter.8.cloned.1.call-start = ((), (), s32[]{:S(2)}) async-start(), calls=%async_computation.8 | async-start | bytes 1548288 | tf_op jit(solution)/shard_map/reduce_scatter | solution.py:869
  345.1 36.8 %collective-permute-start.18 = (bf16[2,384,384]{2,1,0:T(8,128)(2,1)S(1)}, bf16[2,384,384]{2,1,0:T(8,128)(2,1)}, u32[]{:S(2)}, u32[]{:S(2)}) collective-permute-start(bf16[2,384,384]{2,1,0:T(8,128)(2,1)S(1)} %get-tuple-element.267), channel_id=1, source_target_pairs={{0,16},{8,24},{16,0},{24,8},{1,17},{9,25},{17,1},{25,9},{2,18},{10... | collective-permute-start | bytes 1769480 | tf_op jit(solution)/shard_map/ppermute | solution.py:624
  346.4 35.5 %collective-permute-start.17 = (bf16[2,384,384]{2,1,0:T(8,128)(2,1)S(1)}, bf16[2,384,384]{2,1,0:T(8,128)(2,1)}, u32[]{:S(2)}, u32[]{:S(2)}) collective-permute-start(bf16[2,384,384]{2,1,0:T(8,128)(2,1)S(1)} %get-tuple-element.268), channel_id=1, source_target_pairs={{0,8},{8,0},{16,24},{24,16},{1,9},{9,1},{17,25},{25,17},{2,10},{10... | collective-permute-start | bytes 1769480 | tf_op jit(solution)/shard_map/ppermute | solution.py:624
  379.9 16.4 %collective-permute-start.22 = (bf16[2,384,384]{2,1,0:T(8,128)(2,1)}, bf16[2,384,384]{2,1,0:T(8,128)(2,1)S(1)}, u32[]{:S(2)}, u32[]{:S(2)}) collective-permute-start(bf16[2,384,384]{2,1,0:T(8,128)(2,1)} %get-tuple-element.263), channel_id=1, source_target_pairs={{0,16},{8,24},{16,0},{24,8},{1,17},{9,25},{17,1},{25,9},{2,18},{10... | collective-permute-start | bytes 1769480 | tf_op jit(solution)/shard_map/ppermute | solution.py:624
  381.7 16.4 %collective-permute-start.21 = (bf16[2,384,384]{2,1,0:T(8,128)(2,1)}, bf16[2,384,384]{2,1,0:T(8,128)(2,1)S(1)}, u32[]{:S(2)}, u32[]{:S(2)}) collective-permute-start(bf16[2,384,384]{2,1,0:T(8,128)(2,1)} %get-tuple-element.264), channel_id=1, source_target_pairs={{0,8},{8,0},{16,24},{24,16},{1,9},{9,1},{17,25},{25,17},{2,10},{10... | collective-permute-start | bytes 1769480 | tf_op jit(solution)/shard_map/ppermute | solution.py:624
  383.5 17.0 %collective-permute-start.19 = (bf16[384,384]{1,0:T(8,128)(2,1)S(1)}, bf16[384,384]{1,0:T(8,128)(2,1)S(1)}, u32[]{:S(2)}, u32[]{:S(2)}) collective-permute-start(bf16[384,384]{1,0:T(8,128)(2,1)S(1)} %slice_bitcast_fusion.12), channel_id=1, source_target_pairs={{0,16},{8,24},{16,0},{24,8},{1,17},{9,25},{17,1},{25,9},{2,18},{10... | collective-permute-start | bytes 884744 | tf_op jit(solution)/shard_map/ppermute | solution.py:624
  384.9 17.0 %collective-permute-start.20 = (bf16[384,384]{1,0:T(8,128)(2,1)S(1)}, bf16[384,384]{1,0:T(8,128)(2,1)S(1)}, u32[]{:S(2)}, u32[]{:S(2)}) collective-permute-start(bf16[384,384]{1,0:T(8,128)(2,1)S(1)} %slice_bitcast_fusion.11), channel_id=1, source_target_pairs={{0,8},{8,0},{16,24},{24,16},{1,9},{9,1},{17,25},{25,17},{2,10},{10... | collective-permute-start | bytes 884744 | tf_op jit(solution)/shard_map/ppermute | solution.py:624
  402.2 6.8 %collective-permute-start.24 = (bf16[384,384]{1,0:T(8,128)(2,1)S(1)}, bf16[384,384]{1,0:T(8,128)(2,1)S(1)}, u32[]{:S(2)}, u32[]{:S(2)}) collective-permute-start(bf16[384,384]{1,0:T(8,128)(2,1)S(1)} %slice_bitcast_fusion.6), channel_id=1, source_target_pairs={{0,8},{8,0},{16,24},{24,16},{1,9},{9,1},{17,25},{25,17},{2,10},{10... | collective-permute-start | bytes 884744 | tf_op jit(solution)/shard_map/ppermute | solution.py:624
  402.6 6.9 %collective-permute-start.23 = (bf16[384,384]{1,0:T(8,128)(2,1)S(1)}, bf16[384,384]{1,0:T(8,128)(2,1)S(1)}, u32[]{:S(2)}, u32[]{:S(2)}) collective-permute-start(bf16[384,384]{1,0:T(8,128)(2,1)S(1)} %slice_bitcast_fusion.8), channel_id=1, source_target_pairs={{0,16},{8,24},{16,0},{24,8},{1,17},{9,25},{17,1},{25,9},{2,18},{10... | collective-permute-start | bytes 884744 | tf_op jit(solution)/shard_map/ppermute | solution.py:624
  (24 other events, 176.5 us)
Sparse Core Ops, SparseCore 0:
  12.2 26.5 all-gather.4
  41.0 90.3 all-gather.6
  133.0 89.1 all-gather.8
  224.4 97.8 reduce-scatter.3
  324.4 83.7 reduce-scatter.5
  411.1 33.1 reduce-scatter.7

commit v6 on v5

--- a/solution.py
+++ b/solution.py
@@ -80,18 +80,14 @@
         def _():
             out[:, 0:width] = weight[...]
 
-    base = width
-    out[:, base : base + LANES] = jnp.zeros((rows, LANES), BF16)
     scratch[...] = jnp.zeros_like(scratch)
-    scratch[0:1, 0:rows] = gain1[...].astype(F32)
-    scratch[1:2, 0:rows] = gain2[...].astype(F32)
-    scratch[2:4, 0:rows] = vectors[...].astype(F32)
-    columns = scratch[...].T
-    n_router = router.shape[1]
-    n_mix = mix.shape[1]
-    out[:, base : base + n_router] = router[...]
-    out[:, base + n_router : base + n_router + n_mix] = mix[...]
-    out[:, base + 16 : base + 24] = columns[0:rows, 0:8].astype(BF16)
+    n_router = router.shape[0]
+    scratch[0:n_router, 0:rows] = router[...].astype(F32)
+    scratch[n_router : n_router + mix.shape[0], 0:rows] = mix[...].astype(F32)
+    scratch[16:17, 0:rows] = gain1[...].astype(F32)
+    scratch[17:18, 0:rows] = gain2[...].astype(F32)
+    scratch[18:20, 0:rows] = vectors[...].astype(F32)
+    out[:, width : width + LANES] = scratch[...].T[0:rows, :].astype(BF16)
 
 
 def slots_kernel(experts, capacity, stride, routes, order_row, order_col, dest_col, dest_row):
@@ -279,8 +275,8 @@
     sent = refs[:owners]
     weights = refs[owners : owners + 6]
     backs = refs[owners + 6 : 2 * owners + 6]
-    grads = refs[2 * owners + 6 : -4]
-    r_all, s_all, out_acc, row_acc = refs[-4:]
+    grads = refs[2 * owners + 6 : -5]
+    r_all, s_all, r_turned, out_acc, row_acc = refs[-5:]
     step = pl.program_id(0)
     steps = pl.num_programs(0)
     stride, width = sent[0].shape[1:]
@@ -291,6 +287,7 @@
         for k, ref in enumerate(sent):
             r_all[k * stride : (k + 1) * stride, :] = ref[0]
             s_all[k * stride : (k + 1) * stride, :] = ref[1]
+        r_turned[...] = r_all[...].T
         out_acc[...] = jnp.zeros_like(out_acc)
         row_acc[...] = jnp.zeros_like(row_acc)
 
@@ -315,10 +312,11 @@
     out_acc[...] += mm(hid, d)
     gate_g = (hidden_g * (up_pre * (sig + silu * (1.0 - sig)))).astype(BF16)
     up_g = (hidden_g * silu).astype(BF16)
-    row_acc[...] += mm_nt(gate_g, gate) + mm_nt(up_g, up)
+    both_g = jnp.concatenate([gate_g, up_g], axis=1)
+    row_acc[...] += mm_nt(both_g, jnp.concatenate([gate, up], axis=1))
     down_grad = mm_tn(hid, s).astype(BF16)
-    gate_grad = mm_tn(r, gate_g).astype(BF16)
-    up_grad = mm_tn(r, up_g).astype(BF16)
+    gate_grad = mm(r_turned[...], gate_g).astype(BF16)
+    up_grad = mm(r_turned[...], up_g).astype(BF16)
     even = core[0] == 0
     for i in range(2):
         tile = 2 * step + i
@@ -535,8 +533,9 @@
     dq = dq_acc[...] * (HEAD_DIM**-0.5)
     dq_out[...] = (dq * cosine[...] - half_swap(dq) * sine[...]).astype(BF16)
     columns = pl.ds(pl.multiple_of(step * LANES, LANES), LANES)
-    for j, part in enumerate((dq_out, dk_out, dv_out)):
-        grad_out[me[0] ^ j, :, columns] = mm(normed[...], part[...]).astype(BF16)
+    three = mm(normed[...], jnp.concatenate([dq_out[...], dk_out[...], dv_out[...]], axis=1))
+    for j in range(3):
+        grad_out[me[0] ^ j, :, columns] = three[:, j * LANES : (j + 1) * LANES].astype(BF16)
 
 
 def project_back_kernel(me, x, *refs):
@@ -610,14 +609,14 @@
         pack_kernel, "pack", (1,),
         [whole((shard_rows, width))] * 4
         + [whole((1, shard_rows))] * 2
-        + [whole((shard_rows, kinds)), whole((shard_rows, 4)), whole((2, shard_rows))],
+        + [whole((kinds, shard_rows)), whole((4, shard_rows)), whole((2, shard_rows))],
         whole((shard_rows, packed_width)),
         struct((shard_rows, packed_width), BF16),
-        scratch=[pltpu.VMEM((8, LANES), F32)],
+        scratch=[pltpu.VMEM((LANES, LANES), F32)],
         traffic=1 << 20, prefetch=1,
     )(
         me, query_weight, key_weight, value_weight, output_weight, first_gain[None], second_gain[None],
-        router_weight, constant_mix, constant_vectors,
+        router_weight.T, constant_mix.T, constant_vectors,
     )
 
     def send(part, k):
@@ -754,7 +753,8 @@
             [pair] * owners + weights,
             [pair] * owners + [whole(g) for g in grad_shapes],
             [pair_shape] * owners + [struct(g, BF16) for g in grad_shapes],
-            scratch=[pltpu.VMEM((local, width), BF16)] * 2 + [pltpu.VMEM((local, width), F32)] * 2,
+            scratch=[pltpu.VMEM((local, width), BF16)] * 2 + [pltpu.VMEM((width, local), BF16)]
+            + [pltpu.VMEM((local, width), F32)] * 2,
             flops=16 * local * width * ff, traffic=24 << 20, trans=local * ff, prefetch=1,
         )(core, *rows, gate_up, gate_up, gate_up, gate_up, down, down)
         grads = outs[owners:]
@@ -867,8 +867,11 @@
     quarter = jnp.concatenate(quarters + [small_grad], axis=1)
     quarter, expert_sums = lax.optimization_barrier((quarter, expert_sums))
     quarter = lax.psum_scatter(quarter, "shard", scatter_dimension=0, tiled=True)
-    gathered = lax.all_gather(quarter, "expert", axis=0, tiled=False).astype(F32)
-    dense = gathered[:, :, :width]
+    gathered = jnp.stack([quarter] + [send(quarter, k) for k in range(1, owners)]).astype(F32)
+    dense = [
+        lax.dynamic_index_in_dim(gathered[:, :, :width], me[0] ^ j, keepdims=False)
+        for j in range(4)
+    ]
     small = jnp.sum(gathered[:, :, width:], axis=0)
     if aligned:
         out_shapes = [w.shape for w in (gate_weight, up_weight, down_weight)]

time: 476 us -> 472 us (level)
  blocking collectives: 11.6 us -> 0 us
  waiting for transfers between devices: 133 us -> 142 us
    all_gather x1 -> x0, blocking collectives: 11.6 us -> none  [body(): lax.all_gather(quarter, 'expert', axis=0, tiled=False).astype(F32)]
    reduce_scatter x1, waiting for transfers between devices: 28.5 us -> 36.5 us  [body(): lax.psum_scatter(quarter, 'shard', scatter_dimension=0, tiled=True)]
    ppermute x12 -> x15, starting transfers between devices: 14.2 us -> 17.4 us  [send(): return lax.ppermute(part, 'expert', [(i, i ^ k) for i in range(owners)])]
    ppermute x12 -> x15, waiting for transfers between devices: 34.6 us -> 34.8 us  [send(): return lax.ppermute(part, 'expert', [(i, i ^ k) for i in range(owners)])]
  transfers between devices with their start and end apart: 31 -> 34, of which waited for: 19 -> 19; matrix products, arithmetic and copies ran while one was open for 6% -> 6% of each run, Pallas kernels for 51% -> 51%
where the time goes in v6:
time: 472 us; the launch traced here: 463 us
  Pallas kernels  240 us (51%)
  waiting for transfers between devices  142 us (30%)
  starting transfers between devices  31.1 us (7%)
  local copies, waits for them, and re-layouts  18.2 us (4%)
  other arithmetic  16.1 us (3%)
  between operations  15.5 us (3%)
    pallas_call x2, Pallas kernels, run_expert(): call(functools.partial(expert_kernel, owners, aligned, halves), 'expert',...  62.6 us
    pallas_call x2, Pallas kernels, body(): call(functools.partial(attend_back_kernel, start), 'attend_back', (pairs,...  57.6 us
    ppermute x12, waiting for transfers between devices, exchange(): lax.ppermute(part, 'expert', [(i, i ^ k) for i in range(owners)])  43.2 us
    pallas_call x1, Pallas kernels, body(): call(attend_kernel, 'attend', (steps,), [wide, whole((count, width)), who...  39.2 us
    reduce_scatter x1, waiting for transfers between devices, body(): lax.psum_scatter(quarter, 'shard', scatter_dimension=0, tiled=True)  36.5 us
    ppermute x15, waiting for transfers between devices, send(): return lax.ppermute(part, 'expert', [(i, i ^ k) for i in range(owners)])  34.8 us
    pallas_call x1, Pallas kernels, body(): call(functools.partial(combine_kernel, experts, owners, local_experts), '...  27.6 us
    all_gather x1, waiting for transfers between devices, body(): own = lax.all_gather(packed, 'shard', axis=0, tiled=True)  22.7 us
  transfers between devices with their start and end apart: 34, of which 19 were waited for; matrix products, arithmetic and copies ran while one was open for 6% of the time, Pallas kernels for 51%

profile of v6, /device:TPU:0, one launch (start us, length us, event | category | flops | bytes accessed | tf_op | source)
XLA Modules:
  0.0 462.9 jit_solution(18209680765391856202)
XLA Ops:
  7.2 2.0 pack.1
  9.3 2.3 pack_expert.2
  11.7 2.3 pack_expert.3
  14.1 22.7 %all-gather.4.cloned.1.call-done.small = bf16[768,896]{1,0:T(8,128)(2,1)} async-done(((bf16[96,896]{1,0:T(8,128)(2,1)}), bf16[768,896]{1,0:T(8,128)(2,1)}) %all-gather.4.cloned.1.call-update) | async-done | bytes 1376272 | tf_op jit(solution)/shard_map/all_gather | solution.py:630
  41.1 12.5 %collective-permute-done.2 = bf16[1,384,768]{2,1,0:T(8,128)(2,1)S(1)} collective-permute-done((bf16[1,384,768]{2,1,0:T(8,128)(2,1)S(1)}, bf16[1,384,768]{2,1,0:T(8,128)(2,1)S(1)}, u32[]{:S(2)}, u32[]{:S(2)}) %collective-permute-start.2) | collective-permute-done | bytes 589856 | tf_op jit(solution)/shard_map/ppermute | solution.py:623
  63.5 6.9 %slots.1 = (s32[1024,128]{1,0:T(8,128)}, s32[8,1024]{1,0:T(8,128)}) custom-call(s32[1024,2]{1,0:T(8,128)} %copy.65.routes.refs_12_, s32[1,1024]{1,0:T(1,128)} %order_row.1, s32[1024,1]{1,0:T(8,128)} %copy.67.order_col), custom_call_target="tpu_custom_call" | custom-call | flops 805306368 | bytes 1048576 | tf_op jit(solution)/shard_map/slots/pallas_call | solution.py:670
  72.1 10.3 %collective-permute-done.3 = bf16[2,384,768]{2,1,0:T(8,128)(2,1)} collective-permute-done((bf16[2,384,768]{2,1,0:T(8,128)(2,1)}, bf16[2,384,768]{2,1,0:T(8,128)(2,1)}, u32[]{:S(2)}, u32[]{:S(2)}) %collective-permute-start.3) | collective-permute-done | bytes 1179680 | tf_op jit(solution)/shard_map/ppermute | solution.py:623
  84.6 2.7 maximum_maximum_fusion.wq.wk.wv.wo.refs_15_.refs_7_.refs_8_.refs_9_
  87.3 8.6 %project.1 = (bf16[1024,768]{1,0:T(8,128)(2,1)}, bf16[1024,768]{1,0:T(8,128)(2,1)}, bf16[1024,768]{1,0:T(8,128)(2,1)}, bf16[768,1024]{1,0:T(8,128)(2,1)}, f32[128,768]{1,0:T(8,128)}) custom-call(s32[1]{0:T(128)} %bitcast.me, bf16[1024,768]{1,0:T(8,128)(2,1)} %x.5, bf16[4,768,768]{2,1,0:T(8,128)(2,1)} %maximum_maximum_fusion.wq.wk.wv.wo.refs_15_.refs_7_.refs_8_.refs_9_, ...), custom_call_target="tpu_custom_call" | custom-call | flops 3623878656 | bytes 12582912 | tf_op jit(solution)/shard_map/project/pallas_call | solution.py:688
  95.9 39.2 %attend.1 = (bf16[1024,768]{1,0:T(8,128)(2,1)}, f32[16,1024]{1,0:T(8,128)}, f32[1024,768]{1,0:T(8,128)}, bf16[1024,768]{1,0:T(8,128)(2,1)}, f32[1024,128]{1,0:T(8,128)}) custom-call(s32[1]{0:T(128)} %bitcast.me, s32[1]{0:T(128)S(6)} %copy.75.prefix, bf16[1024,768]{1,0:T(8,128)(2,1)} %get-tuple-element.112.q, bf16[1024,768]{1,0:T(8,128)(2,1)} %get-tuple-element.113.k, ...), custom_call_target="tpu_custom_call" | custom-call | flops 32212254720 | bytes 16777216 | tf_op jit(solution)/shard_map/attend/pallas_call | solution.py:696
  135.1 8.3 %dispatch.2 = (bf16[2,176,768]{2,1,0:T(8,128)(2,1)}, bf16[2,176,768]{2,1,0:T(8,128)(2,1)}, bf16[2,176,768]{2,1,0:T(8,128)(2,1)}, bf16[2,176,768]{2,1,0:T(8,128)(2,1)}) custom-call(s32[1]{0:T(128)} %bitcast.me, bf16[1024,768]{1,0:T(8,128)(2,1)} %get-tuple-element.116.normed.refs_9_, bf16[1024,768]{1,0:T(8,128)(2,1)} %refs_10_.1, ...), custom_call_target="tpu_custom_call" | custom-call | flops 2214592512 | bytes 6291456 | tf_op jit(solution)/shard_map/dispatch/pallas_call | solution.py:719
  147.0 7.9 %dispatch.3 = (bf16[2,176,768]{2,1,0:T(8,128)(2,1)}, bf16[2,176,768]{2,1,0:T(8,128)(2,1)}, bf16[2,176,768]{2,1,0:T(8,128)(2,1)}, bf16[2,176,768]{2,1,0:T(8,128)(2,1)}) custom-call(s32[1]{0:T(128)} %bitcast.me, bf16[1024,768]{1,0:T(8,128)(2,1)} %get-tuple-element.116.normed.refs_9_, bf16[1024,768]{1,0:T(8,128)(2,1)} %refs_10_.1, ...), custom_call_target="tpu_custom_call" | custom-call | flops 2214592512 | bytes 6291456 | tf_op jit(solution)/shard_map/dispatch/pallas_call | solution.py:719
  156.6 2.2 collective-permute-done.4.refs_1_
  160.0 8.5 %collective-permute-done.5.refs_2_ = bf16[2,176,768]{2,1,0:T(8,128)(2,1)S(1)} collective-permute-done((bf16[2,176,768]{2,1,0:T(8,128)(2,1)}, bf16[2,176,768]{2,1,0:T(8,128)(2,1)S(1)}, u32[]{:S(2)}, u32[]{:S(2)}) %collective-permute-start.5) | collective-permute-done | bytes 540704 | tf_op jit(solution)/shard_map/ppermute | solution.py:711
  168.5 2.8 collective-permute-done.6.refs_3_
  172.1 30.9 %expert.2 = (bf16[2,176,768]{2,1,0:T(8,128)(2,1)}, bf16[2,176,768]{2,1,0:T(8,128)(2,1)}, bf16[2,176,768]{2,1,0:T(8,128)(2,1)}, bf16[2,176,768]{2,1,0:T(8,128)(2,1)}, bf16[8,2304,256]{2,1,0:T(8,128)(2,1)}) custom-call(s32[1]{0:T(128)} %bitcast.1.core, bf16[2,176,768]{2,1,0:T(8,128)(2,1)} %get-tuple-element.127.refs_0_, bf16[2,176,768]{2,1,0:T(8,128)(2,1)} %copy-done.18, ...), custom_call_target="tpu_custom_call" | custom-call | flops 17716740096 | bytes 25165824 | tf_op jit(solution)/shard_map/expert/pallas_call | solution.py:751
  207.6 11.2 %collective-permute-done.10.refs_1_ = bf16[2,176,768]{2,1,0:T(8,128)(2,1)S(1)} collective-permute-done((bf16[2,176,768]{2,1,0:T(8,128)(2,1)}, bf16[2,176,768]{2,1,0:T(8,128)(2,1)S(1)}, u32[]{:S(2)}, u32[]{:S(2)}) %collective-permute-start.10) | collective-permute-done | bytes 540704 | tf_op jit(solution)/shard_map/ppermute | solution.py:711
  218.8 6.5 %collective-permute-done.11.refs_2_ = bf16[2,176,768]{2,1,0:T(8,128)(2,1)S(1)} collective-permute-done((bf16[2,176,768]{2,1,0:T(8,128)(2,1)S(1)}, bf16[2,176,768]{2,1,0:T(8,128)(2,1)S(1)}, u32[]{:S(2)}, u32[]{:S(2)}) %collective-permute-start.11) | collective-permute-done | bytes 540704 | tf_op jit(solution)/shard_map/ppermute | solution.py:711
  225.3 31.8 %expert.3 = (bf16[2,176,768]{2,1,0:T(8,128)(2,1)}, bf16[2,176,768]{2,1,0:T(8,128)(2,1)}, bf16[2,176,768]{2,1,0:T(8,128)(2,1)}, bf16[2,176,768]{2,1,0:T(8,128)(2,...) custom-call(s32[1]{0:T(128)} %bitcast.1.core, bf16[2,176,768]{2,1,0:T(8,128)(2,1)} %get-tuple-element.144.refs_0_, ...), custom_call_target="tpu_custom_call" | custom-call | flops 17716740096 | bytes 25165824 | tf_op jit(solution)/shard_map/expert/pallas_call | solution.py:751
  260.7 5.0 %collective-permute-done.16 = bf16[4,2304,256]{2,1,0:T(8,128)(2,1)S(1)} collective-permute-done((bf16[4,2304,256]{2,1,0:T(8,128)(2,1)}, bf16[4,2304,256]{2,1,0:T(8,128)(2,1)S(1)}, u32[]{:S(2)}, u32[]{:S(2)}) %collective-permute-start.16) | collective-permute-done | bytes 4718624 | tf_op jit(solution)/shard_map/ppermute | solution.py:773
  265.7 5.9 %add_convert_fusion = bf16[4,2304,256]{2,1,0:T(8,128)(2,1)} fusion(bf16[4,2304,256]{2,1,0:T(8,128)(2,1)S(1)} %collective-permute-done.16, bf16[4,2304,256]{2,1,0:T(8,128)(2,1)} %get-tuple-element.152), kind=kLoop, calls=%fused_computation | loop fusion | flops 9437184 | bytes 14155776 | tf_op jit(solution)/shard_map/convert_element_type | solution.py:626
  272.6 11.1 %collective-permute-done.14.refs_6_ = bf16[2,176,768]{2,1,0:T(8,128)(2,1)S(1)} collective-permute-done((bf16[2,176,768]{2,1,0:T(8,128)(2,1)}, bf16[2,176,768]{2,1,0:T(8,128)(2,1)S(1)}, u32[]{:S(2)}, u32[]{:S(2)}) %collective-permute-start.14) | collective-permute-done | bytes 540704 | tf_op jit(solution)/shard_map/ppermute | solution.py:711
  284.7 27.6 %combine.1 = (bf16[1024,768]{1,0:T(8,128)(2,1)}, f32[1024,12]{1,0:T(8,128)}, f32[1024,768]{1,0:T(8,128)}, bf16[1024,768]{1,0:T(8,128)(2,1)}, f32[16,1024]{1,0:T(...) custom-call(s32[1]{0:T(128)} %bitcast.me, bf16[2,176,768]{2,1,0:T(8,128)(2,1)} %get-tuple-element.140.refs_0_, ...), custom_call_target="tpu_custom_call" | custom-call | flops 9059696640 | bytes 25165824 | tf_op jit(solution)/shard_map/combine/pallas_call | solution.py:798
  312.2 28.7 %attend_back.2 = (bf16[1024,384]{1,0:T(8,128)(2,1)}, bf16[1024,384]{1,0:T(8,128)(2,1)}, bf16[1024,384]{1,0:T(8,128)(2,1)}, bf16[4,768,384]{2,1,0:T(8,128)(2,1)}) custom-call(s32[1]{0:T(128)} %bitcast.me, s32[1]{0:T(128)S(6)} %copy.75.prefix, bf16[1024,768]{1,0:T(8,128)(2,1)} %get-tuple-element.112.q, bf16[1024,768]{1,0:T(8,128)(2,1)} %get-tuple-element.113.k, ...), custom_call_target="tpu_custom_call" | custom-call | flops 32212254720 | bytes 6291456 | tf_op jit(solution)/shard_map/attend_back/pallas_call | solution.py:832
  344.3 28.8 %attend_back.3 = (bf16[1024,384]{1,0:T(8,128)(2,1)}, bf16[1024,384]{1,0:T(8,128)(2,1)}, bf16[1024,384]{1,0:T(8,128)(2,1)}, bf16[4,768,384]{2,1,0:T(8,128)(2,1)}) custom-call(s32[1]{0:T(128)} %bitcast.me, s32[1]{0:T(128)S(6)} %copy.75.prefix, bf16[1024,768]{1,0:T(8,128)(2,1)} %get-tuple-element.112.q, bf16[1024,768]{1,0:T(8,128)(2,1)} %get-tuple-element.113.k, ...), custom_call_target="tpu_custom_call" | custom-call | flops 32212254720 | bytes 6291456 | tf_op jit(solution)/shard_map/attend_back/pallas_call | solution.py:832
  373.2 2.5 fusion.4
  381.5 10.4 %project_back.1 = (f32[1024,768]{1,0:T(8,128)}, bf16[768,128]{1,0:T(8,128)(2,1)}) custom-call(s32[1]{0:T(128)} %bitcast.me, bf16[1024,768]{1,0:T(8,128)(2,1)} %x.5, bf16[1024,384]{1,0:T(8,128)(2,1)} %get-tuple-element.167.refs_0_, bf16[1024,384]{1,0:T(8,128)(2,1)} %get-tuple-element.168.refs_1_, bf16[1024,384]{1,0:T(8,128)(2,1)} %get-tuple-element.169.refs_2_, ...), custom_call_target="tpu_custom_call" | custom-call | flops 3623878656 | bytes 18874368 | tf_op jit(solution)/shard_map/project_back/pallas_call | solution.py:855
  393.5 4.1 collective-permute-done.19
  400.0 4.9 %collective-permute-done.24 = bf16[384,384]{1,0:T(8,128)(2,1)S(1)} collective-permute-done((bf16[384,384]{1,0:T(8,128)(2,1)S(1)}, bf16[384,384]{1,0:T(8,128)(2,1)S(1)}, u32[]{:S(2)}, u32[]{:S(2)}) %collective-permute-start.24) | collective-permute-done | bytes 294944 | tf_op jit(solution)/shard_map/ppermute | solution.py:623
  406.6 36.5 %reduce-scatter.8.cloned.1.call-done = bf16[96,896]{1,0:T(8,128)(2,1)} async-done(((bf16[768,896]{1,0:T(8,128)(2,1)}), bf16[96,896]{1,0:T(8,128)(2,1)}) %reduce-scatter.8.cloned.1.call-update) | async-done | bytes 172048 | tf_op jit(solution)/shard_map/reduce_scatter | solution.py:869
  443.1 2.2 collective-permute-start.27
  447.4 3.9 unpack.1
  (143 shorter events, 56.1 us)
Async XLA Ops:
  7.2 29.6 %all-gather.4.cloned.1.call-start = ((), (), s32[]{:S(2)}) async-start(), calls=%async_computation.3 | async-start | bytes 1548288 | tf_op jit(solution)/shard_map/all_gather | solution.py:630
  9.2 162.1 %all-gather.6.cloned.1.call-start = ((), (), s32[]{:S(2)}) async-start(), calls=%async_computation.4 | async-start | bytes 10616832 | tf_op jit(solution)/shard_map/all_gather | solution.py:655
  11.6 213.7 %all-gather.8.cloned.1.call-start = ((), (), s32[]{:S(2)}) async-start(), calls=%async_computation.5 | async-start | bytes 10616832 | tf_op jit(solution)/shard_map/all_gather | solution.py:655
  14.0 363.8 %reduce-scatter.4.cloned.1.call-start = ((), (), s32[]{:S(2)}) async-start(), calls=%async_computation.6 | async-start | bytes 10616832 | tf_op jit(solution)/shard_map/reduce_scatter | solution.py:778
  38.1 15.5 %collective-permute-start.2 = (bf16[1,384,768]{2,1,0:T(8,128)(2,1)S(1)}, bf16[1,384,768]{2,1,0:T(8,128)(2,1)S(1)}, u32[]{:S(2)}, u32[]{:S(2)}) collective-permute-start(bf16[1,384,768]{2,1,0:T(8,128)(2,1)S(1)} %get-tuple-element.270), channel_id=1, source_target_pairs={{0,16},{8,24},{16,0},{24,8},{1,17},{9,25},{17,1},{25,9},{2,18},{10... | collective-permute-start | bytes 1769480 | tf_op jit(solution)/shard_map/ppermute | solution.py:623
  39.7 16.6 %collective-permute-start = (bf16[1,384,768]{2,1,0:T(8,128)(2,1)S(1)}, bf16[1,384,768]{2,1,0:T(8,128)(2,1)S(1)}, u32[]{:S(2)}, u32[]{:S(2)}) collective-permute-start(bf16[1,384,768]{2,1,0:T(8,128)(2,1)S(1)} %get-tuple-element.269), channel_id=1, source_target_pairs={{0,8},{8,0},{16,24},{24,16},{1,9},{9,1},{17,25},{25,17},{2,10},{10... | collective-permute-start | bytes 1769480 | tf_op jit(solution)/shard_map/ppermute | solution.py:623
  54.8 27.7 %collective-permute-start.3 = (bf16[2,384,768]{2,1,0:T(8,128)(2,1)}, bf16[2,384,768]{2,1,0:T(8,128)(2,1)}, u32[]{:S(2)}, u32[]{:S(2)}) collective-permute-start(bf16[2,384,768]{2,1,0:T(8,128)(2,1)} %pad_maximum_fusion.2), channel_id=1, source_target_pairs={{0,8},{8,0},{16,24},{24,16},{1,9},{9,1},{17,25},{25,17},{2,10},{10... | collective-permute-start | bytes 3538952 | tf_op jit(solution)/shard_map/ppermute | solution.py:623
  57.4 27.3 %collective-permute-start.1 = (bf16[2,384,768]{2,1,0:T(8,128)(2,1)}, bf16[2,384,768]{2,1,0:T(8,128)(2,1)S(1)}, u32[]{:S(2)}, u32[]{:S(2)}) collective-permute-start(bf16[2,384,768]{2,1,0:T(8,128)(2,1)} %pad_maximum_fusion.1), channel_id=1, source_target_pairs={{0,16},{8,24},{16,0},{24,8},{1,17},{9,25},{17,1},{25,9},{2,18},{10... | collective-permute-start | bytes 3538952 | tf_op jit(solution)/shard_map/ppermute | solution.py:623
  143.5 15.4 %collective-permute-start.4 = (bf16[2,176,768]{2,1,0:T(8,128)(2,1)}, bf16[2,176,768]{2,1,0:T(8,128)(2,1)S(1)}, u32[]{:S(2)}, u32[]{:S(2)}) collective-permute-start(bf16[2,176,768]{2,1,0:T(8,128)(2,1)} %get-tuple-element.120), channel_id=1, source_target_pairs={{0,8},{8,0},{16,24},{24,16},{1,9},{9,1},{17,25},{25,17},{2,10},{10... | collective-permute-start | bytes 1622024 | tf_op jit(solution)/shard_map/ppermute | solution.py:711
  143.7 24.8 %collective-permute-start.5 = (bf16[2,176,768]{2,1,0:T(8,128)(2,1)}, bf16[2,176,768]{2,1,0:T(8,128)(2,1)S(1)}, u32[]{:S(2)}, u32[]{:S(2)}) collective-permute-start(bf16[2,176,768]{2,1,0:T(8,128)(2,1)} %get-tuple-element.121), channel_id=1, source_target_pairs={{0,16},{8,24},{16,0},{24,8},{1,17},{9,25},{17,1},{25,9},{2,18},{10... | collective-permute-start | bytes 1622024 | tf_op jit(solution)/shard_map/ppermute | solution.py:711
  145.2 26.1 %collective-permute-start.6 = (bf16[2,176,768]{2,1,0:T(8,128)(2,1)}, bf16[2,176,768]{2,1,0:T(8,128)(2,1)S(1)}, u32[]{:S(2)}, u32[]{:S(2)}) collective-permute-start(bf16[2,176,768]{2,1,0:T(8,128)(2,1)} %get-tuple-element.122), channel_id=1, source_target_pairs={{0,24},{8,16},{16,8},{24,0},{1,25},{9,17},{17,9},{25,1},{2,26},{10... | collective-permute-start | bytes 1622024 | tf_op jit(solution)/shard_map/ppermute | solution.py:711
  154.8 48.2 %collective-permute-start.7 = (bf16[2,176,768]{2,1,0:T(8,128)(2,1)}, bf16[2,176,768]{2,1,0:T(8,128)(2,1)S(1)}, u32[]{:S(2)}, u32[]{:S(2)}) collective-permute-start(bf16[2,176,768]{2,1,0:T(8,128)(2,1)} %get-tuple-element.124), channel_id=1, source_target_pairs={{0,8},{8,0},{16,24},{24,16},{1,9},{9,1},{17,25},{25,17},{2,10},{10... | collective-permute-start | bytes 1622024 | tf_op jit(solution)/shard_map/ppermute | solution.py:711
  155.1 47.9 %collective-permute-start.8 = (bf16[2,176,768]{2,1,0:T(8,128)(2,1)}, bf16[2,176,768]{2,1,0:T(8,128)(2,1)S(1)}, u32[]{:S(2)}, u32[]{:S(2)}) collective-permute-start(bf16[2,176,768]{2,1,0:T(8,128)(2,1)} %get-tuple-element.125), channel_id=1, source_target_pairs={{0,16},{8,24},{16,0},{24,8},{1,17},{9,25},{17,1},{25,9},{2,18},{10... | collective-permute-start | bytes 1622024 | tf_op jit(solution)/shard_map/ppermute | solution.py:711
  158.8 44.2 %collective-permute-start.9 = (bf16[2,176,768]{2,1,0:T(8,128)(2,1)}, bf16[2,176,768]{2,1,0:T(8,128)(2,1)S(1)}, u32[]{:S(2)}, u32[]{:S(2)}) collective-permute-start(bf16[2,176,768]{2,1,0:T(8,128)(2,1)} %get-tuple-element.126), channel_id=1, source_target_pairs={{0,24},{8,16},{16,8},{24,0},{1,25},{9,17},{17,9},{25,1},{2,26},{10... | collective-permute-start | bytes 1622024 | tf_op jit(solution)/shard_map/ppermute | solution.py:711
  204.1 202.5 %reduce-scatter.6.cloned.1.call-start = ((), (), s32[]{:S(2)}) async-start(), calls=%async_computation.7 | async-start | bytes 5898240 | tf_op jit(solution)/shard_map/reduce_scatter | solution.py:778
  204.1 14.7 %collective-permute-start.10 = (bf16[2,176,768]{2,1,0:T(8,128)(2,1)}, bf16[2,176,768]{2,1,0:T(8,128)(2,1)S(1)}, u32[]{:S(2)}, u32[]{:S(2)}) collective-permute-start(bf16[2,176,768]{2,1,0:T(8,128)(2,1)} %get-tuple-element.137), channel_id=1, source_target_pairs={{0,8},{8,0},{16,24},{24,16},{1,9},{9,1},{17,25},{25,17},{2,10},{10... | collective-permute-start | bytes 1622024 | tf_op jit(solution)/shard_map/ppermute | solution.py:711
  204.5 20.8 %collective-permute-start.11 = (bf16[2,176,768]{2,1,0:T(8,128)(2,1)S(1)}, bf16[2,176,768]{2,1,0:T(8,128)(2,1)S(1)}, u32[]{:S(2)}, u32[]{:S(2)}) collective-permute-start(bf16[2,176,768]{2,1,0:T(8,128)(2,1)S(1)} %copy-done.25), channel_id=1, source_target_pairs={{0,16},{8,24},{16,0},{24,8},{1,17},{9,25},{17,1},{25,9},{2,18},{10... | collective-permute-start | bytes 1622024 | tf_op jit(solution)/shard_map/ppermute | solution.py:711
  205.9 19.3 %collective-permute-start.12 = (bf16[2,176,768]{2,1,0:T(8,128)(2,1)S(1)}, bf16[2,176,768]{2,1,0:T(8,128)(2,1)S(1)}, u32[]{:S(2)}, u32[]{:S(2)}) collective-permute-start(bf16[2,176,768]{2,1,0:T(8,128)(2,1)S(1)} %copy-done.24), channel_id=1, source_target_pairs={{0,24},{8,16},{16,8},{24,0},{1,25},{9,17},{17,9},{25,1},{2,26},{10... | collective-permute-start | bytes 1622024 | tf_op jit(solution)/shard_map/ppermute | solution.py:711
  257.1 8.6 %collective-permute-start.16 = (bf16[4,2304,256]{2,1,0:T(8,128)(2,1)}, bf16[4,2304,256]{2,1,0:T(8,128)(2,1)S(1)}, u32[]{:S(2)}, u32[]{:S(2)}) collective-permute-start(bf16[4,2304,256]{2,1,0:T(8,128)(2,1)} %get-tuple-element.153), channel_id=1, source_target_pairs={{0,1},{1,0},{2,3},{3,2},{4,5},{5,4},{6,7},{7,6},{8,9},{9,8},{10,11... | collective-permute-start | bytes 14155784 | tf_op jit(solution)/shard_map/ppermute | solution.py:773
  257.2 15.4 %collective-permute-start.13 = (bf16[2,176,768]{2,1,0:T(8,128)(2,1)}, bf16[2,176,768]{2,1,0:T(8,128)(2,1)S(1)}, u32[]{:S(2)}, u32[]{:S(2)}) collective-permute-start(bf16[2,176,768]{2,1,0:T(8,128)(2,1)} %get-tuple-element.149), channel_id=1, source_target_pairs={{0,8},{8,0},{16,24},{24,16},{1,9},{9,1},{17,25},{25,17},{2,10},{10... | collective-permute-start | bytes 1622024 | tf_op jit(solution)/shard_map/ppermute | solution.py:711
  257.5 26.1 %collective-permute-start.14 = (bf16[2,176,768]{2,1,0:T(8,128)(2,1)}, bf16[2,176,768]{2,1,0:T(8,128)(2,1)S(1)}, u32[]{:S(2)}, u32[]{:S(2)}) collective-permute-start(bf16[2,176,768]{2,1,0:T(8,128)(2,1)} %get-tuple-element.150), channel_id=1, source_target_pairs={{0,16},{8,24},{16,0},{24,8},{1,17},{9,25},{17,1},{25,9},{2,18},{10... | collective-permute-start | bytes 1622024 | tf_op jit(solution)/shard_map/ppermute | solution.py:711
  258.8 24.8 %collective-permute-start.15 = (bf16[2,176,768]{2,1,0:T(8,128)(2,1)}, bf16[2,176,768]{2,1,0:T(8,128)(2,1)S(1)}, u32[]{:S(2)}, u32[]{:S(2)}) collective-permute-start(bf16[2,176,768]{2,1,0:T(8,128)(2,1)} %get-tuple-element.151), channel_id=1, source_target_pairs={{0,24},{8,16},{16,8},{24,0},{1,25},{9,17},{17,9},{25,1},{2,26},{10... | collective-permute-start | bytes 1622024 | tf_op jit(solution)/shard_map/ppermute | solution.py:711
  284.6 158.5 %reduce-scatter.8.cloned.1.call-start = ((), (), s32[]{:S(2)}) async-start(), calls=%async_computation.8 | async-start | bytes 1548288 | tf_op jit(solution)/shard_map/reduce_scatter | solution.py:869
  342.3 35.5 %collective-permute-start.17 = (bf16[2,384,384]{2,1,0:T(8,128)(2,1)S(1)}, bf16[2,384,384]{2,1,0:T(8,128)(2,1)}, u32[]{:S(2)}, u32[]{:S(2)}) collective-permute-start(bf16[2,384,384]{2,1,0:T(8,128)(2,1)S(1)} %get-tuple-element.268), channel_id=1, source_target_pairs={{0,8},{8,0},{16,24},{24,16},{1,9},{9,1},{17,25},{25,17},{2,10},{10... | collective-permute-start | bytes 1769480 | tf_op jit(solution)/shard_map/ppermute | solution.py:623
  344.1 33.8 %collective-permute-start.18 = (bf16[2,384,384]{2,1,0:T(8,128)(2,1)S(1)}, bf16[2,384,384]{2,1,0:T(8,128)(2,1)}, u32[]{:S(2)}, u32[]{:S(2)}) collective-permute-start(bf16[2,384,384]{2,1,0:T(8,128)(2,1)S(1)} %get-tuple-element.267), channel_id=1, source_target_pairs={{0,16},{8,24},{16,0},{24,8},{1,17},{9,25},{17,1},{25,9},{2,18},{10... | collective-permute-start | bytes 1769480 | tf_op jit(solution)/shard_map/ppermute | solution.py:623
  375.7 16.4 %collective-permute-start.21 = (bf16[2,384,384]{2,1,0:T(8,128)(2,1)}, bf16[2,384,384]{2,1,0:T(8,128)(2,1)S(1)}, u32[]{:S(2)}, u32[]{:S(2)}) collective-permute-start(bf16[2,384,384]{2,1,0:T(8,128)(2,1)} %get-tuple-element.264), channel_id=1, source_target_pairs={{0,8},{8,0},{16,24},{24,16},{1,9},{9,1},{17,25},{25,17},{2,10},{10... | collective-permute-start | bytes 1769480 | tf_op jit(solution)/shard_map/ppermute | solution.py:623
  377.1 16.4 %collective-permute-start.22 = (bf16[2,384,384]{2,1,0:T(8,128)(2,1)}, bf16[2,384,384]{2,1,0:T(8,128)(2,1)S(1)}, u32[]{:S(2)}, u32[]{:S(2)}) collective-permute-start(bf16[2,384,384]{2,1,0:T(8,128)(2,1)} %get-tuple-element.263), channel_id=1, source_target_pairs={{0,16},{8,24},{16,0},{24,8},{1,17},{9,25},{17,1},{25,9},{2,18},{10... | collective-permute-start | bytes 1769480 | tf_op jit(solution)/shard_map/ppermute | solution.py:623
  379.5 18.1 %collective-permute-start.19 = (bf16[384,384]{1,0:T(8,128)(2,1)S(1)}, bf16[384,384]{1,0:T(8,128)(2,1)S(1)}, u32[]{:S(2)}, u32[]{:S(2)}) collective-permute-start(bf16[384,384]{1,0:T(8,128)(2,1)S(1)} %slice_bitcast_fusion.8), channel_id=1, source_target_pairs={{0,16},{8,24},{16,0},{24,8},{1,17},{9,25},{17,1},{25,9},{2,18},{10... | collective-permute-start | bytes 884744 | tf_op jit(solution)/shard_map/ppermute | solution.py:623
  380.8 16.8 %collective-permute-start.20 = (bf16[384,384]{1,0:T(8,128)(2,1)S(1)}, bf16[384,384]{1,0:T(8,128)(2,1)S(1)}, u32[]{:S(2)}, u32[]{:S(2)}) collective-permute-start(bf16[384,384]{1,0:T(8,128)(2,1)S(1)} %slice_bitcast_fusion.7), channel_id=1, source_target_pairs={{0,8},{8,0},{16,24},{24,16},{1,9},{9,1},{17,25},{25,17},{2,10},{10... | collective-permute-start | bytes 884744 | tf_op jit(solution)/shard_map/ppermute | solution.py:623
  397.9 7.0 %collective-permute-start.24 = (bf16[384,384]{1,0:T(8,128)(2,1)S(1)}, bf16[384,384]{1,0:T(8,128)(2,1)S(1)}, u32[]{:S(2)}, u32[]{:S(2)}) collective-permute-start(bf16[384,384]{1,0:T(8,128)(2,1)S(1)} %slice_bitcast_fusion.2), channel_id=1, source_target_pairs={{0,8},{8,0},{16,24},{24,16},{1,9},{9,1},{17,25},{25,17},{2,10},{10... | collective-permute-start | bytes 884744 | tf_op jit(solution)/shard_map/ppermute | solution.py:623
  398.5 6.8 %collective-permute-start.23 = (bf16[384,384]{1,0:T(8,128)(2,1)S(1)}, bf16[384,384]{1,0:T(8,128)(2,1)S(1)}, u32[]{:S(2)}, u32[]{:S(2)}) collective-permute-start(bf16[384,384]{1,0:T(8,128)(2,1)S(1)} %slice_bitcast_fusion.4), channel_id=1, source_target_pairs={{0,16},{8,24},{16,0},{24,8},{1,17},{9,25},{17,1},{25,9},{2,18},{10... | collective-permute-start | bytes 884744 | tf_op jit(solution)/shard_map/ppermute | solution.py:623
  443.1 8.2 %collective-permute-start.27 = (bf16[96,896]{1,0:T(8,128)(2,1)}, bf16[96,896]{1,0:T(8,128)(2,1)S(1)}, u32[]{:S(2)}, u32[]{:S(2)}) collective-permute-start(bf16[96,896]{1,0:T(8,128)(2,1)} %reduce-scatter.8.cloned.1.call-done), channel_id=1, source_target_pairs={{0,24},{8,16},{16,8},{24,0},{1,25},{9,17},{17,9},{25,1},{2,26},{10... | collective-permute-start | bytes 516104 | tf_op jit(solution)/shard_map/ppermute | solution.py:623
  (28 other events, 276.9 us)
Sparse Core Ops, SparseCore 0:
  10.2 26.5 all-gather.3
  39.0 90.3 all-gather.5
  131.1 89.0 all-gather.7
  222.4 97.8 reduce-scatter.3
  322.4 83.7 reduce-scatter.5
  408.9 34.1 reduce-scatter.7

commit v7 on v6

--- a/solution.py
+++ b/solution.py
@@ -741,14 +741,14 @@
             pl.BlockSpec((1, width, TILE), lambda f, *rest, j=j: (2 * f + j, 2 if aligned else 0, 0))
             for j in range(2)
         ]
-        halves = aligned and l + 1 == local_experts
+        halves = aligned
         if halves:
             grad_shapes = [(shards // 2, expert_rows, TILE)] * 2
         elif aligned:
             grad_shapes = [(shards, expert_rows, TILE)]
         else:
             grad_shapes = [(1, 2 * tiles * width, TILE), (tiles, width, TILE)]
-        outs = call(
+        *outs, = call(
             functools.partial(expert_kernel, owners, aligned, halves), "expert", (tiles // 2,),
             [pair] * owners + weights,
             [pair] * owners + [whole(g) for g in grad_shapes],
@@ -770,8 +770,10 @@
                 [gate_up_g.reshape(shards, -1, TILE), down_g.reshape(shards, -1, TILE)], axis=1
             )
         if halves:
+            outs[:owners], keep, give, after = lax.optimization_barrier(
+                (outs[:owners], keep, give, after)
+            )
             grad = add(keep, lax.ppermute(give, "shard", [(i, i ^ 1) for i in range(shards)]))
-        grad, after = lax.optimization_barrier((grad, after))
         return outs[:owners], grad.reshape(-1, TILE), after
 
     def reduce_expert(grad):
@@ -786,9 +788,9 @@
     returned = []
     expert_sums = []
     for l in range(local_experts):
-        rows, ahead = lax.optimization_barrier((received[l], returned or dispatched[-1]))
-        returned = ahead if returned else returned
-        back, grad, received[l + 1 :] = run_expert(l, rows, received[l + 1 :])
+        rows, _ = lax.optimization_barrier((received[l], dispatched[-1]))
+        back, grad, ahead = run_expert(l, rows, (received[l + 1 :], returned))
+        received[l + 1 :], returned = ahead
         back = exchange(back)
         if l + 1 == local_experts:
             back, grad = lax.optimization_barrier((back, grad))

time: 472 us -> 465 us (0.985)
  waiting for transfers between devices: 142 us -> 129 us
  other arithmetic: 16.1 us -> 21.7 us
    ppermute x12, waiting for transfers between devices: 43.2 us -> 26.2 us  [exchange(): lax.ppermute(part, 'expert', [(i, i ^ k) for i in range(owners)])]
    ppermute x1 -> x2, waiting for transfers between devices: 4.97 us -> 13.1 us  [run_expert(): lax.ppermute(give, 'shard', [(i, i ^ 1) for i in range(shards)])]
    convert_element_type x6 -> x7, other arithmetic: 8.07 us -> 13.6 us  [add(): return (a.astype(F32) + b.astype(F32)).astype(BF16)]
  transfers between devices with their start and end apart: 34 -> 35, of which waited for: 19 -> 19; matrix products, arithmetic and copies ran while one was open for 6% -> 8% of each run, Pallas kernels for 51% -> 52%
where the time goes in v7:
time: 465 us; the launch traced here: 456 us
  Pallas kernels  239 us (51%)
  waiting for transfers between devices  129 us (28%)
  starting transfers between devices  32 us (7%)
  other arithmetic  21.7 us (5%)
  local copies, waits for them, and re-layouts  19.3 us (4%)
  between operations  15.6 us (3%)
    pallas_call x2, Pallas kernels, run_expert(): call(functools.partial(expert_kernel, owners, aligned, halves), 'expert',...  61.6 us
    pallas_call x2, Pallas kernels, body(): call(functools.partial(attend_back_kernel, start), 'attend_back', (pairs,...  57.6 us
    pallas_call x1, Pallas kernels, body(): call(attend_kernel, 'attend', (steps,), [wide, whole((count, width)), who...  39.2 us
    ppermute x15, waiting for transfers between devices, send(): return lax.ppermute(part, 'expert', [(i, i ^ k) for i in range(owners)])  34.2 us
    reduce_scatter x1, waiting for transfers between devices, body(): lax.psum_scatter(quarter, 'shard', scatter_dimension=0, tiled=True)  32.3 us
    pallas_call x1, Pallas kernels, body(): call(functools.partial(combine_kernel, experts, owners, local_experts), '...  27.6 us
    ppermute x12, waiting for transfers between devices, exchange(): lax.ppermute(part, 'expert', [(i, i ^ k) for i in range(owners)])  26.2 us
    all_gather x1, waiting for transfers between devices, body(): own = lax.all_gather(packed, 'shard', axis=0, tiled=True)  22.7 us
  transfers between devices with their start and end apart: 35, of which 19 were waited for; matrix products, arithmetic and copies ran while one was open for 8% of the time, Pallas kernels for 52%

profile of v7, /device:TPU:0, one launch (start us, length us, event | category | flops | bytes accessed | tf_op | source)
XLA Modules:
  0.0 455.8 jit_solution(8776283493394132128)
XLA Ops:
  7.2 2.0 pack.1
  9.3 2.3 pack_expert.2
  11.7 2.3 pack_expert.3
  14.1 22.7 %all-gather.4.cloned.1.call-done.small = bf16[768,896]{1,0:T(8,128)(2,1)} async-done(((bf16[96,896]{1,0:T(8,128)(2,1)}), bf16[768,896]{1,0:T(8,128)(2,1)}) %all-gather.4.cloned.1.call-update) | async-done | bytes 1376272 | tf_op jit(solution)/shard_map/all_gather | solution.py:630
  41.1 12.5 %collective-permute-done.2 = bf16[1,384,768]{2,1,0:T(8,128)(2,1)S(1)} collective-permute-done((bf16[1,384,768]{2,1,0:T(8,128)(2,1)S(1)}, bf16[1,384,768]{2,1,0:T(8,128)(2,1)S(1)}, u32[]{:S(2)}, u32[]{:S(2)}) %collective-permute-start.2) | collective-permute-done | bytes 589856 | tf_op jit(solution)/shard_map/ppermute | solution.py:623
  64.8 6.9 %slots.1 = (s32[1024,128]{1,0:T(8,128)}, s32[8,1024]{1,0:T(8,128)}) custom-call(s32[1024,2]{1,0:T(8,128)} %copy.65.routes.refs_12_, s32[1,1024]{1,0:T(1,128)} %order_row.1, s32[1024,1]{1,0:T(8,128)} %copy.67.order_col), custom_call_target="tpu_custom_call" | custom-call | flops 805306368 | bytes 1048576 | tf_op jit(solution)/shard_map/slots/pallas_call | solution.py:670
  73.5 8.9 %collective-permute-done.3 = bf16[2,384,768]{2,1,0:T(8,128)(2,1)} collective-permute-done((bf16[2,384,768]{2,1,0:T(8,128)(2,1)}, bf16[2,384,768]{2,1,0:T(8,128)(2,1)}, u32[]{:S(2)}, u32[]{:S(2)}) %collective-permute-start.3) | collective-permute-done | bytes 1179680 | tf_op jit(solution)/shard_map/ppermute | solution.py:623
  84.6 2.7 maximum_maximum_fusion.wq.wk.wv.wo.refs_15_.refs_7_.refs_8_.refs_9_
  87.4 8.6 %project.1 = (bf16[1024,768]{1,0:T(8,128)(2,1)}, bf16[1024,768]{1,0:T(8,128)(2,1)}, bf16[1024,768]{1,0:T(8,128)(2,1)}, bf16[768,1024]{1,0:T(8,128)(2,1)}, f32[128,768]{1,0:T(8,128)}) custom-call(s32[1]{0:T(128)} %bitcast.me, bf16[1024,768]{1,0:T(8,128)(2,1)} %x.5, bf16[4,768,768]{2,1,0:T(8,128)(2,1)} %maximum_maximum_fusion.wq.wk.wv.wo.refs_15_.refs_7_.refs_8_.refs_9_, ...), custom_call_target="tpu_custom_call" | custom-call | flops 3623878656 | bytes 12582912 | tf_op jit(solution)/shard_map/project/pallas_call | solution.py:688
  96.0 39.2 %attend.1 = (bf16[1024,768]{1,0:T(8,128)(2,1)}, f32[16,1024]{1,0:T(8,128)}, f32[1024,768]{1,0:T(8,128)}, bf16[1024,768]{1,0:T(8,128)(2,1)}, f32[1024,128]{1,0:T(8,128)}) custom-call(s32[1]{0:T(128)} %bitcast.me, s32[1]{0:T(128)S(6)} %copy.75.prefix, bf16[1024,768]{1,0:T(8,128)(2,1)} %get-tuple-element.124.q, bf16[1024,768]{1,0:T(8,128)(2,1)} %get-tuple-element.125.k, ...), custom_call_target="tpu_custom_call" | custom-call | flops 32212254720 | bytes 16777216 | tf_op jit(solution)/shard_map/attend/pallas_call | solution.py:696
  135.2 8.3 %dispatch.2 = (bf16[2,176,768]{2,1,0:T(8,128)(2,1)}, bf16[2,176,768]{2,1,0:T(8,128)(2,1)}, bf16[2,176,768]{2,1,0:T(8,128)(2,1)}, bf16[2,176,768]{2,1,0:T(8,128)(2,1)}) custom-call(s32[1]{0:T(128)} %bitcast.me, bf16[1024,768]{1,0:T(8,128)(2,1)} %get-tuple-element.128.normed.refs_9_, bf16[1024,768]{1,0:T(8,128)(2,1)} %refs_10_.1, ...), custom_call_target="tpu_custom_call" | custom-call | flops 2214592512 | bytes 6291456 | tf_op jit(solution)/shard_map/dispatch/pallas_call | solution.py:719
  147.0 7.9 %dispatch.3 = (bf16[2,176,768]{2,1,0:T(8,128)(2,1)}, bf16[2,176,768]{2,1,0:T(8,128)(2,1)}, bf16[2,176,768]{2,1,0:T(8,128)(2,1)}, bf16[2,176,768]{2,1,0:T(8,128)(2,1)}) custom-call(s32[1]{0:T(128)} %bitcast.me, bf16[1024,768]{1,0:T(8,128)(2,1)} %get-tuple-element.128.normed.refs_9_, bf16[1024,768]{1,0:T(8,128)(2,1)} %refs_10_.1, ...), custom_call_target="tpu_custom_call" | custom-call | flops 2214592512 | bytes 6291456 | tf_op jit(solution)/shard_map/dispatch/pallas_call | solution.py:719
  156.7 2.1 collective-permute-done.4.refs_1_
  160.1 8.3 %collective-permute-done.5.refs_2_ = bf16[2,176,768]{2,1,0:T(8,128)(2,1)S(1)} collective-permute-done((bf16[2,176,768]{2,1,0:T(8,128)(2,1)}, bf16[2,176,768]{2,1,0:T(8,128)(2,1)S(1)}, u32[]{:S(2)}, u32[]{:S(2)}) %collective-permute-start.5) | collective-permute-done | bytes 540704 | tf_op jit(solution)/shard_map/ppermute | solution.py:711
  168.4 3.0 collective-permute-done.6.refs_3_
  172.2 30.8 %expert.2 = (bf16[2,176,768]{2,1,0:T(8,128)(2,1)}, bf16[2,176,768]{2,1,0:T(8,128)(2,1)}, bf16[2,176,768]{2,1,0:T(8,128)(2,1)}, bf16[2,176,768]{2,1,0:T(8,128)(2,...) custom-call(s32[1]{0:T(128)} %bitcast.1.core, bf16[2,176,768]{2,1,0:T(8,128)(2,1)} %get-tuple-element.139.refs_0_, ...), custom_call_target="tpu_custom_call" | custom-call | flops 17716740096 | bytes 25165824 | tf_op jit(solution)/shard_map/expert/pallas_call | solution.py:751
  203.1 8.5 %collective-permute-done.19 = bf16[4,2304,256]{2,1,0:T(8,128)(2,1)S(1)} collective-permute-done((bf16[4,2304,256]{2,1,0:T(8,128)(2,1)}, bf16[4,2304,256]{2,1,0:T(8,128)(2,1)S(1)}, u32[]{:S(2)}, u32[]{:S(2)}) %collective-permute-start.19) | collective-permute-done | bytes 4718624 | tf_op jit(solution)/shard_map/ppermute | solution.py:776
  211.7 5.8 %add_convert_fusion = bf16[4,2304,256]{2,1,0:T(8,128)(2,1)} fusion(bf16[4,2304,256]{2,1,0:T(8,128)(2,1)S(1)} %collective-permute-done.19, bf16[4,2304,256]{2,1,0:T(8,128)(2,1)} %get-tuple-element.197), kind=kLoop, calls=%fused_computation | loop fusion | flops 9437184 | bytes 14155776 | tf_op jit(solution)/shard_map/convert_element_type | solution.py:626
  222.0 30.8 %expert.3 = (bf16[2,176,768]{2,1,0:T(8,128)(2,1)}, bf16[2,176,768]{2,1,0:T(8,128)(2,1)}, bf16[2,176,768]{2,1,0:T(8,128)(2,1)}, bf16[2,176,768]{2,1,0:T(8,128)(2,...) custom-call(s32[1]{0:T(128)} %bitcast.1.core, bf16[2,176,768]{2,1,0:T(8,128)(2,1)} %get-tuple-element.153.refs_0_, ...), custom_call_target="tpu_custom_call" | custom-call | flops 17716740096 | bytes 25165824 | tf_op jit(solution)/shard_map/expert/pallas_call | solution.py:751
  256.5 4.6 collective-permute-done.16
  261.1 5.7 %add_convert_fusion.1 = bf16[4,2304,256]{2,1,0:T(8,128)(2,1)} fusion(bf16[4,2304,256]{2,1,0:T(8,128)(2,1)S(1)} %collective-permute-done.16, bf16[4,2304,256]{2,1,0:T(8,128)(2,1)} %get-tuple-element.175), kind=kLoop, calls=%fused_computation.1 | loop fusion | flops 9437184 | bytes 14155776 | tf_op jit(solution)/shard_map/convert_element_type | solution.py:626
  268.5 11.0 %collective-permute-done.15.refs_7_ = bf16[2,176,768]{2,1,0:T(8,128)(2,1)S(1)} collective-permute-done((bf16[2,176,768]{2,1,0:T(8,128)(2,1)}, bf16[2,176,768]{2,1,0:T(8,128)(2,1)S(1)}, u32[]{:S(2)}, u32[]{:S(2)}) %collective-permute-start.15) | collective-permute-done | bytes 540704 | tf_op jit(solution)/shard_map/ppermute | solution.py:711
  280.3 27.6 %combine.1 = (bf16[1024,768]{1,0:T(8,128)(2,1)}, f32[1024,12]{1,0:T(8,128)}, f32[1024,768]{1,0:T(8,128)}, bf16[1024,768]{1,0:T(8,128)(2,1)}, f32[16,1024]{1,0:T(...) custom-call(s32[1]{0:T(128)} %bitcast.me, bf16[2,176,768]{2,1,0:T(8,128)(2,1)} %get-tuple-element.167.refs_0_, ...), custom_call_target="tpu_custom_call" | custom-call | flops 9059696640 | bytes 25165824 | tf_op jit(solution)/shard_map/combine/pallas_call | solution.py:800
  307.9 28.6 %attend_back.2 = (bf16[1024,384]{1,0:T(8,128)(2,1)}, bf16[1024,384]{1,0:T(8,128)(2,1)}, bf16[1024,384]{1,0:T(8,128)(2,1)}, bf16[4,768,384]{2,1,0:T(8,128)(2,1)}) custom-call(s32[1]{0:T(128)} %bitcast.me, s32[1]{0:T(128)S(6)} %copy.75.prefix, bf16[1024,768]{1,0:T(8,128)(2,1)} %get-tuple-element.124.q, bf16[1024,768]{1,0:T(8,128)(2,1)} %get-tuple-element.125.k, ...), custom_call_target="tpu_custom_call" | custom-call | flops 32212254720 | bytes 6291456 | tf_op jit(solution)/shard_map/attend_back/pallas_call | solution.py:834
  337.9 2.0 collective-permute-start.17
  340.4 28.9 %attend_back.3 = (bf16[1024,384]{1,0:T(8,128)(2,1)}, bf16[1024,384]{1,0:T(8,128)(2,1)}, bf16[1024,384]{1,0:T(8,128)(2,1)}, bf16[4,768,384]{2,1,0:T(8,128)(2,1)}) custom-call(s32[1]{0:T(128)} %bitcast.me, s32[1]{0:T(128)S(6)} %copy.75.prefix, bf16[1024,768]{1,0:T(8,128)(2,1)} %get-tuple-element.124.q, bf16[1024,768]{1,0:T(8,128)(2,1)} %get-tuple-element.125.k, ...), custom_call_target="tpu_custom_call" | custom-call | flops 32212254720 | bytes 6291456 | tf_op jit(solution)/shard_map/attend_back/pallas_call | solution.py:834
  369.3 2.5 fusion.4
  377.7 10.4 %project_back.1 = (f32[1024,768]{1,0:T(8,128)}, bf16[768,128]{1,0:T(8,128)(2,1)}) custom-call(s32[1]{0:T(128)} %bitcast.me, bf16[1024,768]{1,0:T(8,128)(2,1)} %x.5, bf16[1024,384]{1,0:T(8,128)(2,1)} %get-tuple-element.190.refs_0_, bf16[1024,384]{1,0:T(8,128)(2,1)} %get-tuple-element.191.refs_1_, bf16[1024,384]{1,0:T(8,128)(2,1)} %get-tuple-element.192.refs_2_, ...), custom_call_target="tpu_custom_call" | custom-call | flops 3623878656 | bytes 18874368 | tf_op jit(solution)/shard_map/project_back/pallas_call | solution.py:857
  389.3 4.1 collective-permute-done.20
  396.0 4.7 %collective-permute-done.24 = bf16[384,384]{1,0:T(8,128)(2,1)S(1)} collective-permute-done((bf16[384,384]{1,0:T(8,128)(2,1)S(1)}, bf16[384,384]{1,0:T(8,128)(2,1)S(1)}, u32[]{:S(2)}, u32[]{:S(2)}) %collective-permute-start.24) | collective-permute-done | bytes 294944 | tf_op jit(solution)/shard_map/ppermute | solution.py:623
  402.5 32.3 %reduce-scatter.8.cloned.1.call-done = bf16[96,896]{1,0:T(8,128)(2,1)} async-done(((bf16[768,896]{1,0:T(8,128)(2,1)}), bf16[96,896]{1,0:T(8,128)(2,1)}) %reduce-scatter.8.cloned.1.call-update) | async-done | bytes 172048 | tf_op jit(solution)/shard_map/reduce_scatter | solution.py:871
  439.1 3.9 unpack.1
  (144 shorter events, 60.1 us)
Async XLA Ops:
  7.2 29.6 %all-gather.4.cloned.1.call-start = ((), (), s32[]{:S(2)}) async-start(), calls=%async_computation.3 | async-start | bytes 1548288 | tf_op jit(solution)/shard_map/all_gather | solution.py:630
  9.2 162.2 %all-gather.6.cloned.1.call-start = ((), (), s32[]{:S(2)}) async-start(), calls=%async_computation.4 | async-start | bytes 10616832 | tf_op jit(solution)/shard_map/all_gather | solution.py:655
  11.6 210.4 %all-gather.8.cloned.1.call-start = ((), (), s32[]{:S(2)}) async-start(), calls=%async_computation.5 | async-start | bytes 10616832 | tf_op jit(solution)/shard_map/all_gather | solution.py:655
  14.0 359.5 %reduce-scatter.4.cloned.1.call-start = ((), (), s32[]{:S(2)}) async-start(), calls=%async_computation.6 | async-start | bytes 5898240 | tf_op jit(solution)/shard_map/reduce_scatter | solution.py:780
  38.1 15.5 %collective-permute-start.2 = (bf16[1,384,768]{2,1,0:T(8,128)(2,1)S(1)}, bf16[1,384,768]{2,1,0:T(8,128)(2,1)S(1)}, u32[]{:S(2)}, u32[]{:S(2)}) collective-permute-start(bf16[1,384,768]{2,1,0:T(8,128)(2,1)S(1)} %get-tuple-element.294), channel_id=1, source_target_pairs={{0,16},{8,24},{16,0},{24,8},{1,17},{9,25},{17,1},{25,9},{2,18},{10... | collective-permute-start | bytes 1769480 | tf_op jit(solution)/shard_map/ppermute | solution.py:623
  39.7 16.6 %collective-permute-start = (bf16[1,384,768]{2,1,0:T(8,128)(2,1)S(1)}, bf16[1,384,768]{2,1,0:T(8,128)(2,1)S(1)}, u32[]{:S(2)}, u32[]{:S(2)}) collective-permute-start(bf16[1,384,768]{2,1,0:T(8,128)(2,1)S(1)} %get-tuple-element.293), channel_id=1, source_target_pairs={{0,8},{8,0},{16,24},{24,16},{1,9},{9,1},{17,25},{25,17},{2,10},{10... | collective-permute-start | bytes 1769480 | tf_op jit(solution)/shard_map/ppermute | solution.py:623
  54.8 27.7 %collective-permute-start.3 = (bf16[2,384,768]{2,1,0:T(8,128)(2,1)}, bf16[2,384,768]{2,1,0:T(8,128)(2,1)}, u32[]{:S(2)}, u32[]{:S(2)}) collective-permute-start(bf16[2,384,768]{2,1,0:T(8,128)(2,1)} %pad_maximum_fusion.2), channel_id=1, source_target_pairs={{0,8},{8,0},{16,24},{24,16},{1,9},{9,1},{17,25},{25,17},{2,10},{10... | collective-permute-start | bytes 3538952 | tf_op jit(solution)/shard_map/ppermute | solution.py:623
  57.4 27.3 %collective-permute-start.1 = (bf16[2,384,768]{2,1,0:T(8,128)(2,1)}, bf16[2,384,768]{2,1,0:T(8,128)(2,1)S(1)}, u32[]{:S(2)}, u32[]{:S(2)}) collective-permute-start(bf16[2,384,768]{2,1,0:T(8,128)(2,1)} %pad_maximum_fusion.1), channel_id=1, source_target_pairs={{0,16},{8,24},{16,0},{24,8},{1,17},{9,25},{17,1},{25,9},{2,18},{10... | collective-permute-start | bytes 3538952 | tf_op jit(solution)/shard_map/ppermute | solution.py:623
  143.5 15.4 %collective-permute-start.4 = (bf16[2,176,768]{2,1,0:T(8,128)(2,1)}, bf16[2,176,768]{2,1,0:T(8,128)(2,1)S(1)}, u32[]{:S(2)}, u32[]{:S(2)}) collective-permute-start(bf16[2,176,768]{2,1,0:T(8,128)(2,1)} %get-tuple-element.132), channel_id=1, source_target_pairs={{0,8},{8,0},{16,24},{24,16},{1,9},{9,1},{17,25},{25,17},{2,10},{10... | collective-permute-start | bytes 1622024 | tf_op jit(solution)/shard_map/ppermute | solution.py:711
  143.8 24.6 %collective-permute-start.5 = (bf16[2,176,768]{2,1,0:T(8,128)(2,1)}, bf16[2,176,768]{2,1,0:T(8,128)(2,1)S(1)}, u32[]{:S(2)}, u32[]{:S(2)}) collective-permute-start(bf16[2,176,768]{2,1,0:T(8,128)(2,1)} %get-tuple-element.133), channel_id=1, source_target_pairs={{0,16},{8,24},{16,0},{24,8},{1,17},{9,25},{17,1},{25,9},{2,18},{10... | collective-permute-start | bytes 1622024 | tf_op jit(solution)/shard_map/ppermute | solution.py:711
  145.3 26.1 %collective-permute-start.6 = (bf16[2,176,768]{2,1,0:T(8,128)(2,1)}, bf16[2,176,768]{2,1,0:T(8,128)(2,1)S(1)}, u32[]{:S(2)}, u32[]{:S(2)}) collective-permute-start(bf16[2,176,768]{2,1,0:T(8,128)(2,1)} %get-tuple-element.134), channel_id=1, source_target_pairs={{0,24},{8,16},{16,8},{24,0},{1,25},{9,17},{17,9},{25,1},{2,26},{10... | collective-permute-start | bytes 1622024 | tf_op jit(solution)/shard_map/ppermute | solution.py:711
  154.9 48.0 %collective-permute-start.7 = (bf16[2,176,768]{2,1,0:T(8,128)(2,1)}, bf16[2,176,768]{2,1,0:T(8,128)(2,1)S(1)}, u32[]{:S(2)}, u32[]{:S(2)}) collective-permute-start(bf16[2,176,768]{2,1,0:T(8,128)(2,1)} %get-tuple-element.136), channel_id=1, source_target_pairs={{0,8},{8,0},{16,24},{24,16},{1,9},{9,1},{17,25},{25,17},{2,10},{10... | collective-permute-start | bytes 1622024 | tf_op jit(solution)/shard_map/ppermute | solution.py:711
  155.3 47.7 %collective-permute-start.8 = (bf16[2,176,768]{2,1,0:T(8,128)(2,1)}, bf16[2,176,768]{2,1,0:T(8,128)(2,1)S(1)}, u32[]{:S(2)}, u32[]{:S(2)}) collective-permute-start(bf16[2,176,768]{2,1,0:T(8,128)(2,1)} %get-tuple-element.137), channel_id=1, source_target_pairs={{0,16},{8,24},{16,0},{24,8},{1,17},{9,25},{17,1},{25,9},{2,18},{10... | collective-permute-start | bytes 1622024 | tf_op jit(solution)/shard_map/ppermute | solution.py:711
  158.9 44.1 %collective-permute-start.9 = (bf16[2,176,768]{2,1,0:T(8,128)(2,1)}, bf16[2,176,768]{2,1,0:T(8,128)(2,1)S(1)}, u32[]{:S(2)}, u32[]{:S(2)}) collective-permute-start(bf16[2,176,768]{2,1,0:T(8,128)(2,1)} %get-tuple-element.138), channel_id=1, source_target_pairs={{0,24},{8,16},{16,8},{24,0},{1,25},{9,17},{17,9},{25,1},{2,26},{10... | collective-permute-start | bytes 1622024 | tf_op jit(solution)/shard_map/ppermute | solution.py:711
  203.0 8.6 %collective-permute-start.19 = (bf16[4,2304,256]{2,1,0:T(8,128)(2,1)}, bf16[4,2304,256]{2,1,0:T(8,128)(2,1)S(1)}, u32[]{:S(2)}, u32[]{:S(2)}) collective-permute-start(bf16[4,2304,256]{2,1,0:T(8,128)(2,1)} %get-tuple-element.198), channel_id=1, source_target_pairs={{0,1},{1,0},{2,3},{3,2},{4,5},{5,4},{6,7},{7,6},{8,9},{9,8},{10,11... | collective-permute-start | bytes 14155784 | tf_op jit(solution)/shard_map/ppermute | solution.py:776
  217.5 184.9 %reduce-scatter.6.cloned.1.call-start = ((), (), s32[]{:S(2)}) async-start(), calls=%async_computation.7 | async-start | bytes 5898240 | tf_op jit(solution)/shard_map/reduce_scatter | solution.py:780
  218.5 34.3 %collective-permute-start.10 = (bf16[2,176,768]{2,1,0:T(8,128)(2,1)S(1)}, bf16[2,176,768]{2,1,0:T(8,128)(2,1)S(1)}, u32[]{:S(2)}, u32[]{:S(2)}) collective-permute-start(bf16[2,176,768]{2,1,0:T(8,128)(2,1)S(1)} %copy-done.21), channel_id=1, source_target_pairs={{0,8},{8,0},{16,24},{24,16},{1,9},{9,1},{17,25},{25,17},{2,10},{10... | collective-permute-start | bytes 1622024 | tf_op jit(solution)/shard_map/ppermute | solution.py:711
  218.9 34.0 %collective-permute-start.11 = (bf16[2,176,768]{2,1,0:T(8,128)(2,1)S(1)}, bf16[2,176,768]{2,1,0:T(8,128)(2,1)S(1)}, u32[]{:S(2)}, u32[]{:S(2)}) collective-permute-start(bf16[2,176,768]{2,1,0:T(8,128)(2,1)S(1)} %copy-done.20), channel_id=1, source_target_pairs={{0,16},{8,24},{16,0},{24,8},{1,17},{9,25},{17,1},{25,9},{2,18},{10... | collective-permute-start | bytes 1622024 | tf_op jit(solution)/shard_map/ppermute | solution.py:711
  220.3 32.6 %collective-permute-start.12 = (bf16[2,176,768]{2,1,0:T(8,128)(2,1)S(1)}, bf16[2,176,768]{2,1,0:T(8,128)(2,1)S(1)}, u32[]{:S(2)}, u32[]{:S(2)}) collective-permute-start(bf16[2,176,768]{2,1,0:T(8,128)(2,1)S(1)} %copy-done.18), channel_id=1, source_target_pairs={{0,24},{8,16},{16,8},{24,0},{1,25},{9,17},{17,9},{25,1},{2,26},{10... | collective-permute-start | bytes 1622024 | tf_op jit(solution)/shard_map/ppermute | solution.py:711
  252.9 8.2 %collective-permute-start.16 = (bf16[4,2304,256]{2,1,0:T(8,128)(2,1)}, bf16[4,2304,256]{2,1,0:T(8,128)(2,1)S(1)}, u32[]{:S(2)}, u32[]{:S(2)}) collective-permute-start(bf16[4,2304,256]{2,1,0:T(8,128)(2,1)} %get-tuple-element.176), channel_id=1, source_target_pairs={{0,1},{1,0},{2,3},{3,2},{4,5},{5,4},{6,7},{7,6},{8,9},{9,8},{10,11... | collective-permute-start | bytes 14155784 | tf_op jit(solution)/shard_map/ppermute | solution.py:776
  253.0 15.4 %collective-permute-start.13 = (bf16[2,176,768]{2,1,0:T(8,128)(2,1)}, bf16[2,176,768]{2,1,0:T(8,128)(2,1)S(1)}, u32[]{:S(2)}, u32[]{:S(2)}) collective-permute-start(bf16[2,176,768]{2,1,0:T(8,128)(2,1)} %get-tuple-element.172), channel_id=1, source_target_pairs={{0,8},{8,0},{16,24},{24,16},{1,9},{9,1},{17,25},{25,17},{2,10},{10... | collective-permute-start | bytes 1622024 | tf_op jit(solution)/shard_map/ppermute | solution.py:711
  253.4 15.1 %collective-permute-start.14 = (bf16[2,176,768]{2,1,0:T(8,128)(2,1)}, bf16[2,176,768]{2,1,0:T(8,128)(2,1)S(1)}, u32[]{:S(2)}, u32[]{:S(2)}) collective-permute-start(bf16[2,176,768]{2,1,0:T(8,128)(2,1)} %get-tuple-element.173), channel_id=1, source_target_pairs={{0,16},{8,24},{16,0},{24,8},{1,17},{9,25},{17,1},{25,9},{2,18},{10... | collective-permute-start | bytes 1622024 | tf_op jit(solution)/shard_map/ppermute | solution.py:711
  254.8 24.7 %collective-permute-start.15 = (bf16[2,176,768]{2,1,0:T(8,128)(2,1)}, bf16[2,176,768]{2,1,0:T(8,128)(2,1)S(1)}, u32[]{:S(2)}, u32[]{:S(2)}) collective-permute-start(bf16[2,176,768]{2,1,0:T(8,128)(2,1)} %get-tuple-element.174), channel_id=1, source_target_pairs={{0,24},{8,16},{16,8},{24,0},{1,25},{9,17},{17,9},{25,1},{2,26},{10... | collective-permute-start | bytes 1622024 | tf_op jit(solution)/shard_map/ppermute | solution.py:711
  280.3 154.5 %reduce-scatter.8.cloned.1.call-start = ((), (), s32[]{:S(2)}) async-start(), calls=%async_computation.8 | async-start | bytes 1548288 | tf_op jit(solution)/shard_map/reduce_scatter | solution.py:871
  337.9 35.6 %collective-permute-start.17 = (bf16[2,384,384]{2,1,0:T(8,128)(2,1)S(1)}, bf16[2,384,384]{2,1,0:T(8,128)(2,1)}, u32[]{:S(2)}, u32[]{:S(2)}) collective-permute-start(bf16[2,384,384]{2,1,0:T(8,128)(2,1)S(1)} %get-tuple-element.292), channel_id=1, source_target_pairs={{0,8},{8,0},{16,24},{24,16},{1,9},{9,1},{17,25},{25,17},{2,10},{10... | collective-permute-start | bytes 1769480 | tf_op jit(solution)/shard_map/ppermute | solution.py:623
  339.8 33.6 %collective-permute-start.18 = (bf16[2,384,384]{2,1,0:T(8,128)(2,1)S(1)}, bf16[2,384,384]{2,1,0:T(8,128)(2,1)}, u32[]{:S(2)}, u32[]{:S(2)}) collective-permute-start(bf16[2,384,384]{2,1,0:T(8,128)(2,1)S(1)} %get-tuple-element.291), channel_id=1, source_target_pairs={{0,16},{8,24},{16,0},{24,8},{1,17},{9,25},{17,1},{25,9},{2,18},{10... | collective-permute-start | bytes 1769480 | tf_op jit(solution)/shard_map/ppermute | solution.py:623
  371.8 16.4 %collective-permute-start.22 = (bf16[2,384,384]{2,1,0:T(8,128)(2,1)}, bf16[2,384,384]{2,1,0:T(8,128)(2,1)S(1)}, u32[]{:S(2)}, u32[]{:S(2)}) collective-permute-start(bf16[2,384,384]{2,1,0:T(8,128)(2,1)} %get-tuple-element.288), channel_id=1, source_target_pairs={{0,8},{8,0},{16,24},{24,16},{1,9},{9,1},{17,25},{25,17},{2,10},{10... | collective-permute-start | bytes 1769480 | tf_op jit(solution)/shard_map/ppermute | solution.py:623
  372.9 16.4 %collective-permute-start.23 = (bf16[2,384,384]{2,1,0:T(8,128)(2,1)}, bf16[2,384,384]{2,1,0:T(8,128)(2,1)S(1)}, u32[]{:S(2)}, u32[]{:S(2)}) collective-permute-start(bf16[2,384,384]{2,1,0:T(8,128)(2,1)} %get-tuple-element.287), channel_id=1, source_target_pairs={{0,16},{8,24},{16,0},{24,8},{1,17},{9,25},{17,1},{25,9},{2,18},{10... | collective-permute-start | bytes 1769480 | tf_op jit(solution)/shard_map/ppermute | solution.py:623
  375.1 18.3 %collective-permute-start.20 = (bf16[384,384]{1,0:T(8,128)(2,1)S(1)}, bf16[384,384]{1,0:T(8,128)(2,1)S(1)}, u32[]{:S(2)}, u32[]{:S(2)}) collective-permute-start(bf16[384,384]{1,0:T(8,128)(2,1)S(1)} %slice_bitcast_fusion.8), channel_id=1, source_target_pairs={{0,16},{8,24},{16,0},{24,8},{1,17},{9,25},{17,1},{25,9},{2,18},{10... | collective-permute-start | bytes 884744 | tf_op jit(solution)/shard_map/ppermute | solution.py:623
  376.6 16.8 %collective-permute-start.21 = (bf16[384,384]{1,0:T(8,128)(2,1)S(1)}, bf16[384,384]{1,0:T(8,128)(2,1)S(1)}, u32[]{:S(2)}, u32[]{:S(2)}) collective-permute-start(bf16[384,384]{1,0:T(8,128)(2,1)S(1)} %slice_bitcast_fusion.7), channel_id=1, source_target_pairs={{0,8},{8,0},{16,24},{24,16},{1,9},{9,1},{17,25},{25,17},{2,10},{10... | collective-permute-start | bytes 884744 | tf_op jit(solution)/shard_map/ppermute | solution.py:623
  393.7 6.9 %collective-permute-start.24 = (bf16[384,384]{1,0:T(8,128)(2,1)S(1)}, bf16[384,384]{1,0:T(8,128)(2,1)S(1)}, u32[]{:S(2)}, u32[]{:S(2)}) collective-permute-start(bf16[384,384]{1,0:T(8,128)(2,1)S(1)} %slice_bitcast_fusion.4), channel_id=1, source_target_pairs={{0,16},{8,24},{16,0},{24,8},{1,17},{9,25},{17,1},{25,9},{2,18},{10... | collective-permute-start | bytes 884744 | tf_op jit(solution)/shard_map/ppermute | solution.py:623
  434.8 8.2 %collective-permute-start.26 = (bf16[96,896]{1,0:T(8,128)(2,1)}, bf16[96,896]{1,0:T(8,128)(2,1)S(1)}, u32[]{:S(2)}, u32[]{:S(2)}) collective-permute-start(bf16[96,896]{1,0:T(8,128)(2,1)} %reduce-scatter.8.cloned.1.call-done), channel_id=1, source_target_pairs={{0,8},{8,0},{16,24},{24,16},{1,9},{9,1},{17,25},{25,17},{2,10},{10... | collective-permute-start | bytes 516104 | tf_op jit(solution)/shard_map/ppermute | solution.py:623
  (28 other events, 267.1 us)
Sparse Core Ops, SparseCore 0:
  10.2 26.5 all-gather.3
  39.0 90.3 all-gather.5
  131.1 89.1 all-gather.7
  222.4 83.6 reduce-scatter.3
  308.3 85.7 reduce-scatter.5
  402.6 32.1 reduce-scatter.7
